TPU v7x, 32 devices: a whole 2x2x4 slice. The times are simulated.
32 devices in a mesh: parts: 2 (over y), pencil: 4 (over z), slab: 2 (over x), field: 2 (over core).
Axes of the slice: x: 2, y: 2, z: 4, core: 2. Of those that a mesh axis runs over, the one named last changes fastest.
Arguments:
- state: bfloat16 [16, 2, 512, 512], P('parts', 'slab', 'pencil'), parts along dimension 0, may hold values from -6 to 6
- tangents: bfloat16 [16, 8, 2, 512, 512], P(('parts', 'field'), None, 'slab', 'pencil'), parts along dimension 0, may hold values from -6 to 6
- d1: bfloat16 [512, 512], replicated, may hold values from -0.25 to 0.25
- d2: bfloat16 [512, 512], replicated, may hold values from -0.25 to 0.25
- filt: bfloat16 [512, 512], replicated, may hold values from -0.25 to 0.25
- advect: float32 [2, 8], replicated, may hold values from 0.3 to 1
- diffuse: float32 [8], replicated, may hold values from 0.3 to 1
- coef: float32 [8, 8], replicated, may hold values from -3 to 3
- rates: float32 [8, 8], replicated, may hold values from -3.6 to 3.6
Outputs:
- state_out: bfloat16 [16, 2, 512, 512], P('parts', 'slab', 'pencil'), parts along dimension 0
- tangent_out: bfloat16 [16, 8, 2, 512, 512], P(('parts', 'field'), None, 'slab', 'pencil'), parts along dimension 0
There are 2 independent parts, one for each index of `parts`. A program takes and returns all parts, laid end to end along the dimension named above; an argument that names none is the same for every part. Nothing has to cross between parts.
All inputs are finite; a program needn't handle non-finite values.
Results may differ from a plain program's by a relative error of at most 0.0094.
Values may be sent and summed in bfloat16 or wider, within the bound.
No kernel may reach another device: no remote copies, remote signals or barrier semaphores. Data moves between devices by JAX's collectives and lax.ppermute only.
A program may use at most 128 MiB of HBM per device.

v0:
```python
import functools

import jax
import jax.numpy as jnp
from jax import lax
from jax.experimental import pallas as pl
from jax.experimental.pallas import tpu as pltpu
from jax.sharding import PartitionSpec as P


highest = lax.Precision.HIGHEST
time_step = 0.4
f32 = jnp.float32
bf16 = jnp.bfloat16
LANES = 128
WIDE = 2 * LANES
DEPTH = 32


def spread(values, fields):
    return values.reshape(values.shape + (1,) * (fields.ndim - values.ndim))


def reaction(state, tangent, coef, rates, offset):
    state_float = state.astype(f32)
    argument = jnp.einsum("ps,s...->p...", rates, state_float, precision=highest)
    activity = jnp.tanh(argument)
    slopes = 1.0 - activity * activity
    state_rate = jnp.einsum("ps,p...->s...", coef, activity, precision=highest)
    tangent_float = tangent.astype(f32)
    mixing = jnp.einsum("pt,qt...->qp...", rates, tangent_float, precision=highest)
    number = tangent.shape[0]
    own_coef = lax.dynamic_slice_in_dim(coef, offset, number, 0)
    own_activity = lax.dynamic_slice_in_dim(activity, offset, number, 0)
    tangent_rate = jnp.einsum("ps,qp...->qs...", coef, slopes[None] * mixing, precision=highest)
    tangent_rate = tangent_rate + spread(own_coef, tangent) * own_activity[:, None]
    return (state_rate, tangent_rate)


def update(fields, rate, speeds, diffusivity, operators):
    derivative_op, diffusion_op, filter_op = operators
    slope_term = jnp.dot(fields, derivative_op, preferred_element_type=f32)
    curve_term = jnp.dot(fields, diffusion_op, preferred_element_type=f32)
    middle = fields.astype(f32) + time_step * (
        spread(diffusivity, fields) * curve_term - spread(speeds, fields) * slope_term + rate
    )
    middle = middle.astype(bf16)
    return jnp.dot(middle, filter_op, preferred_element_type=f32).astype(bf16)


def plain(state, tangents, d1, d2, filt, advect, diffuse, coef, rates):
    params_here = tangents.shape[0]
    state_count = state.shape[0]
    offset = lax.axis_index("field") * params_here
    operators = (d1, d2, filt)
    for direction in range(2):
        speeds = advect[direction]
        state_rate, tangent_rate = reaction(state, tangents, coef, rates, offset)
        tangents = update(tangents, tangent_rate, speeds[None, :], diffuse[None, :], operators)
        outgoing = update(state, state_rate, speeds, diffuse, operators)
        merged = tangents.reshape((params_here * state_count,) + tangents.shape[2:])
        arrived = lax.all_to_all(outgoing, "pencil", split_axis=3, concat_axis=2, tiled=True)
        merged = lax.all_to_all(merged, "pencil", split_axis=3, concat_axis=2, tiled=True)
        state = jnp.swapaxes(arrived, 2, 3)
        merged = jnp.swapaxes(merged, 2, 3)
        tangents = merged.reshape((params_here, state_count) + merged.shape[1:])
    return (state, tangents)


def aligned(index, size):
    return pl.ds(pl.multiple_of(index * size, size), size)


def fill_mixer(entry, high, low):
    rows, columns = high.shape
    lane = lax.broadcasted_iota(jnp.int32, (8, columns), 1)
    row = lax.broadcasted_iota(jnp.int32, (8, columns), 0)
    group = lane // DEPTH
    within = lane - group * DEPTH
    for a in range(rows // DEPTH):
        values = jnp.zeros((8, columns), f32)
        for b in range(columns // DEPTH):
            values = jnp.where(group == b, entry(a, b), values)
        pieces = [jnp.where(within == row + 8 * k, values, 0.0) for k in range(DEPTH // 8)]
        block = jnp.concatenate(pieces, axis=0)
        rounded = block.astype(bf16)
        high[a * DEPTH : (a + 1) * DEPTH, :] = rounded
        low[a * DEPTH : (a + 1) * DEPTH, :] = (block - rounded.astype(f32)).astype(bf16)


def mixed(mixer, fields):
    high, low = mixer
    return jnp.dot(high[...], fields, preferred_element_type=f32) + jnp.dot(
        low[...], fields, preferred_element_type=f32
    )


def mixed_float(mixer, values):
    rounded = values.astype(bf16)
    left = (values - rounded.astype(f32)).astype(bf16)
    return mixed(mixer, rounded) + jnp.dot(mixer[0][...], left, preferred_element_type=f32)


def tangent_scaled(activity, mixing, own):
    scaled = (1.0 - activity * activity) * mixing
    group = lax.broadcasted_iota(jnp.int32, activity.shape, 0) // DEPTH
    return scaled + jnp.where(group == own, activity, 0.0)


def advance(v, curve, slope, rate, diffusivity, speed):
    return (v.astype(f32) + time_step * (diffusivity * curve - speed * slope + rate)).astype(bf16)


def x_kernel(n, q, params_here, rates, coef, advect, diffuse, state, *rest):
    if q is not None:
        tangent, rest = rest[0], rest[1:]
    d1, d2, filt = rest[:3]
    outs, rest = rest[3 : 3 + n], rest[3 + n :]
    filt_own, rates_high, rates_low, coef_high, coef_low, middle = rest
    me, half = lax.axis_index("pencil"), lax.axis_index("field")
    count, rows, length = state.shape
    fields = outs[0].shape[0]
    size = length // n
    first = half * fields if q is None else 0

    @pl.when(pl.program_id(0) == 0)
    def _():
        fill_mixer(lambda a, b: rates[a, b], rates_high, rates_low)
        fill_mixer(lambda a, b: coef[b, first + a], coef_high, coef_low)
        for r in range(n):
            filt_own[:, r * size : (r + 1) * size] = filt[:, aligned(me ^ r, size)]

    source = state[pl.ds(first, fields)] if q is None else tangent[...]
    own = source.reshape(fields * rows, length)
    for c in range(length // WIDE):
        across = slice(c * WIDE, (c + 1) * WIDE)
        u = state[:, :, across].reshape(count * rows, WIDE)
        activity = jnp.tanh(mixed((rates_high, rates_low), u))
        if q is None:
            scaled = activity
        else:
            mixing = mixed((rates_high, rates_low), own[:, across])
            scaled = tangent_scaled(activity, mixing, half * params_here + q)
        rate = mixed_float((coef_high, coef_low), scaled)
        slope = jnp.dot(own, d1[:, across], preferred_element_type=f32)
        curve = jnp.dot(own, d2[:, across], preferred_element_type=f32)
        for s in range(fields):
            at = slice(s * rows, (s + 1) * rows)
            middle[at, across] = advance(
                own[at, across], curve[at], slope[at], rate[at], diffuse[first + s], advect[0, first + s]
            )
    result = jnp.dot(middle[...], filt_own[...], preferred_element_type=f32).astype(bf16)
    for r in range(n):
        outs[r][...] = result[:, r * size : (r + 1) * size].reshape(fields, rows, size)


def y_kernel(n, q, params_here, rates, coef, advect, diffuse, *rest):
    own, rest = rest[:n], rest[n:]
    other, rest = rest[:n], rest[n:]
    if q is None:
        arrived = own
    else:
        arrived, rest = rest[:n], rest[n:]
    d1t, d2t, filtt = rest[:3]
    outs, rest = rest[3 : 3 + n], rest[3 + n :]
    filt_own, v_full, rate_full, state_high, state_low, coef_high, coef_low = rest[:7]
    me, half = lax.axis_index("pencil"), lax.axis_index("field")
    here = own[0].shape[0]
    count = rates.shape[1]
    size = own[0].shape[1]
    fields = outs[0].shape[0]
    first = half * here if q is None else 0

    fill_mixer(lambda a, b: rates[a, lax.rem(half * here + b, count)], state_high, state_low)
    fill_mixer(lambda a, b: coef[b, first + a], coef_high, coef_low)
    if q is not None:
        rates_high, rates_low = rest[7:]
        fill_mixer(lambda a, b: rates[a, b], rates_high, rates_low)

    def tile(refs, down):
        return jnp.concatenate([ref[:, down, :].reshape(ref.shape[0] * DEPTH, size) for ref in refs], axis=0)

    def pair(refs, j):
        starts = [(2 * j + k) * DEPTH for k in range(2)]
        return jnp.concatenate([tile(refs, pl.ds(pl.multiple_of(at, DEPTH), DEPTH)) for at in starts], axis=1)

    for r in range(n):
        filt_own[r * size : (r + 1) * size, :] = filtt[aligned(me ^ r, size), :]
        for s in range(fields):
            v_full[aligned(me ^ r, size), s * size : (s + 1) * size] = arrived[r][s]

        def rate_block(j, carry, r=r):
            activity = jnp.tanh(mixed((state_high, state_low), pair((own[r], other[r]), j)))
            if q is None:
                scaled = activity
            else:
                mixing = mixed((rates_high, rates_low), pair((arrived[r],), j))
                scaled = tangent_scaled(activity, mixing, half * params_here + q)
            rate = mixed_float((coef_high, coef_low), scaled)
            for k in range(2):
                down = pl.ds(pl.multiple_of((me ^ r) * size + (2 * j + k) * DEPTH, DEPTH), DEPTH)
                for s in range(fields):
                    rate_full[down, s * size : (s + 1) * size] = rate[
                        s * DEPTH : (s + 1) * DEPTH, k * size : (k + 1) * size
                    ]
            return carry

        lax.fori_loop(0, size // (2 * DEPTH), rate_block, 0)

    def two_fields(f, carry):
        v = v_full[:, aligned(f, 2 * size)]
        slope = jnp.dot(d1t[...], v, preferred_element_type=f32)
        curve = jnp.dot(d2t[...], v, preferred_element_type=f32)
        columns = []
        for k in range(2):
            s = 2 * f + k
            across = slice(k * size, (k + 1) * size)
            columns.append(
                advance(
                    v[:, across],
                    curve[:, across],
                    slope[:, across],
                    rate_full[:, aligned(s, size)],
                    diffuse[first + s],
                    advect[1, first + s],
                )
            )
        middle = jnp.concatenate(columns, axis=1)
        result = jnp.dot(filt_own[...], middle, preferred_element_type=f32).astype(bf16)
        for r in range(n):
            for k in range(2):
                outs[r][2 * f + k] = result[r * size : (r + 1) * size, k * size : (k + 1) * size]
        return carry

    lax.fori_loop(0, fields // 2, two_fields, 0)


def place_kernel(n, slots_of, *rest):
    me, half = lax.axis_index("pencil"), lax.axis_index("field")
    out = rest[-1]
    slots = rest[: n * slots_of]
    here = slots[0].shape[0]
    size = slots[0].shape[2]
    for g in range(slots_of):
        for r in range(n):
            slot = slots[g * n + r]
            for s in range(here):
                if slots_of == 1:
                    out[0, s, 0, :, aligned(me ^ r, size)] = slot[s]
                else:
                    at = (half if g == 0 else 1 - half) * here + s
                    out[at, 0, :, aligned(me ^ r, size)] = slot[s]


SMEM = pl.BlockSpec(memory_space=pltpu.SMEM)
VMEM = pl.BlockSpec(memory_space=pltpu.VMEM)
HBM = pl.BlockSpec(memory_space=pl.ANY)
GRANT = pltpu.CompilerParams(vmem_limit_bytes=32 * 1024 * 1024)


def cost(flops, moved):
    return pl.CostEstimate(flops=flops, bytes_accessed=moved, transcendentals=0)


def mixers(fields, count):
    return [pltpu.VMEM((fields * DEPTH, count * DEPTH), bf16)] * 2


def x_call(n, q, scalars, state, tangents, d1, d2, filt, here):
    count, _, deep, length = state.shape
    size = length // n
    fields = here if q is None else count
    whole = pl.BlockSpec((length, length), lambda i: (0, 0))
    arrays = [state]
    specs = [pl.BlockSpec((count, None, DEPTH, length), lambda i: (0, 0, i, 0))]
    if q is not None:
        arrays.append(tangents)
        specs.append(pl.BlockSpec((None, count, None, DEPTH, length), lambda i: (q, 0, 0, i, 0)))
    return pl.pallas_call(
        functools.partial(x_kernel, n, q, None if q is None else tangents.shape[0]),
        grid=(deep // DEPTH,),
        out_shape=[jax.ShapeDtypeStruct((fields, deep, size), bf16)] * n,
        in_specs=[SMEM] * 4 + specs + [whole] * 3,
        out_specs=[pl.BlockSpec((fields, DEPTH, size), lambda i: (0, i, 0))] * n,
        scratch_shapes=[pltpu.VMEM((length, length), bf16)]
        + mixers(count, count)
        + mixers(fields, count)
        + [pltpu.VMEM((fields * DEPTH, length), bf16)],
        cost_estimate=cost(6 * fields * deep * length * length, 4 * fields * deep * length),
    )(*scalars, *arrays, d1, d2, filt)


def y_call(n, q, params_here, scalars, own, other, arrived, turned):
    here, deep, size = own[0].shape
    count = scalars[0].shape[1]
    length = deep * n
    fields = here if q is None else count
    arrays = list(own) + list(other) + list(arrived or ())
    return pl.pallas_call(
        functools.partial(y_kernel, n, q, params_here),
        out_shape=[jax.ShapeDtypeStruct((fields, deep, size), bf16)] * n,
        in_specs=[SMEM] * 4 + [VMEM] * (len(arrays) + 3),
        out_specs=[VMEM] * n,
        scratch_shapes=[
            pltpu.VMEM((length, length), bf16),
            pltpu.VMEM((length, fields * size), bf16),
            pltpu.VMEM((length, fields * size), f32),
        ]
        + mixers(count, count)
        + mixers(fields, count)
        + ([] if q is None else mixers(count, count)),
        compiler_params=GRANT,
        cost_estimate=cost(6 * fields * deep * length * length, 4 * fields * deep * length),
    )(*scalars, *arrays, *turned)


def place_state(n, shape, own, other):
    return pl.pallas_call(
        functools.partial(place_kernel, n, 2),
        out_shape=jax.ShapeDtypeStruct(shape, bf16),
        in_specs=[VMEM] * (2 * n),
        out_specs=VMEM,
        compiler_params=GRANT,
        name="place_state",
    )(*own, *other)


def place_tangent(n, q, shape, slots, buffer):
    count, deep, size = slots[0].shape
    part = 2
    specs = [pl.BlockSpec((part, deep, size), lambda i: (i, 0, 0))] * n
    arrays = list(slots)
    aliases = {}
    if buffer is not None:
        specs.append(HBM)
        arrays.append(buffer)
        aliases = {n: 0}
    return pl.pallas_call(
        functools.partial(place_kernel, n, 1),
        grid=(count // part,),
        out_shape=jax.ShapeDtypeStruct(shape, bf16),
        in_specs=specs,
        out_specs=pl.BlockSpec((1, part, 1, deep, shape[-1]), lambda i: (q, i, 0, 0, 0)),
        input_output_aliases=aliases,
        compiler_params=GRANT,
    )(*arrays)


def exchange(n, slots):
    order = list(range(n // 2, n)) + list(range(1, n // 2))
    arrived = {r: lax.ppermute(slots[r], "pencil", [(i, i ^ r) for i in range(n)]) for r in order}
    return [slots[0]] + [arrived[r] for r in range(1, n)]


def swap(slots):
    return [lax.ppermute(slot, "field", [(0, 1), (1, 0)]) for slot in slots]


def pipelined(n, state, tangents, d1, d2, filt, advect, diffuse, coef, rates):
    params = range(tangents.shape[0])
    here = state.shape[0] // 2
    scalars = (rates, coef, advect, diffuse)

    def forth(q):
        return x_call(n, q, scalars, state, tangents, d1, d2, filt, here)

    own = exchange(n, forth(None))
    sent = [exchange(n, forth(q)) for q in params]
    turned = (d1.T, d2.T, filt.T)
    other = swap(own)

    def turn(q):
        return y_call(n, q, len(params), scalars, own, other, None if q is None else sent[q], turned)

    mine = exchange(n, turn(None))
    theirs = swap(mine)
    buffer = None
    for q in params:
        back = exchange(n, turn(q))
        buffer = place_tangent(n, q, tangents.shape, back, buffer)
    return (place_state(n, state.shape, mine, theirs), buffer)


def solution(mesh):
    in_specs = (
        P("parts", "slab", "pencil", None),
        P(("parts", "field"), None, "slab", "pencil", None),
        P(),
        P(),
        P(),
        P(),
        P(),
        P(),
        P(),
    )
    out_specs = (
        P("parts", "slab", "pencil", None),
        P(("parts", "field"), None, "slab", "pencil", None),
    )
    n = mesh.shape["pencil"]

    def step(state, tangents, *others):
        count, planes, _, length = state.shape
        count //= mesh.shape["parts"]
        params_here = tangents.shape[0] // (mesh.shape["parts"] * mesh.shape["field"])
        fits = (
            n & (n - 1) == 0
            and mesh.shape["field"] == 2
            and count * DEPTH == WIDE
            and others[-1].shape[0] == count
            and params_here * 2 == count
            and planes == mesh.shape["slab"]
            and n * LANES == length == state.shape[2]
            and length % WIDE == 0
        )
        local = functools.partial(pipelined, n) if fits else plain
        call = jax.shard_map(local, mesh=mesh, in_specs=in_specs, out_specs=out_specs, check_vma=False)
        return call(state, tangents, *others)

    return step
```

profile of v0, /device:TPU:0, one launch (start us, length us, event | category | flops | bytes accessed | tf_op | source)
XLA Modules:
  0.0 226.2 jit_solution(6887884612317035857)
XLA Ops:
  0.6 7.3 %shard_map.104 = (bf16[4,128,128]{2,1,0:T(8,128)(2,1)}, bf16[4,128,128]{2,1,0:T(8,128)(2,1)}, bf16[4,128,128]{2,1,0:T(8,128)(2,1)}, bf16[4,128,128]{2,1,0:T(8,128)(2,1)}) custom-call(f32[8,8]{1,0:T(8,128)} %rates.19, f32[8,8]{1,0:T(8,128)} %coef.19, f32[2,8]{1,0:T(2,128)} %advect.19, f32[8]{0:T(128)} %diffuse.19, bf16[8,1,128,512]{3,2,1,0:T(8,128)(2,1)} %state.9, ...), custom_call_target="tpu_custom_call" | custom-call | flops 805306368 | bytes 1048576 | tf_op jit(solution)/shard_map/pallas_call | solution.py:279
  7.9 3.1 %collective-permute-start = (bf16[4,128,128]{2,1,0:T(8,128)(2,1)}, bf16[4,128,128]{2,1,0:T(8,128)(2,1)S(1)}, u32[]{:S(2)}, u32[]{:S(2)}) collective-permute-start(bf16[4,128,128]{2,1,0:T(8,128)(2,1)} %get-tuple-element.43), channel_id=1, source_target_pairs={{0,4},{4,0},{8,12},{12,8},{1,5},{5,1},{9,13},{13,9},{2,6},{6,2},{1... | collective-permute-start | bytes 393224 | tf_op jit(solution)/shard_map/ppermute | solution.py:351
  11.0 2.6 %collective-permute-start.1 = (bf16[4,128,128]{2,1,0:T(8,128)(2,1)}, bf16[4,128,128]{2,1,0:T(8,128)(2,1)S(1)}, u32[]{:S(2)}, u32[]{:S(2)}) collective-permute-start(bf16[4,128,128]{2,1,0:T(8,128)(2,1)} %get-tuple-element.44), channel_id=1, source_target_pairs={{0,8},{4,12},{8,0},{12,4},{1,9},{5,13},{9,1},{13,5},{2,10},{6,14},... | collective-permute-start | bytes 393224 | tf_op jit(solution)/shard_map/ppermute | solution.py:351
  13.6 8.5 %shard_map.112 = (bf16[8,128,128]{2,1,0:T(8,128)(2,1)}, bf16[8,128,128]{2,1,0:T(8,128)(2,1)}, bf16[8,128,128]{2,1,0:T(8,128)(2,1)}, bf16[8,128,128]{2,1,0:T(8,128)(2,1)}) custom-call(f32[8,8]{1,0:T(8,128)} %rates.19, f32[8,8]{1,0:T(8,128)} %coef.19, f32[2,8]{1,0:T(2,128)} %advect.19, f32[8]{0:T(128)} %diffuse.19, bf16[8,1,128,512]{3,2,1,0:T(8,128)(2,1)} %state.9, ...), custom_call_target="tpu_custom_call" | custom-call | flops 1610612736 | bytes 2097152 | tf_op jit(solution)/shard_map/pallas_call | solution.py:279
  23.1 3.5 %collective-permute-start.33 = (bf16[8,128,128]{2,1,0:T(8,128)(2,1)}, bf16[8,128,128]{2,1,0:T(8,128)(2,1)S(1)}, u32[]{:S(2)}, u32[]{:S(2)}) collective-permute-start(bf16[8,128,128]{2,1,0:T(8,128)(2,1)} %get-tuple-element.76), channel_id=1, source_target_pairs={{0,8},{4,12},{8,0},{12,4},{1,9},{5,13},{9,1},{13,5},{2,10},{6,14},... | collective-permute-start | bytes 786440 | tf_op jit(solution)/shard_map/ppermute | solution.py:351
  26.6 8.6 %shard_map.110 = (bf16[8,128,128]{2,1,0:T(8,128)(2,1)}, bf16[8,128,128]{2,1,0:T(8,128)(2,1)}, bf16[8,128,128]{2,1,0:T(8,128)(2,1)}, bf16[8,128,128]{2,1,0:T(8,128)(2,1)}) custom-call(f32[8,8]{1,0:T(8,128)} %rates.19, f32[8,8]{1,0:T(8,128)} %coef.19, f32[2,8]{1,0:T(2,128)} %advect.19, f32[8]{0:T(128)} %diffuse.19, bf16[8,1,128,512]{3,2,1,0:T(8,128)(2,1)} %state.9, ...), custom_call_target="tpu_custom_call" | custom-call | flops 1610612736 | bytes 2097152 | tf_op jit(solution)/shard_map/pallas_call | solution.py:279
  35.9 8.5 %shard_map.108 = (bf16[8,128,128]{2,1,0:T(8,128)(2,1)}, bf16[8,128,128]{2,1,0:T(8,128)(2,1)}, bf16[8,128,128]{2,1,0:T(8,128)(2,1)}, bf16[8,128,128]{2,1,0:T(8,128)(2,1)}) custom-call(f32[8,8]{1,0:T(8,128)} %rates.19, f32[8,8]{1,0:T(8,128)} %coef.19, f32[2,8]{1,0:T(2,128)} %advect.19, f32[8]{0:T(128)} %diffuse.19, bf16[8,1,128,512]{3,2,1,0:T(8,128)(2,1)} %state.9, ...), custom_call_target="tpu_custom_call" | custom-call | flops 1610612736 | bytes 2097152 | tf_op jit(solution)/shard_map/pallas_call | solution.py:279
  46.6 3.5 %collective-permute-start.27 = (bf16[8,128,128]{2,1,0:T(8,128)(2,1)}, bf16[8,128,128]{2,1,0:T(8,128)(2,1)S(1)}, u32[]{:S(2)}, u32[]{:S(2)}) collective-permute-start(bf16[8,128,128]{2,1,0:T(8,128)(2,1)} %get-tuple-element.68), channel_id=1, source_target_pairs={{0,8},{4,12},{8,0},{12,4},{1,9},{5,13},{9,1},{13,5},{2,10},{6,14},... | collective-permute-start | bytes 786440 | tf_op jit(solution)/shard_map/ppermute | solution.py:351
  51.6 3.8 %collective-permute-start.21 = (bf16[8,128,128]{2,1,0:T(8,128)(2,1)}, bf16[8,128,128]{2,1,0:T(8,128)(2,1)S(1)}, u32[]{:S(2)}, u32[]{:S(2)}) collective-permute-start(bf16[8,128,128]{2,1,0:T(8,128)(2,1)} %get-tuple-element.60), channel_id=1, source_target_pairs={{0,8},{4,12},{8,0},{12,4},{1,9},{5,13},{9,1},{13,5},{2,10},{6,14},... | collective-permute-start | bytes 786440 | tf_op jit(solution)/shard_map/ppermute | solution.py:351
  55.4 8.6 %shard_map.106 = (bf16[8,128,128]{2,1,0:T(8,128)(2,1)}, bf16[8,128,128]{2,1,0:T(8,128)(2,1)}, bf16[8,128,128]{2,1,0:T(8,128)(2,1)}, bf16[8,128,128]{2,1,0:T(8,128)(2,1)}) custom-call(f32[8,8]{1,0:T(8,128)} %rates.19, f32[8,8]{1,0:T(8,128)} %coef.19, f32[2,8]{1,0:T(2,128)} %advect.19, f32[8]{0:T(128)} %diffuse.19, bf16[8,1,128,512]{3,2,1,0:T(8,128)(2,1)} %state.9, ...), custom_call_target="tpu_custom_call" | custom-call | flops 1610612736 | bytes 2097152 | tf_op jit(solution)/shard_map/pallas_call | solution.py:279
  64.8 4.0 %collective-permute-done.27.rest_10_ = bf16[8,128,128]{2,1,0:T(8,128)(2,1)S(1)} collective-permute-done((bf16[8,128,128]{2,1,0:T(8,128)(2,1)}, bf16[8,128,128]{2,1,0:T(8,128)(2,1)S(1)}, u32[]{:S(2)}, u32[]{:S(2)}) %collective-permute-start.27) | collective-permute-done | bytes 262176 | tf_op jit(solution)/shard_map/ppermute | solution.py:351
  70.2 17.6 %collective-permute-start.15 = (bf16[8,128,128]{2,1,0:T(8,128)(2,1)}, bf16[8,128,128]{2,1,0:T(8,128)(2,1)S(1)}, u32[]{:S(2)}, u32[]{:S(2)}) collective-permute-start(bf16[8,128,128]{2,1,0:T(8,128)(2,1)} %get-tuple-element.52), channel_id=1, source_target_pairs={{0,8},{4,12},{8,0},{12,4},{1,9},{5,13},{9,1},{13,5},{2,10},{6,14},... | collective-permute-start | bytes 786440 | tf_op jit(solution)/shard_map/ppermute | solution.py:351
  97.4 6.9 %shard_map.105 = (bf16[4,128,128]{2,1,0:T(8,128)(2,1)S(1)}, bf16[4,128,128]{2,1,0:T(8,128)(2,1)S(1)}, bf16[4,128,128]{2,1,0:T(8,128)(2,1)S(1)}, bf16[4,128,128]{2,1,0:T(8,128)(2,1)S(1)}) custom-call(f32[8,8]{1,0:T(8,128)S(1)} %copy-done, f32[8,8]{1,0:T(8,128)S(1)} %copy-done.1, f32[2,8]{1,0:T(2,128)S(1)} %copy-done.2, f32[8]{0:T(128)S(1)} %copy-done.3, ...), custom_call_target="tpu_custom_call" | custom-call | flops 805306368 | bytes 1048576 | tf_op jit(solution)/shard_map/pallas_call | solution.py:299
  107.2 10.8 %shard_map.113 = (bf16[8,128,128]{2,1,0:T(8,128)(2,1)S(1)}, bf16[8,128,128]{2,1,0:T(8,128)(2,1)S(1)}, bf16[8,128,128]{2,1,0:T(8,128)(2,1)S(1)}, bf16[8,128,128]{2,1,0:T(8,128)(2,1)S(1)}) custom-call(f32[8,8]{1,0:T(8,128)S(1)} %copy-done, f32[8,8]{1,0:T(8,128)S(1)} %copy-done.1, f32[2,8]{1,0:T(2,128)S(1)} %copy-done.2, f32[8]{0:T(128)S(1)} %copy-done.3, ...), custom_call_target="tpu_custom_call" | custom-call | flops 1610612736 | bytes 2097152 | tf_op jit(solution)/shard_map/pallas_call | solution.py:299
  118.0 2.1 collective-permute-start.35
  123.0 2.4 %collective-permute-start.9 = (bf16[4,128,128]{2,1,0:T(8,128)(2,1)S(1)}, bf16[4,128,128]{2,1,0:T(8,128)(2,1)S(1)}, u32[]{:S(2)}, u32[]{:S(2)}) collective-permute-start(bf16[4,128,128]{2,1,0:T(8,128)(2,1)S(1)} %get-tuple-element.49), channel_id=1, source_target_pairs={{0,12},{4,8},{8,4},{12,0},{1,13},{5,9},{9,5},{13,1},{2,14},{6,10},... | collective-permute-start | bytes 393224 | tf_op jit(solution)/shard_map/ppermute | solution.py:351
  125.4 10.7 %shard_map.111 = (bf16[8,128,128]{2,1,0:T(8,128)(2,1)S(1)}, bf16[8,128,128]{2,1,0:T(8,128)(2,1)S(1)}, bf16[8,128,128]{2,1,0:T(8,128)(2,1)S(1)}, bf16[8,128,128]{2,1,0:T(8,128)(2,1)S(1)}) custom-call(f32[8,8]{1,0:T(8,128)S(1)} %copy-done, f32[8,8]{1,0:T(8,128)S(1)} %copy-done.1, f32[2,8]{1,0:T(2,128)S(1)} %copy-done.2, f32[8]{0:T(128)S(1)} %copy-done.3, ...), custom_call_target="tpu_custom_call" | custom-call | flops 1610612736 | bytes 2097152 | tf_op jit(solution)/shard_map/pallas_call | solution.py:299
  136.1 9.8 %collective-permute-done.8.rest_2_ = bf16[4,128,128]{2,1,0:T(8,128)(2,1)S(1)} collective-permute-done((bf16[4,128,128]{2,1,0:T(8,128)(2,1)S(1)}, bf16[4,128,128]{2,1,0:T(8,128)(2,1)S(1)}, u32[]{:S(2)}, u32[]{:S(2)}) %collective-permute-start.8) | collective-permute-done | bytes 131104 | tf_op jit(solution)/shard_map/ppermute | solution.py:351
  145.9 9.0 %collective-permute-start.29 = (bf16[8,128,128]{2,1,0:T(8,128)(2,1)S(1)}, bf16[8,128,128]{2,1,0:T(8,128)(2,1)S(1)}, u32[]{:S(2)}, u32[]{:S(2)}) collective-permute-start(bf16[8,128,128]{2,1,0:T(8,128)(2,1)S(1)} %get-tuple-element.71), channel_id=1, source_target_pairs={{0,4},{4,0},{8,12},{12,8},{1,5},{5,1},{9,13},{13,9},{2,6},{6,2},{1... | collective-permute-start | bytes 786440 | tf_op jit(solution)/shard_map/ppermute | solution.py:351
  154.9 10.9 %shard_map.109 = (bf16[8,128,128]{2,1,0:T(8,128)(2,1)S(1)}, bf16[8,128,128]{2,1,0:T(8,128)(2,1)S(1)}, bf16[8,128,128]{2,1,0:T(8,128)(2,1)S(1)}, bf16[8,128,128]{2,1,0:T(8,128)(2,1)S(1)}) custom-call(f32[8,8]{1,0:T(8,128)S(1)} %copy-done, f32[8,8]{1,0:T(8,128)S(1)} %copy-done.1, f32[2,8]{1,0:T(2,128)S(1)} %copy-done.2, f32[8]{0:T(128)S(1)} %copy-done.3, ...), custom_call_target="tpu_custom_call" | custom-call | flops 1610612736 | bytes 2097152 | tf_op jit(solution)/shard_map/pallas_call | solution.py:299
  165.8 2.4 %collective-permute-start.31 = (bf16[8,128,128]{2,1,0:T(8,128)(2,1)S(1)}, bf16[8,128,128]{2,1,0:T(8,128)(2,1)S(1)}, u32[]{:S(2)}, u32[]{:S(2)}) collective-permute-start(bf16[8,128,128]{2,1,0:T(8,128)(2,1)S(1)} %get-tuple-element.73), channel_id=1, source_target_pairs={{0,12},{4,8},{8,4},{12,0},{1,13},{5,9},{9,5},{13,1},{2,14},{6,10},... | collective-permute-start | bytes 786440 | tf_op jit(solution)/shard_map/ppermute | solution.py:351
  171.2 10.6 %shard_map.107 = (bf16[8,128,128]{2,1,0:T(8,128)(2,1)S(1)}, bf16[8,128,128]{2,1,0:T(8,128)(2,1)S(1)}, bf16[8,128,128]{2,1,0:T(8,128)(2,1)S(1)}, bf16[8,128,128]{2,1,0:T(8,128)(2,1)S(1)}) custom-call(f32[8,8]{1,0:T(8,128)S(1)} %copy-done, f32[8,8]{1,0:T(8,128)S(1)} %copy-done.1, f32[2,8]{1,0:T(2,128)S(1)} %copy-done.2, f32[8]{0:T(128)S(1)} %copy-done.3, ...), custom_call_target="tpu_custom_call" | custom-call | flops 1610612736 | bytes 2097152 | tf_op jit(solution)/shard_map/pallas_call | solution.py:299
  192.7 9.7 %collective-permute-done.24.rest_2_ = bf16[8,128,128]{2,1,0:T(8,128)(2,1)S(1)} collective-permute-done((bf16[8,128,128]{2,1,0:T(8,128)(2,1)S(1)}, bf16[8,128,128]{2,1,0:T(8,128)(2,1)S(1)}, u32[]{:S(2)}, u32[]{:S(2)}) %collective-permute-start.24) | collective-permute-done | bytes 262176 | tf_op jit(solution)/shard_map/ppermute | solution.py:351
  204.0 20.6 %collective-permute-done.18.rest_2_ = bf16[8,128,128]{2,1,0:T(8,128)(2,1)S(1)} collective-permute-done((bf16[8,128,128]{2,1,0:T(8,128)(2,1)S(1)}, bf16[8,128,128]{2,1,0:T(8,128)(2,1)S(1)}, u32[]{:S(2)}, u32[]{:S(2)}) %collective-permute-start.18) | collective-permute-done | bytes 262176 | tf_op jit(solution)/shard_map/ppermute | solution.py:351
  (150 shorter events, 39.7 us)
Async XLA Ops:
  13.6 21.6 %collective-permute-start.2 = (bf16[4,128,128]{2,1,0:T(8,128)(2,1)}, bf16[4,128,128]{2,1,0:T(8,128)(2,1)S(1)}, u32[]{:S(2)}, u32[]{:S(2)}) collective-permute-start(bf16[4,128,128]{2,1,0:T(8,128)(2,1)} %get-tuple-element.45), channel_id=1, source_target_pairs={{0,12},{4,8},{8,4},{12,0},{1,13},{5,9},{9,5},{13,1},{2,14},{6,10},... | collective-permute-start | bytes 393224 | tf_op jit(solution)/shard_map/ppermute | solution.py:351
  13.6 21.8 %collective-permute-start.3 = (bf16[4,128,128]{2,1,0:T(8,128)(2,1)}, bf16[4,128,128]{2,1,0:T(8,128)(2,1)S(1)}, u32[]{:S(2)}, u32[]{:S(2)}) collective-permute-start(bf16[4,128,128]{2,1,0:T(8,128)(2,1)} %get-tuple-element.42.rest_0_), channel_id=1, source_target_pairs={{0,1},{1,0},{2,3},{3,2},{4,5},{5,4},{6,7},{7,6},{8,9},{9,8},{10,11... | collective-permute-start | bytes 393224 | tf_op jit(solution)/shard_map/ppermute | solution.py:356
  22.1 28.0 %collective-permute-start.32 = (bf16[8,128,128]{2,1,0:T(8,128)(2,1)}, bf16[8,128,128]{2,1,0:T(8,128)(2,1)S(1)}, u32[]{:S(2)}, u32[]{:S(2)}) collective-permute-start(bf16[8,128,128]{2,1,0:T(8,128)(2,1)} %get-tuple-element.75), channel_id=1, source_target_pairs={{0,4},{4,0},{8,12},{12,8},{1,5},{5,1},{9,13},{13,9},{2,6},{6,2},{1... | collective-permute-start | bytes 786440 | tf_op jit(solution)/shard_map/ppermute | solution.py:351
  23.1 27.2 %collective-permute-start.33 = (bf16[8,128,128]{2,1,0:T(8,128)(2,1)}, bf16[8,128,128]{2,1,0:T(8,128)(2,1)S(1)}, u32[]{:S(2)}, u32[]{:S(2)}) collective-permute-start(bf16[8,128,128]{2,1,0:T(8,128)(2,1)} %get-tuple-element.76), channel_id=1, source_target_pairs={{0,8},{4,12},{8,0},{12,4},{1,9},{5,13},{9,1},{13,5},{2,10},{6,14},... | collective-permute-start | bytes 786440 | tf_op jit(solution)/shard_map/ppermute | solution.py:351
  46.6 22.2 %collective-permute-start.27 = (bf16[8,128,128]{2,1,0:T(8,128)(2,1)}, bf16[8,128,128]{2,1,0:T(8,128)(2,1)S(1)}, u32[]{:S(2)}, u32[]{:S(2)}) collective-permute-start(bf16[8,128,128]{2,1,0:T(8,128)(2,1)} %get-tuple-element.68), channel_id=1, source_target_pairs={{0,8},{4,12},{8,0},{12,4},{1,9},{5,13},{9,1},{13,5},{2,10},{6,14},... | collective-permute-start | bytes 786440 | tf_op jit(solution)/shard_map/ppermute | solution.py:351
  50.3 37.5 %collective-permute-start.20 = (bf16[8,128,128]{2,1,0:T(8,128)(2,1)}, bf16[8,128,128]{2,1,0:T(8,128)(2,1)S(1)}, u32[]{:S(2)}, u32[]{:S(2)}) collective-permute-start(bf16[8,128,128]{2,1,0:T(8,128)(2,1)} %get-tuple-element.59), channel_id=1, source_target_pairs={{0,4},{4,0},{8,12},{12,8},{1,5},{5,1},{9,13},{13,9},{2,6},{6,2},{1... | collective-permute-start | bytes 786440 | tf_op jit(solution)/shard_map/ppermute | solution.py:351
  51.6 52.7 %collective-permute-start.21 = (bf16[8,128,128]{2,1,0:T(8,128)(2,1)}, bf16[8,128,128]{2,1,0:T(8,128)(2,1)S(1)}, u32[]{:S(2)}, u32[]{:S(2)}) collective-permute-start(bf16[8,128,128]{2,1,0:T(8,128)(2,1)} %get-tuple-element.60), channel_id=1, source_target_pairs={{0,8},{4,12},{8,0},{12,4},{1,9},{5,13},{9,1},{13,5},{2,10},{6,14},... | collective-permute-start | bytes 786440 | tf_op jit(solution)/shard_map/ppermute | solution.py:351
  64.6 53.4 %collective-permute-start.22 = (bf16[8,128,128]{2,1,0:T(8,128)(2,1)}, bf16[8,128,128]{2,1,0:T(8,128)(2,1)}, u32[]{:S(2)}, u32[]{:S(2)}) collective-permute-start(bf16[8,128,128]{2,1,0:T(8,128)(2,1)} %get-tuple-element.61), channel_id=1, source_target_pairs={{0,12},{4,8},{8,4},{12,0},{1,13},{5,9},{9,5},{13,1},{2,14},{6,10},... | collective-permute-start | bytes 786440 | tf_op jit(solution)/shard_map/ppermute | solution.py:351
  69.5 50.6 %collective-permute-start.14 = (bf16[8,128,128]{2,1,0:T(8,128)(2,1)}, bf16[8,128,128]{2,1,0:T(8,128)(2,1)S(1)}, u32[]{:S(2)}, u32[]{:S(2)}) collective-permute-start(bf16[8,128,128]{2,1,0:T(8,128)(2,1)} %get-tuple-element.51), channel_id=1, source_target_pairs={{0,4},{4,0},{8,12},{12,8},{1,5},{5,1},{9,13},{13,9},{2,6},{6,2},{1... | collective-permute-start | bytes 786440 | tf_op jit(solution)/shard_map/ppermute | solution.py:351
  70.2 50.9 %collective-permute-start.15 = (bf16[8,128,128]{2,1,0:T(8,128)(2,1)}, bf16[8,128,128]{2,1,0:T(8,128)(2,1)S(1)}, u32[]{:S(2)}, u32[]{:S(2)}) collective-permute-start(bf16[8,128,128]{2,1,0:T(8,128)(2,1)} %get-tuple-element.52), channel_id=1, source_target_pairs={{0,8},{4,12},{8,0},{12,4},{1,9},{5,13},{9,1},{13,5},{2,10},{6,14},... | collective-permute-start | bytes 786440 | tf_op jit(solution)/shard_map/ppermute | solution.py:351
  87.8 35.2 %collective-permute-start.16 = (bf16[8,128,128]{2,1,0:T(8,128)(2,1)}, bf16[8,128,128]{2,1,0:T(8,128)(2,1)S(1)}, u32[]{:S(2)}, u32[]{:S(2)}) collective-permute-start(bf16[8,128,128]{2,1,0:T(8,128)(2,1)} %get-tuple-element.53), channel_id=1, source_target_pairs={{0,12},{4,8},{8,4},{12,0},{1,13},{5,9},{9,5},{13,1},{2,14},{6,10},... | collective-permute-start | bytes 786440 | tf_op jit(solution)/shard_map/ppermute | solution.py:351
  104.3 21.1 %collective-permute-start.7 = (bf16[4,128,128]{2,1,0:T(8,128)(2,1)S(1)}, bf16[4,128,128]{2,1,0:T(8,128)(2,1)S(1)}, u32[]{:S(2)}, u32[]{:S(2)}) collective-permute-start(bf16[4,128,128]{2,1,0:T(8,128)(2,1)S(1)} %get-tuple-element.47), channel_id=1, source_target_pairs={{0,4},{4,0},{8,12},{12,8},{1,5},{5,1},{9,13},{13,9},{2,6},{6,2},{1... | collective-permute-start | bytes 393224 | tf_op jit(solution)/shard_map/ppermute | solution.py:351
  118.0 47.8 %collective-permute-start.35 = (bf16[8,128,128]{2,1,0:T(8,128)(2,1)S(1)}, bf16[8,128,128]{2,1,0:T(8,128)(2,1)S(1)}, u32[]{:S(2)}, u32[]{:S(2)}) collective-permute-start(bf16[8,128,128]{2,1,0:T(8,128)(2,1)S(1)} %get-tuple-element.79), channel_id=1, source_target_pairs={{0,4},{4,0},{8,12},{12,8},{1,5},{5,1},{9,13},{13,9},{2,6},{6,2},{1... | collective-permute-start | bytes 786440 | tf_op jit(solution)/shard_map/ppermute | solution.py:351
  120.1 48.1 %collective-permute-start.36 = (bf16[8,128,128]{2,1,0:T(8,128)(2,1)S(1)}, bf16[8,128,128]{2,1,0:T(8,128)(2,1)S(1)}, u32[]{:S(2)}, u32[]{:S(2)}) collective-permute-start(bf16[8,128,128]{2,1,0:T(8,128)(2,1)S(1)} %get-tuple-element.80), channel_id=1, source_target_pairs={{0,8},{4,12},{8,0},{12,4},{1,9},{5,13},{9,1},{13,5},{2,10},{6,14},... | collective-permute-start | bytes 786440 | tf_op jit(solution)/shard_map/ppermute | solution.py:351
  121.1 24.8 %collective-permute-start.8 = (bf16[4,128,128]{2,1,0:T(8,128)(2,1)S(1)}, bf16[4,128,128]{2,1,0:T(8,128)(2,1)S(1)}, u32[]{:S(2)}, u32[]{:S(2)}) collective-permute-start(bf16[4,128,128]{2,1,0:T(8,128)(2,1)S(1)} %get-tuple-element.48), channel_id=1, source_target_pairs={{0,8},{4,12},{8,0},{12,4},{1,9},{5,13},{9,1},{13,5},{2,10},{6,14},... | collective-permute-start | bytes 393224 | tf_op jit(solution)/shard_map/ppermute | solution.py:351
  123.0 22.9 %collective-permute-start.9 = (bf16[4,128,128]{2,1,0:T(8,128)(2,1)S(1)}, bf16[4,128,128]{2,1,0:T(8,128)(2,1)S(1)}, u32[]{:S(2)}, u32[]{:S(2)}) collective-permute-start(bf16[4,128,128]{2,1,0:T(8,128)(2,1)S(1)} %get-tuple-element.49), channel_id=1, source_target_pairs={{0,12},{4,8},{8,4},{12,0},{1,13},{5,9},{9,5},{13,1},{2,14},{6,10},... | collective-permute-start | bytes 393224 | tf_op jit(solution)/shard_map/ppermute | solution.py:351
  125.4 29.5 %collective-permute-start.10 = (bf16[4,128,128]{2,1,0:T(8,128)(2,1)S(1)}, bf16[4,128,128]{2,1,0:T(8,128)(2,1)S(1)}, u32[]{:S(2)}, u32[]{:S(2)}) collective-permute-start(bf16[4,128,128]{2,1,0:T(8,128)(2,1)S(1)} %get-tuple-element.46.rest_0_), channel_id=1, source_target_pairs={{0,1},{1,0},{2,3},{3,2},{4,5},{5,4},{6,7},{7,6},{8,9},{9,8},{10,11... | collective-permute-start | bytes 393224 | tf_op jit(solution)/shard_map/ppermute | solution.py:356
  145.9 23.5 %collective-permute-start.37 = (bf16[8,128,128]{2,1,0:T(8,128)(2,1)S(1)}, bf16[8,128,128]{2,1,0:T(8,128)(2,1)S(1)}, u32[]{:S(2)}, u32[]{:S(2)}) collective-permute-start(bf16[8,128,128]{2,1,0:T(8,128)(2,1)S(1)} %get-tuple-element.81), channel_id=1, source_target_pairs={{0,12},{4,8},{8,4},{12,0},{1,13},{5,9},{9,5},{13,1},{2,14},{6,10},... | collective-permute-start | bytes 786440 | tf_op jit(solution)/shard_map/ppermute | solution.py:351
  145.9 23.5 %collective-permute-start.29 = (bf16[8,128,128]{2,1,0:T(8,128)(2,1)S(1)}, bf16[8,128,128]{2,1,0:T(8,128)(2,1)S(1)}, u32[]{:S(2)}, u32[]{:S(2)}) collective-permute-start(bf16[8,128,128]{2,1,0:T(8,128)(2,1)S(1)} %get-tuple-element.71), channel_id=1, source_target_pairs={{0,4},{4,0},{8,12},{12,8},{1,5},{5,1},{9,13},{13,9},{2,6},{6,2},{1... | collective-permute-start | bytes 786440 | tf_op jit(solution)/shard_map/ppermute | solution.py:351
  181.8 20.6 %collective-permute-start.24 = (bf16[8,128,128]{2,1,0:T(8,128)(2,1)S(1)}, bf16[8,128,128]{2,1,0:T(8,128)(2,1)S(1)}, u32[]{:S(2)}, u32[]{:S(2)}) collective-permute-start(bf16[8,128,128]{2,1,0:T(8,128)(2,1)S(1)} %get-tuple-element.64), channel_id=1, source_target_pairs={{0,8},{4,12},{8,0},{12,4},{1,9},{5,13},{9,1},{13,5},{2,10},{6,14},... | collective-permute-start | bytes 786440 | tf_op jit(solution)/shard_map/ppermute | solution.py:351
  181.9 20.5 %collective-permute-start.25 = (bf16[8,128,128]{2,1,0:T(8,128)(2,1)S(1)}, bf16[8,128,128]{2,1,0:T(8,128)(2,1)S(1)}, u32[]{:S(2)}, u32[]{:S(2)}) collective-permute-start(bf16[8,128,128]{2,1,0:T(8,128)(2,1)S(1)} %get-tuple-element.65), channel_id=1, source_target_pairs={{0,12},{4,8},{8,4},{12,0},{1,13},{5,9},{9,5},{13,1},{2,14},{6,10},... | collective-permute-start | bytes 786440 | tf_op jit(solution)/shard_map/ppermute | solution.py:351
  183.9 20.0 %collective-permute-start.17 = (bf16[8,128,128]{2,1,0:T(8,128)(2,1)S(1)}, bf16[8,128,128]{2,1,0:T(8,128)(2,1)S(1)}, u32[]{:S(2)}, u32[]{:S(2)}) collective-permute-start(bf16[8,128,128]{2,1,0:T(8,128)(2,1)S(1)} %get-tuple-element.55), channel_id=1, source_target_pairs={{0,4},{4,0},{8,12},{12,8},{1,5},{5,1},{9,13},{13,9},{2,6},{6,2},{1... | collective-permute-start | bytes 786440 | tf_op jit(solution)/shard_map/ppermute | solution.py:351
  185.4 39.2 %collective-permute-start.18 = (bf16[8,128,128]{2,1,0:T(8,128)(2,1)S(1)}, bf16[8,128,128]{2,1,0:T(8,128)(2,1)S(1)}, u32[]{:S(2)}, u32[]{:S(2)}) collective-permute-start(bf16[8,128,128]{2,1,0:T(8,128)(2,1)S(1)} %get-tuple-element.56), channel_id=1, source_target_pairs={{0,8},{4,12},{8,0},{12,4},{1,9},{5,13},{9,1},{13,5},{2,10},{6,14},... | collective-permute-start | bytes 786440 | tf_op jit(solution)/shard_map/ppermute | solution.py:351
  186.4 38.3 %collective-permute-start.19 = (bf16[8,128,128]{2,1,0:T(8,128)(2,1)S(1)}, bf16[8,128,128]{2,1,0:T(8,128)(2,1)S(1)}, u32[]{:S(2)}, u32[]{:S(2)}) collective-permute-start(bf16[8,128,128]{2,1,0:T(8,128)(2,1)S(1)} %get-tuple-element.57), channel_id=1, source_target_pairs={{0,12},{4,8},{8,4},{12,0},{1,13},{5,9},{9,5},{13,1},{2,14},{6,10},... | collective-permute-start | bytes 786440 | tf_op jit(solution)/shard_map/ppermute | solution.py:351
  (54 other events, 947.3 us)
where the time goes:
time: 230 us; the launch traced here: 226 us
  Pallas kernels  98.8 us (43%)
  starting transfers between devices  65.8 us (29%)
  waiting for transfers between devices  45.5 us (20%)
  local copies, waits for them, and re-layouts  15 us (7%)
    ppermute x30, starting transfers between devices, exchange(): lax.ppermute(slots[r], 'pencil', [(i, i ^ r) for i in range(n)])  64.7 us
    pallas_call x5, Pallas kernels, y_call(): pl.pallas_call(functools.partial(y_kernel, n, q, params_here), out_shape=...  49.8 us
    ppermute x30, waiting for transfers between devices, exchange(): lax.ppermute(slots[r], 'pencil', [(i, i ^ r) for i in range(n)])  45.5 us
    pallas_call x5, Pallas kernels, x_call(): pl.pallas_call(functools.partial(x_kernel, n, q, None if q is None else t...  41.5 us
    unnamed x83, local copies, waits for them, and re-layouts  15 us
    pallas_call x4, Pallas kernels, place_tangent(): pl.pallas_call(functools.partial(place_kernel, n, 1), grid=(count // part...  6.34 us
  transfers between devices with their start and end apart: 38, of which 5 were waited for; matrix products, arithmetic and copies ran while one was open for 1% of the time, Pallas kernels for 40%

commit v1 on v0

--- a/solution.py
+++ b/solution.py
@@ -111,47 +111,88 @@
     return (v.astype(f32) + time_step * (diffusivity * curve - speed * slope + rate)).astype(bf16)
 
 
-def x_kernel(n, q, params_here, rates, coef, advect, diffuse, state, *rest):
-    if q is not None:
-        tangent, rest = rest[0], rest[1:]
-    d1, d2, filt = rest[:3]
-    outs, rest = rest[3 : 3 + n], rest[3 + n :]
-    filt_own, rates_high, rates_low, coef_high, coef_low, middle = rest
+def x_state_kernel(n, rates, coef, advect, diffuse, state_far, d1_far, d2_far, filt_far, *rest):
+    outs, rest = rest[:n], rest[n:]
+    state, d1, d2, filt, filt_own, rates_high, rates_low, rate, middle, sems = rest
+    copies = [
+        pltpu.make_async_copy(far, near, sems.at[i])
+        for i, (far, near) in enumerate(
+            [(state_far, state), (d1_far, d1), (d2_far, d2), (filt_far, filt)]
+        )
+    ]
+    for copy in copies:
+        copy.start()
     me, half = lax.axis_index("pencil"), lax.axis_index("field")
-    count, rows, length = state.shape
+    count, _, rows, length = state.shape
     fields = outs[0].shape[0]
     size = length // n
-    first = half * fields if q is None else 0
-
-    @pl.when(pl.program_id(0) == 0)
-    def _():
-        fill_mixer(lambda a, b: rates[a, b], rates_high, rates_low)
-        fill_mixer(lambda a, b: coef[b, first + a], coef_high, coef_low)
-        for r in range(n):
-            filt_own[:, r * size : (r + 1) * size] = filt[:, aligned(me ^ r, size)]
-
-    source = state[pl.ds(first, fields)] if q is None else tangent[...]
-    own = source.reshape(fields * rows, length)
+    first = half * fields
+    fill_mixer(lambda a, b: rates[a, b], rates_high, rates_low)
+    copies[0].wait()
+    for j in range(rows // DEPTH):
+        down = slice(j * DEPTH, (j + 1) * DEPTH)
+        for c in range(length // WIDE):
+            across = slice(c * WIDE, (c + 1) * WIDE)
+            u = state[:, 0, down, across].reshape(count * DEPTH, WIDE)
+            activity = jnp.tanh(mixed((rates_high, rates_low), u))
+            for s in range(fields):
+                total = None
+                for p in range(rates.shape[0]):
+                    term = coef[p, first + s] * activity[p * DEPTH : (p + 1) * DEPTH]
+                    total = term if total is None else total + term
+                rate[s * rows + j * DEPTH : s * rows + (j + 1) * DEPTH, across] = total
+    own = state[pl.ds(first, fields), 0].reshape(fields * rows, length)
+    copies[1].wait()
+    copies[2].wait()
     for c in range(length // WIDE):
         across = slice(c * WIDE, (c + 1) * WIDE)
-        u = state[:, :, across].reshape(count * rows, WIDE)
-        activity = jnp.tanh(mixed((rates_high, rates_low), u))
-        if q is None:
-            scaled = activity
-        else:
-            mixing = mixed((rates_high, rates_low), own[:, across])
-            scaled = tangent_scaled(activity, mixing, half * params_here + q)
-        rate = mixed_float((coef_high, coef_low), scaled)
         slope = jnp.dot(own, d1[:, across], preferred_element_type=f32)
         curve = jnp.dot(own, d2[:, across], preferred_element_type=f32)
         for s in range(fields):
             at = slice(s * rows, (s + 1) * rows)
             middle[at, across] = advance(
-                own[at, across], curve[at], slope[at], rate[at], diffuse[first + s], advect[0, first + s]
+                own[at, across], curve[at], slope[at], rate[at, across], diffuse[first + s], advect[0, first + s]
+            )
+    copies[3].wait()
+    for r in range(n):
+        filt_own[:, r * size : (r + 1) * size] = filt[:, aligned(me ^ r, size)]
+    result = jnp.dot(middle[...], filt_own[...], preferred_element_type=f32).astype(bf16)
+    for r in range(n):
+        outs[r][...] = result[:, r * size : (r + 1) * size].reshape(fields, rows, size)
+
+
+def x_kernel(n, q, params_here, rates, coef, advect, diffuse, state, tangent, d1, d2, filt, *rest):
+    outs, rest = rest[:n], rest[n:]
+    filt_own, rates_high, rates_low, coef_high, coef_low, middle = rest
+    me, half = lax.axis_index("pencil"), lax.axis_index("field")
+    count, rows, length = state.shape
+    size = length // n
+
+    @pl.when(pl.program_id(0) == 0)
+    def _():
+        fill_mixer(lambda a, b: rates[a, b], rates_high, rates_low)
+        fill_mixer(lambda a, b: coef[b, a], coef_high, coef_low)
+        for r in range(n):
+            filt_own[:, r * size : (r + 1) * size] = filt[:, aligned(me ^ r, size)]
+
+    own = tangent[...].reshape(count * rows, length)
+    for c in range(length // WIDE):
+        across = slice(c * WIDE, (c + 1) * WIDE)
+        u = state[:, :, across].reshape(count * rows, WIDE)
+        activity = jnp.tanh(mixed((rates_high, rates_low), u))
+        mixing = mixed((rates_high, rates_low), own[:, across])
+        scaled = tangent_scaled(activity, mixing, half * params_here + q)
+        rate = mixed_float((coef_high, coef_low), scaled)
+        slope = jnp.dot(own, d1[:, across], preferred_element_type=f32)
+        curve = jnp.dot(own, d2[:, across], preferred_element_type=f32)
+        for s in range(count):
+            at = slice(s * rows, (s + 1) * rows)
+            middle[at, across] = advance(
+                own[at, across], curve[at], slope[at], rate[at], diffuse[s], advect[0, s]
             )
     result = jnp.dot(middle[...], filt_own[...], preferred_element_type=f32).astype(bf16)
     for r in range(n):
-        outs[r][...] = result[:, r * size : (r + 1) * size].reshape(fields, rows, size)
+        outs[r][...] = result[:, r * size : (r + 1) * size].reshape(count, rows, size)
 
 
 def y_kernel(n, q, params_here, rates, coef, advect, diffuse, *rest):
@@ -235,21 +276,25 @@
     lax.fori_loop(0, fields // 2, two_fields, 0)
 
 
-def place_kernel(n, slots_of, *rest):
+def place_kernel(n, q, *rest):
+    out, sems = rest[-2:]
     me, half = lax.axis_index("pencil"), lax.axis_index("field")
-    out = rest[-1]
-    slots = rest[: n * slots_of]
-    here = slots[0].shape[0]
-    size = slots[0].shape[2]
-    for g in range(slots_of):
+    groups = 2 if q is None else 1
+    copies = []
+    for g in range(groups):
         for r in range(n):
-            slot = slots[g * n + r]
-            for s in range(here):
-                if slots_of == 1:
-                    out[0, s, 0, :, aligned(me ^ r, size)] = slot[s]
-                else:
-                    at = (half if g == 0 else 1 - half) * here + s
-                    out[at, 0, :, aligned(me ^ r, size)] = slot[s]
+            slot = rest[g * n + r]
+            here, _, size = slot.shape
+            across = aligned(me ^ r, size)
+            if q is None:
+                target = out.at[aligned(half if g == 0 else 1 - half, here), 0, :, across]
+            else:
+                target = out.at[q, :, 0, :, across]
+            copies.append(pltpu.make_async_copy(slot, target, sems.at[g * n + r]))
+    for copy in copies:
+        copy.start()
+    for copy in copies:
+        copy.wait()
 
 
 SMEM = pl.BlockSpec(memory_space=pltpu.SMEM)
@@ -266,28 +311,46 @@
     return [pltpu.VMEM((fields * DEPTH, count * DEPTH), bf16)] * 2
 
 
-def x_call(n, q, scalars, state, tangents, d1, d2, filt, here):
+def x_state_call(n, scalars, state, d1, d2, filt, here):
     count, _, deep, length = state.shape
+    square = pltpu.VMEM((length, length), bf16)
+    return pl.pallas_call(
+        functools.partial(x_state_kernel, n),
+        out_shape=[jax.ShapeDtypeStruct((here, deep, length // n), bf16)] * n,
+        in_specs=[SMEM] * 4 + [HBM] * 4,
+        out_specs=[VMEM] * n,
+        scratch_shapes=[pltpu.VMEM(state.shape, bf16), square, square, square, square]
+        + mixers(count, count)
+        + [
+            pltpu.VMEM((here * deep, length), f32),
+            pltpu.VMEM((here * deep, length), bf16),
+            pltpu.SemaphoreType.DMA((4,)),
+        ],
+        cost_estimate=cost(6 * here * deep * length * length, 4 * here * deep * length),
+        name="x_state",
+    )(*scalars, state, d1, d2, filt)
+
+
+def x_call(n, q, scalars, state, tangents, d1, d2, filt):
+    params_here, count, _, deep, length = tangents.shape
     size = length // n
-    fields = here if q is None else count
     whole = pl.BlockSpec((length, length), lambda i: (0, 0))
-    arrays = [state]
-    specs = [pl.BlockSpec((count, None, DEPTH, length), lambda i: (0, 0, i, 0))]
-    if q is not None:
-        arrays.append(tangents)
-        specs.append(pl.BlockSpec((None, count, None, DEPTH, length), lambda i: (q, 0, 0, i, 0)))
     return pl.pallas_call(
-        functools.partial(x_kernel, n, q, None if q is None else tangents.shape[0]),
+        functools.partial(x_kernel, n, q, params_here),
         grid=(deep // DEPTH,),
-        out_shape=[jax.ShapeDtypeStruct((fields, deep, size), bf16)] * n,
-        in_specs=[SMEM] * 4 + specs + [whole] * 3,
-        out_specs=[pl.BlockSpec((fields, DEPTH, size), lambda i: (0, i, 0))] * n,
+        out_shape=[jax.ShapeDtypeStruct((count, deep, size), bf16)] * n,
+        in_specs=[SMEM] * 4
+        + [
+            pl.BlockSpec((count, None, DEPTH, length), lambda i: (0, 0, i, 0)),
+            pl.BlockSpec((None, count, None, DEPTH, length), lambda i: (q, 0, 0, i, 0)),
+        ]
+        + [whole] * 3,
+        out_specs=[pl.BlockSpec((count, DEPTH, size), lambda i: (0, i, 0))] * n,
         scratch_shapes=[pltpu.VMEM((length, length), bf16)]
-        + mixers(count, count)
-        + mixers(fields, count)
-        + [pltpu.VMEM((fields * DEPTH, length), bf16)],
-        cost_estimate=cost(6 * fields * deep * length * length, 4 * fields * deep * length),
-    )(*scalars, *arrays, d1, d2, filt)
+        + mixers(count, count) * 2
+        + [pltpu.VMEM((count * DEPTH, length), bf16)],
+        cost_estimate=cost(6 * count * deep * length * length, 4 * count * deep * length),
+    )(*scalars, state, tangents, d1, d2, filt)
 
 
 def y_call(n, q, params_here, scalars, own, other, arrived, turned):
@@ -316,34 +379,27 @@
 
 def place_state(n, shape, own, other):
     return pl.pallas_call(
-        functools.partial(place_kernel, n, 2),
+        functools.partial(place_kernel, n, None),
         out_shape=jax.ShapeDtypeStruct(shape, bf16),
         in_specs=[VMEM] * (2 * n),
-        out_specs=VMEM,
+        out_specs=HBM,
+        scratch_shapes=[pltpu.SemaphoreType.DMA((2 * n,))],
         compiler_params=GRANT,
         name="place_state",
     )(*own, *other)
 
 
 def place_tangent(n, q, shape, slots, buffer):
-    count, deep, size = slots[0].shape
-    part = 2
-    specs = [pl.BlockSpec((part, deep, size), lambda i: (i, 0, 0))] * n
-    arrays = list(slots)
-    aliases = {}
-    if buffer is not None:
-        specs.append(HBM)
-        arrays.append(buffer)
-        aliases = {n: 0}
+    earlier = [] if buffer is None else [buffer]
     return pl.pallas_call(
-        functools.partial(place_kernel, n, 1),
-        grid=(count // part,),
+        functools.partial(place_kernel, n, q),
         out_shape=jax.ShapeDtypeStruct(shape, bf16),
-        in_specs=specs,
-        out_specs=pl.BlockSpec((1, part, 1, deep, shape[-1]), lambda i: (q, i, 0, 0, 0)),
-        input_output_aliases=aliases,
+        in_specs=[VMEM] * n + [HBM] * len(earlier),
+        out_specs=HBM,
+        scratch_shapes=[pltpu.SemaphoreType.DMA((n,))],
+        input_output_aliases={n: 0} if earlier else {},
         compiler_params=GRANT,
-    )(*arrays)
+    )(*slots, *earlier)
 
 
 def exchange(n, slots):
@@ -362,7 +418,9 @@
     scalars = (rates, coef, advect, diffuse)
 
     def forth(q):
-        return x_call(n, q, scalars, state, tangents, d1, d2, filt, here)
+        if q is None:
+            return x_state_call(n, scalars, state, d1, d2, filt, here)
+        return x_call(n, q, scalars, state, tangents, d1, d2, filt)
 
     own = exchange(n, forth(None))
     sent = [exchange(n, forth(q)) for q in params]

time: 230 us -> 228 us (level)
  Pallas kernels: 98.8 us -> 94.6 us
    pallas_call x10, Pallas kernels: 49 us -> 44.7 us  [the longest x4 34.4 us: x_call(): pl.pallas_call(functools.partial(x_kernel, n, q, params_here), grid=(deep...]
  transfers between devices with their start and end apart: 38 -> 38, of which waited for: 5 -> 6; matrix products, arithmetic and copies ran while one was open for 1% -> 1% of each run, Pallas kernels for 40% -> 39%
where the time goes in v1:
time: 228 us; the launch traced here: 224 us
  Pallas kernels  94.6 us (41%)
  starting transfers between devices  65.8 us (29%)
  waiting for transfers between devices  47.3 us (21%)
  local copies, waits for them, and re-layouts  15 us (7%)
    ppermute x30, starting transfers between devices, exchange(): lax.ppermute(slots[r], 'pencil', [(i, i ^ r) for i in range(n)])  64.7 us
    pallas_call x5, Pallas kernels, y_call(): pl.pallas_call(functools.partial(y_kernel, n, q, params_here), out_shape=...  49.9 us
    ppermute x30, waiting for transfers between devices, exchange(): lax.ppermute(slots[r], 'pencil', [(i, i ^ r) for i in range(n)])  47.3 us
    pallas_call x4, Pallas kernels, x_call(): pl.pallas_call(functools.partial(x_kernel, n, q, params_here), grid=(deep...  34.4 us
    unnamed x83, local copies, waits for them, and re-layouts  15 us
    pallas_call x1, Pallas kernels, x_state_call(): pl.pallas_call(functools.partial(x_state_kernel, n), out_shape=[jax.Shape...  5.28 us
  transfers between devices with their start and end apart: 38, of which 6 were waited for; matrix products, arithmetic and copies ran while one was open for 1% of the time, Pallas kernels for 39%

profile of v1, /device:TPU:0, one launch (start us, length us, event | category | flops | bytes accessed | tf_op | source)
XLA Modules:
  0.0 224.1 jit_solution(10691375835441398859)
XLA Ops:
  0.6 5.3 %x_state.1 = (bf16[4,128,128]{2,1,0:T(8,128)(2,1)}, bf16[4,128,128]{2,1,0:T(8,128)(2,1)}, bf16[4,128,128]{2,1,0:T(8,128)(2,1)}, bf16[4,128,128]{2,1,0:T(8,128)(2,1)}) custom-call(f32[8,8]{1,0:T(8,128)} %rates.19, f32[8,8]{1,0:T(8,128)} %coef.19, f32[2,8]{1,0:T(2,128)} %advect.19, f32[8]{0:T(128)} %diffuse.19, bf16[8,1,128,512]{3,2,1,0:T(8,128)(2,1)} %state.7, ...), custom_call_target="tpu_custom_call" | custom-call | flops 805306368 | bytes 1048576 | tf_op jit(solution)/shard_map/x_state/pallas_call | solution.py:317
  5.9 3.1 %collective-permute-start = (bf16[4,128,128]{2,1,0:T(8,128)(2,1)}, bf16[4,128,128]{2,1,0:T(8,128)(2,1)S(1)}, u32[]{:S(2)}, u32[]{:S(2)}) collective-permute-start(bf16[4,128,128]{2,1,0:T(8,128)(2,1)} %get-tuple-element.43), channel_id=1, source_target_pairs={{0,4},{4,0},{8,12},{12,8},{1,5},{5,1},{9,13},{13,9},{2,6},{6,2},{1... | collective-permute-start | bytes 393224 | tf_op jit(solution)/shard_map/ppermute | solution.py:407
  9.0 2.6 %collective-permute-start.1 = (bf16[4,128,128]{2,1,0:T(8,128)(2,1)}, bf16[4,128,128]{2,1,0:T(8,128)(2,1)S(1)}, u32[]{:S(2)}, u32[]{:S(2)}) collective-permute-start(bf16[4,128,128]{2,1,0:T(8,128)(2,1)} %get-tuple-element.44), channel_id=1, source_target_pairs={{0,8},{4,12},{8,0},{12,4},{1,9},{5,13},{9,1},{13,5},{2,10},{6,14},... | collective-permute-start | bytes 393224 | tf_op jit(solution)/shard_map/ppermute | solution.py:407
  11.6 8.7 %shard_map.111 = (bf16[8,128,128]{2,1,0:T(8,128)(2,1)}, bf16[8,128,128]{2,1,0:T(8,128)(2,1)}, bf16[8,128,128]{2,1,0:T(8,128)(2,1)}, bf16[8,128,128]{2,1,0:T(8,128)(2,1)}) custom-call(f32[8,8]{1,0:T(8,128)} %rates.19, f32[8,8]{1,0:T(8,128)} %coef.19, f32[2,8]{1,0:T(2,128)} %advect.19, f32[8]{0:T(128)} %diffuse.19, bf16[8,1,128,512]{3,2,1,0:T(8,128)(2,1)} %state.7, ...), custom_call_target="tpu_custom_call" | custom-call | flops 1610612736 | bytes 2097152 | tf_op jit(solution)/shard_map/pallas_call | solution.py:338
  21.3 3.5 %collective-permute-start.33 = (bf16[8,128,128]{2,1,0:T(8,128)(2,1)}, bf16[8,128,128]{2,1,0:T(8,128)(2,1)S(1)}, u32[]{:S(2)}, u32[]{:S(2)}) collective-permute-start(bf16[8,128,128]{2,1,0:T(8,128)(2,1)} %get-tuple-element.76), channel_id=1, source_target_pairs={{0,8},{4,12},{8,0},{12,4},{1,9},{5,13},{9,1},{13,5},{2,10},{6,14},... | collective-permute-start | bytes 786440 | tf_op jit(solution)/shard_map/ppermute | solution.py:407
  24.8 8.6 %shard_map.109 = (bf16[8,128,128]{2,1,0:T(8,128)(2,1)}, bf16[8,128,128]{2,1,0:T(8,128)(2,1)}, bf16[8,128,128]{2,1,0:T(8,128)(2,1)}, bf16[8,128,128]{2,1,0:T(8,128)(2,1)}) custom-call(f32[8,8]{1,0:T(8,128)} %rates.19, f32[8,8]{1,0:T(8,128)} %coef.19, f32[2,8]{1,0:T(2,128)} %advect.19, f32[8]{0:T(128)} %diffuse.19, bf16[8,1,128,512]{3,2,1,0:T(8,128)(2,1)} %state.7, ...), custom_call_target="tpu_custom_call" | custom-call | flops 1610612736 | bytes 2097152 | tf_op jit(solution)/shard_map/pallas_call | solution.py:338
  34.2 8.5 %shard_map.107 = (bf16[8,128,128]{2,1,0:T(8,128)(2,1)}, bf16[8,128,128]{2,1,0:T(8,128)(2,1)}, bf16[8,128,128]{2,1,0:T(8,128)(2,1)}, bf16[8,128,128]{2,1,0:T(8,128)(2,1)}) custom-call(f32[8,8]{1,0:T(8,128)} %rates.19, f32[8,8]{1,0:T(8,128)} %coef.19, f32[2,8]{1,0:T(2,128)} %advect.19, f32[8]{0:T(128)} %diffuse.19, bf16[8,1,128,512]{3,2,1,0:T(8,128)(2,1)} %state.7, ...), custom_call_target="tpu_custom_call" | custom-call | flops 1610612736 | bytes 2097152 | tf_op jit(solution)/shard_map/pallas_call | solution.py:338
  44.8 3.5 %collective-permute-start.27 = (bf16[8,128,128]{2,1,0:T(8,128)(2,1)}, bf16[8,128,128]{2,1,0:T(8,128)(2,1)S(1)}, u32[]{:S(2)}, u32[]{:S(2)}) collective-permute-start(bf16[8,128,128]{2,1,0:T(8,128)(2,1)} %get-tuple-element.68), channel_id=1, source_target_pairs={{0,8},{4,12},{8,0},{12,4},{1,9},{5,13},{9,1},{13,5},{2,10},{6,14},... | collective-permute-start | bytes 786440 | tf_op jit(solution)/shard_map/ppermute | solution.py:407
  49.8 3.8 %collective-permute-start.21 = (bf16[8,128,128]{2,1,0:T(8,128)(2,1)}, bf16[8,128,128]{2,1,0:T(8,128)(2,1)S(1)}, u32[]{:S(2)}, u32[]{:S(2)}) collective-permute-start(bf16[8,128,128]{2,1,0:T(8,128)(2,1)} %get-tuple-element.60), channel_id=1, source_target_pairs={{0,8},{4,12},{8,0},{12,4},{1,9},{5,13},{9,1},{13,5},{2,10},{6,14},... | collective-permute-start | bytes 786440 | tf_op jit(solution)/shard_map/ppermute | solution.py:407
  53.6 8.6 %shard_map.105 = (bf16[8,128,128]{2,1,0:T(8,128)(2,1)}, bf16[8,128,128]{2,1,0:T(8,128)(2,1)}, bf16[8,128,128]{2,1,0:T(8,128)(2,1)}, bf16[8,128,128]{2,1,0:T(8,128)(2,1)}) custom-call(f32[8,8]{1,0:T(8,128)} %rates.19, f32[8,8]{1,0:T(8,128)} %coef.19, f32[2,8]{1,0:T(2,128)} %advect.19, f32[8]{0:T(128)} %diffuse.19, bf16[8,1,128,512]{3,2,1,0:T(8,128)(2,1)} %state.7, ...), custom_call_target="tpu_custom_call" | custom-call | flops 1610612736 | bytes 2097152 | tf_op jit(solution)/shard_map/pallas_call | solution.py:338
  63.0 4.0 %collective-permute-done.27.rest_10_ = bf16[8,128,128]{2,1,0:T(8,128)(2,1)S(1)} collective-permute-done((bf16[8,128,128]{2,1,0:T(8,128)(2,1)}, bf16[8,128,128]{2,1,0:T(8,128)(2,1)S(1)}, u32[]{:S(2)}, u32[]{:S(2)}) %collective-permute-start.27) | collective-permute-done | bytes 262176 | tf_op jit(solution)/shard_map/ppermute | solution.py:407
  68.4 17.6 %collective-permute-start.15 = (bf16[8,128,128]{2,1,0:T(8,128)(2,1)}, bf16[8,128,128]{2,1,0:T(8,128)(2,1)S(1)}, u32[]{:S(2)}, u32[]{:S(2)}) collective-permute-start(bf16[8,128,128]{2,1,0:T(8,128)(2,1)} %get-tuple-element.52), channel_id=1, source_target_pairs={{0,8},{4,12},{8,0},{12,4},{1,9},{5,13},{9,1},{13,5},{2,10},{6,14},... | collective-permute-start | bytes 786440 | tf_op jit(solution)/shard_map/ppermute | solution.py:407
  95.6 6.9 %shard_map.104 = (bf16[4,128,128]{2,1,0:T(8,128)(2,1)S(1)}, bf16[4,128,128]{2,1,0:T(8,128)(2,1)S(1)}, bf16[4,128,128]{2,1,0:T(8,128)(2,1)S(1)}, bf16[4,128,128]{2,1,0:T(8,128)(2,1)S(1)}) custom-call(f32[8,8]{1,0:T(8,128)S(1)} %copy-done, f32[8,8]{1,0:T(8,128)S(1)} %copy-done.1, f32[2,8]{1,0:T(2,128)S(1)} %copy-done.2, f32[8]{0:T(128)S(1)} %copy-done.3, ...), custom_call_target="tpu_custom_call" | custom-call | flops 805306368 | bytes 1048576 | tf_op jit(solution)/shard_map/pallas_call | solution.py:362
  105.4 10.8 %shard_map.112 = (bf16[8,128,128]{2,1,0:T(8,128)(2,1)S(1)}, bf16[8,128,128]{2,1,0:T(8,128)(2,1)S(1)}, bf16[8,128,128]{2,1,0:T(8,128)(2,1)S(1)}, bf16[8,128,128]{2,1,0:T(8,128)(2,1)S(1)}) custom-call(f32[8,8]{1,0:T(8,128)S(1)} %copy-done, f32[8,8]{1,0:T(8,128)S(1)} %copy-done.1, f32[2,8]{1,0:T(2,128)S(1)} %copy-done.2, f32[8]{0:T(128)S(1)} %copy-done.3, ...), custom_call_target="tpu_custom_call" | custom-call | flops 1610612736 | bytes 2097152 | tf_op jit(solution)/shard_map/pallas_call | solution.py:362
  116.3 2.1 collective-permute-start.35
  121.3 2.4 %collective-permute-start.9 = (bf16[4,128,128]{2,1,0:T(8,128)(2,1)S(1)}, bf16[4,128,128]{2,1,0:T(8,128)(2,1)S(1)}, u32[]{:S(2)}, u32[]{:S(2)}) collective-permute-start(bf16[4,128,128]{2,1,0:T(8,128)(2,1)S(1)} %get-tuple-element.49), channel_id=1, source_target_pairs={{0,12},{4,8},{8,4},{12,0},{1,13},{5,9},{9,5},{13,1},{2,14},{6,10},... | collective-permute-start | bytes 393224 | tf_op jit(solution)/shard_map/ppermute | solution.py:407
  123.7 10.7 %shard_map.110 = (bf16[8,128,128]{2,1,0:T(8,128)(2,1)S(1)}, bf16[8,128,128]{2,1,0:T(8,128)(2,1)S(1)}, bf16[8,128,128]{2,1,0:T(8,128)(2,1)S(1)}, bf16[8,128,128]{2,1,0:T(8,128)(2,1)S(1)}) custom-call(f32[8,8]{1,0:T(8,128)S(1)} %copy-done, f32[8,8]{1,0:T(8,128)S(1)} %copy-done.1, f32[2,8]{1,0:T(2,128)S(1)} %copy-done.2, f32[8]{0:T(128)S(1)} %copy-done.3, ...), custom_call_target="tpu_custom_call" | custom-call | flops 1610612736 | bytes 2097152 | tf_op jit(solution)/shard_map/pallas_call | solution.py:362
  134.4 9.8 %collective-permute-done.8.rest_2_ = bf16[4,128,128]{2,1,0:T(8,128)(2,1)S(1)} collective-permute-done((bf16[4,128,128]{2,1,0:T(8,128)(2,1)S(1)}, bf16[4,128,128]{2,1,0:T(8,128)(2,1)S(1)}, u32[]{:S(2)}, u32[]{:S(2)}) %collective-permute-start.8) | collective-permute-done | bytes 131104 | tf_op jit(solution)/shard_map/ppermute | solution.py:407
  144.2 9.0 %collective-permute-start.29 = (bf16[8,128,128]{2,1,0:T(8,128)(2,1)S(1)}, bf16[8,128,128]{2,1,0:T(8,128)(2,1)S(1)}, u32[]{:S(2)}, u32[]{:S(2)}) collective-permute-start(bf16[8,128,128]{2,1,0:T(8,128)(2,1)S(1)} %get-tuple-element.71), channel_id=1, source_target_pairs={{0,4},{4,0},{8,12},{12,8},{1,5},{5,1},{9,13},{13,9},{2,6},{6,2},{1... | collective-permute-start | bytes 786440 | tf_op jit(solution)/shard_map/ppermute | solution.py:407
  153.2 10.9 %shard_map.108 = (bf16[8,128,128]{2,1,0:T(8,128)(2,1)S(1)}, bf16[8,128,128]{2,1,0:T(8,128)(2,1)S(1)}, bf16[8,128,128]{2,1,0:T(8,128)(2,1)S(1)}, bf16[8,128,128]{2,1,0:T(8,128)(2,1)S(1)}) custom-call(f32[8,8]{1,0:T(8,128)S(1)} %copy-done, f32[8,8]{1,0:T(8,128)S(1)} %copy-done.1, f32[2,8]{1,0:T(2,128)S(1)} %copy-done.2, f32[8]{0:T(128)S(1)} %copy-done.3, ...), custom_call_target="tpu_custom_call" | custom-call | flops 1610612736 | bytes 2097152 | tf_op jit(solution)/shard_map/pallas_call | solution.py:362
  164.1 2.4 %collective-permute-start.31 = (bf16[8,128,128]{2,1,0:T(8,128)(2,1)S(1)}, bf16[8,128,128]{2,1,0:T(8,128)(2,1)S(1)}, u32[]{:S(2)}, u32[]{:S(2)}) collective-permute-start(bf16[8,128,128]{2,1,0:T(8,128)(2,1)S(1)} %get-tuple-element.73), channel_id=1, source_target_pairs={{0,12},{4,8},{8,4},{12,0},{1,13},{5,9},{9,5},{13,1},{2,14},{6,10},... | collective-permute-start | bytes 786440 | tf_op jit(solution)/shard_map/ppermute | solution.py:407
  169.5 10.6 %shard_map.106 = (bf16[8,128,128]{2,1,0:T(8,128)(2,1)S(1)}, bf16[8,128,128]{2,1,0:T(8,128)(2,1)S(1)}, bf16[8,128,128]{2,1,0:T(8,128)(2,1)S(1)}, bf16[8,128,128]{2,1,0:T(8,128)(2,1)S(1)}) custom-call(f32[8,8]{1,0:T(8,128)S(1)} %copy-done, f32[8,8]{1,0:T(8,128)S(1)} %copy-done.1, f32[2,8]{1,0:T(2,128)S(1)} %copy-done.2, f32[8]{0:T(128)S(1)} %copy-done.3, ...), custom_call_target="tpu_custom_call" | custom-call | flops 1610612736 | bytes 2097152 | tf_op jit(solution)/shard_map/pallas_call | solution.py:362
  189.7 11.0 %collective-permute-done.24.rest_2_ = bf16[8,128,128]{2,1,0:T(8,128)(2,1)S(1)} collective-permute-done((bf16[8,128,128]{2,1,0:T(8,128)(2,1)S(1)}, bf16[8,128,128]{2,1,0:T(8,128)(2,1)S(1)}, u32[]{:S(2)}, u32[]{:S(2)}) %collective-permute-start.24) | collective-permute-done | bytes 262176 | tf_op jit(solution)/shard_map/ppermute | solution.py:407
  201.8 21.1 %collective-permute-done.18.rest_2_ = bf16[8,128,128]{2,1,0:T(8,128)(2,1)S(1)} collective-permute-done((bf16[8,128,128]{2,1,0:T(8,128)(2,1)S(1)}, bf16[8,128,128]{2,1,0:T(8,128)(2,1)S(1)}, u32[]{:S(2)}, u32[]{:S(2)}) %collective-permute-start.18) | collective-permute-done | bytes 262176 | tf_op jit(solution)/shard_map/ppermute | solution.py:407
  (150 shorter events, 37.4 us)
Async XLA Ops:
  11.6 21.8 %collective-permute-start.2 = (bf16[4,128,128]{2,1,0:T(8,128)(2,1)}, bf16[4,128,128]{2,1,0:T(8,128)(2,1)S(1)}, u32[]{:S(2)}, u32[]{:S(2)}) collective-permute-start(bf16[4,128,128]{2,1,0:T(8,128)(2,1)} %get-tuple-element.45), channel_id=1, source_target_pairs={{0,12},{4,8},{8,4},{12,0},{1,13},{5,9},{9,5},{13,1},{2,14},{6,10},... | collective-permute-start | bytes 393224 | tf_op jit(solution)/shard_map/ppermute | solution.py:407
  11.6 22.0 %collective-permute-start.3 = (bf16[4,128,128]{2,1,0:T(8,128)(2,1)}, bf16[4,128,128]{2,1,0:T(8,128)(2,1)S(1)}, u32[]{:S(2)}, u32[]{:S(2)}) collective-permute-start(bf16[4,128,128]{2,1,0:T(8,128)(2,1)} %get-tuple-element.42.rest_0_), channel_id=1, source_target_pairs={{0,1},{1,0},{2,3},{3,2},{4,5},{5,4},{6,7},{7,6},{8,9},{9,8},{10,11... | collective-permute-start | bytes 393224 | tf_op jit(solution)/shard_map/ppermute | solution.py:412
  20.4 28.0 %collective-permute-start.32 = (bf16[8,128,128]{2,1,0:T(8,128)(2,1)}, bf16[8,128,128]{2,1,0:T(8,128)(2,1)S(1)}, u32[]{:S(2)}, u32[]{:S(2)}) collective-permute-start(bf16[8,128,128]{2,1,0:T(8,128)(2,1)} %get-tuple-element.75), channel_id=1, source_target_pairs={{0,4},{4,0},{8,12},{12,8},{1,5},{5,1},{9,13},{13,9},{2,6},{6,2},{1... | collective-permute-start | bytes 786440 | tf_op jit(solution)/shard_map/ppermute | solution.py:407
  21.3 27.2 %collective-permute-start.33 = (bf16[8,128,128]{2,1,0:T(8,128)(2,1)}, bf16[8,128,128]{2,1,0:T(8,128)(2,1)S(1)}, u32[]{:S(2)}, u32[]{:S(2)}) collective-permute-start(bf16[8,128,128]{2,1,0:T(8,128)(2,1)} %get-tuple-element.76), channel_id=1, source_target_pairs={{0,8},{4,12},{8,0},{12,4},{1,9},{5,13},{9,1},{13,5},{2,10},{6,14},... | collective-permute-start | bytes 786440 | tf_op jit(solution)/shard_map/ppermute | solution.py:407
  44.8 22.2 %collective-permute-start.27 = (bf16[8,128,128]{2,1,0:T(8,128)(2,1)}, bf16[8,128,128]{2,1,0:T(8,128)(2,1)S(1)}, u32[]{:S(2)}, u32[]{:S(2)}) collective-permute-start(bf16[8,128,128]{2,1,0:T(8,128)(2,1)} %get-tuple-element.68), channel_id=1, source_target_pairs={{0,8},{4,12},{8,0},{12,4},{1,9},{5,13},{9,1},{13,5},{2,10},{6,14},... | collective-permute-start | bytes 786440 | tf_op jit(solution)/shard_map/ppermute | solution.py:407
  48.5 37.5 %collective-permute-start.20 = (bf16[8,128,128]{2,1,0:T(8,128)(2,1)}, bf16[8,128,128]{2,1,0:T(8,128)(2,1)S(1)}, u32[]{:S(2)}, u32[]{:S(2)}) collective-permute-start(bf16[8,128,128]{2,1,0:T(8,128)(2,1)} %get-tuple-element.59), channel_id=1, source_target_pairs={{0,4},{4,0},{8,12},{12,8},{1,5},{5,1},{9,13},{13,9},{2,6},{6,2},{1... | collective-permute-start | bytes 786440 | tf_op jit(solution)/shard_map/ppermute | solution.py:407
  49.8 52.7 %collective-permute-start.21 = (bf16[8,128,128]{2,1,0:T(8,128)(2,1)}, bf16[8,128,128]{2,1,0:T(8,128)(2,1)S(1)}, u32[]{:S(2)}, u32[]{:S(2)}) collective-permute-start(bf16[8,128,128]{2,1,0:T(8,128)(2,1)} %get-tuple-element.60), channel_id=1, source_target_pairs={{0,8},{4,12},{8,0},{12,4},{1,9},{5,13},{9,1},{13,5},{2,10},{6,14},... | collective-permute-start | bytes 786440 | tf_op jit(solution)/shard_map/ppermute | solution.py:407
  62.9 53.4 %collective-permute-start.22 = (bf16[8,128,128]{2,1,0:T(8,128)(2,1)}, bf16[8,128,128]{2,1,0:T(8,128)(2,1)}, u32[]{:S(2)}, u32[]{:S(2)}) collective-permute-start(bf16[8,128,128]{2,1,0:T(8,128)(2,1)} %get-tuple-element.61), channel_id=1, source_target_pairs={{0,12},{4,8},{8,4},{12,0},{1,13},{5,9},{9,5},{13,1},{2,14},{6,10},... | collective-permute-start | bytes 786440 | tf_op jit(solution)/shard_map/ppermute | solution.py:407
  67.7 50.7 %collective-permute-start.14 = (bf16[8,128,128]{2,1,0:T(8,128)(2,1)}, bf16[8,128,128]{2,1,0:T(8,128)(2,1)S(1)}, u32[]{:S(2)}, u32[]{:S(2)}) collective-permute-start(bf16[8,128,128]{2,1,0:T(8,128)(2,1)} %get-tuple-element.51), channel_id=1, source_target_pairs={{0,4},{4,0},{8,12},{12,8},{1,5},{5,1},{9,13},{13,9},{2,6},{6,2},{1... | collective-permute-start | bytes 786440 | tf_op jit(solution)/shard_map/ppermute | solution.py:407
  68.4 50.9 %collective-permute-start.15 = (bf16[8,128,128]{2,1,0:T(8,128)(2,1)}, bf16[8,128,128]{2,1,0:T(8,128)(2,1)S(1)}, u32[]{:S(2)}, u32[]{:S(2)}) collective-permute-start(bf16[8,128,128]{2,1,0:T(8,128)(2,1)} %get-tuple-element.52), channel_id=1, source_target_pairs={{0,8},{4,12},{8,0},{12,4},{1,9},{5,13},{9,1},{13,5},{2,10},{6,14},... | collective-permute-start | bytes 786440 | tf_op jit(solution)/shard_map/ppermute | solution.py:407
  86.1 35.3 %collective-permute-start.16 = (bf16[8,128,128]{2,1,0:T(8,128)(2,1)}, bf16[8,128,128]{2,1,0:T(8,128)(2,1)S(1)}, u32[]{:S(2)}, u32[]{:S(2)}) collective-permute-start(bf16[8,128,128]{2,1,0:T(8,128)(2,1)} %get-tuple-element.53), channel_id=1, source_target_pairs={{0,12},{4,8},{8,4},{12,0},{1,13},{5,9},{9,5},{13,1},{2,14},{6,10},... | collective-permute-start | bytes 786440 | tf_op jit(solution)/shard_map/ppermute | solution.py:407
  102.5 21.2 %collective-permute-start.7 = (bf16[4,128,128]{2,1,0:T(8,128)(2,1)S(1)}, bf16[4,128,128]{2,1,0:T(8,128)(2,1)S(1)}, u32[]{:S(2)}, u32[]{:S(2)}) collective-permute-start(bf16[4,128,128]{2,1,0:T(8,128)(2,1)S(1)} %get-tuple-element.47), channel_id=1, source_target_pairs={{0,4},{4,0},{8,12},{12,8},{1,5},{5,1},{9,13},{13,9},{2,6},{6,2},{1... | collective-permute-start | bytes 393224 | tf_op jit(solution)/shard_map/ppermute | solution.py:407
  116.3 47.8 %collective-permute-start.35 = (bf16[8,128,128]{2,1,0:T(8,128)(2,1)S(1)}, bf16[8,128,128]{2,1,0:T(8,128)(2,1)S(1)}, u32[]{:S(2)}, u32[]{:S(2)}) collective-permute-start(bf16[8,128,128]{2,1,0:T(8,128)(2,1)S(1)} %get-tuple-element.79), channel_id=1, source_target_pairs={{0,4},{4,0},{8,12},{12,8},{1,5},{5,1},{9,13},{13,9},{2,6},{6,2},{1... | collective-permute-start | bytes 786440 | tf_op jit(solution)/shard_map/ppermute | solution.py:407
  118.4 48.2 %collective-permute-start.36 = (bf16[8,128,128]{2,1,0:T(8,128)(2,1)S(1)}, bf16[8,128,128]{2,1,0:T(8,128)(2,1)S(1)}, u32[]{:S(2)}, u32[]{:S(2)}) collective-permute-start(bf16[8,128,128]{2,1,0:T(8,128)(2,1)S(1)} %get-tuple-element.80), channel_id=1, source_target_pairs={{0,8},{4,12},{8,0},{12,4},{1,9},{5,13},{9,1},{13,5},{2,10},{6,14},... | collective-permute-start | bytes 786440 | tf_op jit(solution)/shard_map/ppermute | solution.py:407
  119.4 24.8 %collective-permute-start.8 = (bf16[4,128,128]{2,1,0:T(8,128)(2,1)S(1)}, bf16[4,128,128]{2,1,0:T(8,128)(2,1)S(1)}, u32[]{:S(2)}, u32[]{:S(2)}) collective-permute-start(bf16[4,128,128]{2,1,0:T(8,128)(2,1)S(1)} %get-tuple-element.48), channel_id=1, source_target_pairs={{0,8},{4,12},{8,0},{12,4},{1,9},{5,13},{9,1},{13,5},{2,10},{6,14},... | collective-permute-start | bytes 393224 | tf_op jit(solution)/shard_map/ppermute | solution.py:407
  121.3 22.9 %collective-permute-start.9 = (bf16[4,128,128]{2,1,0:T(8,128)(2,1)S(1)}, bf16[4,128,128]{2,1,0:T(8,128)(2,1)S(1)}, u32[]{:S(2)}, u32[]{:S(2)}) collective-permute-start(bf16[4,128,128]{2,1,0:T(8,128)(2,1)S(1)} %get-tuple-element.49), channel_id=1, source_target_pairs={{0,12},{4,8},{8,4},{12,0},{1,13},{5,9},{9,5},{13,1},{2,14},{6,10},... | collective-permute-start | bytes 393224 | tf_op jit(solution)/shard_map/ppermute | solution.py:407
  123.7 29.5 %collective-permute-start.10 = (bf16[4,128,128]{2,1,0:T(8,128)(2,1)S(1)}, bf16[4,128,128]{2,1,0:T(8,128)(2,1)S(1)}, u32[]{:S(2)}, u32[]{:S(2)}) collective-permute-start(bf16[4,128,128]{2,1,0:T(8,128)(2,1)S(1)} %get-tuple-element.46.rest_0_), channel_id=1, source_target_pairs={{0,1},{1,0},{2,3},{3,2},{4,5},{5,4},{6,7},{7,6},{8,9},{9,8},{10,11... | collective-permute-start | bytes 393224 | tf_op jit(solution)/shard_map/ppermute | solution.py:412
  144.2 23.5 %collective-permute-start.37 = (bf16[8,128,128]{2,1,0:T(8,128)(2,1)S(1)}, bf16[8,128,128]{2,1,0:T(8,128)(2,1)S(1)}, u32[]{:S(2)}, u32[]{:S(2)}) collective-permute-start(bf16[8,128,128]{2,1,0:T(8,128)(2,1)S(1)} %get-tuple-element.81), channel_id=1, source_target_pairs={{0,12},{4,8},{8,4},{12,0},{1,13},{5,9},{9,5},{13,1},{2,14},{6,10},... | collective-permute-start | bytes 786440 | tf_op jit(solution)/shard_map/ppermute | solution.py:407
  144.2 23.5 %collective-permute-start.29 = (bf16[8,128,128]{2,1,0:T(8,128)(2,1)S(1)}, bf16[8,128,128]{2,1,0:T(8,128)(2,1)S(1)}, u32[]{:S(2)}, u32[]{:S(2)}) collective-permute-start(bf16[8,128,128]{2,1,0:T(8,128)(2,1)S(1)} %get-tuple-element.71), channel_id=1, source_target_pairs={{0,4},{4,0},{8,12},{12,8},{1,5},{5,1},{9,13},{13,9},{2,6},{6,2},{1... | collective-permute-start | bytes 786440 | tf_op jit(solution)/shard_map/ppermute | solution.py:407
  180.1 20.6 %collective-permute-start.24 = (bf16[8,128,128]{2,1,0:T(8,128)(2,1)S(1)}, bf16[8,128,128]{2,1,0:T(8,128)(2,1)S(1)}, u32[]{:S(2)}, u32[]{:S(2)}) collective-permute-start(bf16[8,128,128]{2,1,0:T(8,128)(2,1)S(1)} %get-tuple-element.64), channel_id=1, source_target_pairs={{0,8},{4,12},{8,0},{12,4},{1,9},{5,13},{9,1},{13,5},{2,10},{6,14},... | collective-permute-start | bytes 786440 | tf_op jit(solution)/shard_map/ppermute | solution.py:407
  180.2 20.5 %collective-permute-start.25 = (bf16[8,128,128]{2,1,0:T(8,128)(2,1)S(1)}, bf16[8,128,128]{2,1,0:T(8,128)(2,1)S(1)}, u32[]{:S(2)}, u32[]{:S(2)}) collective-permute-start(bf16[8,128,128]{2,1,0:T(8,128)(2,1)S(1)} %get-tuple-element.65), channel_id=1, source_target_pairs={{0,12},{4,8},{8,4},{12,0},{1,13},{5,9},{9,5},{13,1},{2,14},{6,10},... | collective-permute-start | bytes 786440 | tf_op jit(solution)/shard_map/ppermute | solution.py:407
  182.2 19.6 %collective-permute-start.17 = (bf16[8,128,128]{2,1,0:T(8,128)(2,1)S(1)}, bf16[8,128,128]{2,1,0:T(8,128)(2,1)S(1)}, u32[]{:S(2)}, u32[]{:S(2)}) collective-permute-start(bf16[8,128,128]{2,1,0:T(8,128)(2,1)S(1)} %get-tuple-element.55), channel_id=1, source_target_pairs={{0,4},{4,0},{8,12},{12,8},{1,5},{5,1},{9,13},{13,9},{2,6},{6,2},{1... | collective-permute-start | bytes 786440 | tf_op jit(solution)/shard_map/ppermute | solution.py:407
  183.7 39.2 %collective-permute-start.18 = (bf16[8,128,128]{2,1,0:T(8,128)(2,1)S(1)}, bf16[8,128,128]{2,1,0:T(8,128)(2,1)S(1)}, u32[]{:S(2)}, u32[]{:S(2)}) collective-permute-start(bf16[8,128,128]{2,1,0:T(8,128)(2,1)S(1)} %get-tuple-element.56), channel_id=1, source_target_pairs={{0,8},{4,12},{8,0},{12,4},{1,9},{5,13},{9,1},{13,5},{2,10},{6,14},... | collective-permute-start | bytes 786440 | tf_op jit(solution)/shard_map/ppermute | solution.py:407
  184.7 38.2 %collective-permute-start.19 = (bf16[8,128,128]{2,1,0:T(8,128)(2,1)S(1)}, bf16[8,128,128]{2,1,0:T(8,128)(2,1)S(1)}, u32[]{:S(2)}, u32[]{:S(2)}) collective-permute-start(bf16[8,128,128]{2,1,0:T(8,128)(2,1)S(1)} %get-tuple-element.57), channel_id=1, source_target_pairs={{0,12},{4,8},{8,4},{12,0},{1,13},{5,9},{9,5},{13,1},{2,14},{6,10},... | collective-permute-start | bytes 786440 | tf_op jit(solution)/shard_map/ppermute | solution.py:407
  (54 other events, 948.1 us)

commit v2 on v1

--- a/solution.py
+++ b/solution.py
@@ -101,6 +101,14 @@
     return mixed(mixer, rounded) + jnp.dot(mixer[0][...], left, preferred_element_type=f32)
 
 
+def weighted(coef, s, channels):
+    total = None
+    for p in range(coef.shape[0]):
+        term = coef[p, s] * channels[p * DEPTH : (p + 1) * DEPTH]
+        total = term if total is None else total + term
+    return total
+
+
 def tangent_scaled(activity, mixing, own):
     scaled = (1.0 - activity * activity) * mixing
     group = lax.broadcasted_iota(jnp.int32, activity.shape, 0) // DEPTH
@@ -111,15 +119,11 @@
     return (v.astype(f32) + time_step * (diffusivity * curve - speed * slope + rate)).astype(bf16)
 
 
-def x_state_kernel(n, rates, coef, advect, diffuse, state_far, d1_far, d2_far, filt_far, *rest):
-    outs, rest = rest[:n], rest[n:]
-    state, d1, d2, filt, filt_own, rates_high, rates_low, rate, middle, sems = rest
-    copies = [
-        pltpu.make_async_copy(far, near, sems.at[i])
-        for i, (far, near) in enumerate(
-            [(state_far, state), (d1_far, d1), (d2_far, d2), (filt_far, filt)]
-        )
-    ]
+def x_state_kernel(n, *refs):
+    far, outs, near, rest = refs[:8], refs[8 : 8 + n], refs[8 + n : 16 + n], refs[16 + n :]
+    rates, coef, advect, diffuse, state, d1, d2, filt = near
+    filt_own, rates_high, rates_low, rate, middle, ready, sems, out_sems = rest
+    copies = [pltpu.make_async_copy(far[i], near[i], sems.at[i]) for i in range(8)]
     for copy in copies:
         copy.start()
     me, half = lax.axis_index("pencil"), lax.axis_index("field")
@@ -127,8 +131,10 @@
     fields = outs[0].shape[0]
     size = length // n
     first = half * fields
+    for copy in copies[:4]:
+        copy.wait()
     fill_mixer(lambda a, b: rates[a, b], rates_high, rates_low)
-    copies[0].wait()
+    copies[4].wait()
     for j in range(rows // DEPTH):
         down = slice(j * DEPTH, (j + 1) * DEPTH)
         for c in range(length // WIDE):
@@ -136,14 +142,11 @@
             u = state[:, 0, down, across].reshape(count * DEPTH, WIDE)
             activity = jnp.tanh(mixed((rates_high, rates_low), u))
             for s in range(fields):
-                total = None
-                for p in range(rates.shape[0]):
-                    term = coef[p, first + s] * activity[p * DEPTH : (p + 1) * DEPTH]
-                    total = term if total is None else total + term
-                rate[s * rows + j * DEPTH : s * rows + (j + 1) * DEPTH, across] = total
+                at = slice(s * rows + j * DEPTH, s * rows + (j + 1) * DEPTH)
+                rate[at, across] = weighted(coef, first + s, activity)
     own = state[pl.ds(first, fields), 0].reshape(fields * rows, length)
-    copies[1].wait()
-    copies[2].wait()
+    copies[5].wait()
+    copies[6].wait()
     for c in range(length // WIDE):
         across = slice(c * WIDE, (c + 1) * WIDE)
         slope = jnp.dot(own, d1[:, across], preferred_element_type=f32)
@@ -153,17 +156,25 @@
             middle[at, across] = advance(
                 own[at, across], curve[at], slope[at], rate[at, across], diffuse[first + s], advect[0, first + s]
             )
-    copies[3].wait()
+    copies[7].wait()
     for r in range(n):
         filt_own[:, r * size : (r + 1) * size] = filt[:, aligned(me ^ r, size)]
-    result = jnp.dot(middle[...], filt_own[...], preferred_element_type=f32).astype(bf16)
-    for r in range(n):
-        outs[r][...] = result[:, r * size : (r + 1) * size].reshape(fields, rows, size)
+    sends = []
+    for c in reversed(range(length // WIDE)):
+        across = slice(c * WIDE, (c + 1) * WIDE)
+        result = jnp.dot(middle[...], filt_own[:, across], preferred_element_type=f32).astype(bf16)
+        for k in range(WIDE // size):
+            r = c * (WIDE // size) + k
+            ready[r] = result[:, k * size : (k + 1) * size].reshape(fields, rows, size)
+            sends.append(pltpu.make_async_copy(ready.at[r], outs[r], out_sems.at[r]))
+            sends[-1].start()
+    for send in sends:
+        send.wait()
 
 
 def x_kernel(n, q, params_here, rates, coef, advect, diffuse, state, tangent, d1, d2, filt, *rest):
     outs, rest = rest[:n], rest[n:]
-    filt_own, rates_high, rates_low, coef_high, coef_low, middle = rest
+    filt_own, rates_high, rates_low, middle = rest
     me, half = lax.axis_index("pencil"), lax.axis_index("field")
     count, rows, length = state.shape
     size = length // n
@@ -171,7 +182,6 @@
     @pl.when(pl.program_id(0) == 0)
     def _():
         fill_mixer(lambda a, b: rates[a, b], rates_high, rates_low)
-        fill_mixer(lambda a, b: coef[b, a], coef_high, coef_low)
         for r in range(n):
             filt_own[:, r * size : (r + 1) * size] = filt[:, aligned(me ^ r, size)]
 
@@ -182,13 +192,13 @@
         activity = jnp.tanh(mixed((rates_high, rates_low), u))
         mixing = mixed((rates_high, rates_low), own[:, across])
         scaled = tangent_scaled(activity, mixing, half * params_here + q)
-        rate = mixed_float((coef_high, coef_low), scaled)
         slope = jnp.dot(own, d1[:, across], preferred_element_type=f32)
         curve = jnp.dot(own, d2[:, across], preferred_element_type=f32)
         for s in range(count):
             at = slice(s * rows, (s + 1) * rows)
+            rate = weighted(coef, s, scaled)
             middle[at, across] = advance(
-                own[at, across], curve[at], slope[at], rate[at], diffuse[s], advect[0, s]
+                own[at, across], curve[at], slope[at], rate, diffuse[s], advect[0, s]
             )
     result = jnp.dot(middle[...], filt_own[...], preferred_element_type=f32).astype(bf16)
     for r in range(n):
@@ -317,14 +327,17 @@
     return pl.pallas_call(
         functools.partial(x_state_kernel, n),
         out_shape=[jax.ShapeDtypeStruct((here, deep, length // n), bf16)] * n,
-        in_specs=[SMEM] * 4 + [HBM] * 4,
-        out_specs=[VMEM] * n,
-        scratch_shapes=[pltpu.VMEM(state.shape, bf16), square, square, square, square]
+        in_specs=[HBM] * 8,
+        out_specs=[HBM] * n,
+        scratch_shapes=[pltpu.SMEM(scalar.shape, f32) for scalar in scalars]
+        + [pltpu.VMEM(state.shape, bf16), square, square, square, square]
         + mixers(count, count)
         + [
             pltpu.VMEM((here * deep, length), f32),
             pltpu.VMEM((here * deep, length), bf16),
-            pltpu.SemaphoreType.DMA((4,)),
+            pltpu.VMEM((n, here, deep, length // n), bf16),
+            pltpu.SemaphoreType.DMA((8,)),
+            pltpu.SemaphoreType.DMA((n,)),
         ],
         cost_estimate=cost(6 * here * deep * length * length, 4 * here * deep * length),
         name="x_state",
@@ -347,7 +360,7 @@
         + [whole] * 3,
         out_specs=[pl.BlockSpec((count, DEPTH, size), lambda i: (0, i, 0))] * n,
         scratch_shapes=[pltpu.VMEM((length, length), bf16)]
-        + mixers(count, count) * 2
+        + mixers(count, count)
         + [pltpu.VMEM((count * DEPTH, length), bf16)],
         cost_estimate=cost(6 * count * deep * length * length, 4 * count * deep * length),
     )(*scalars, state, tangents, d1, d2, filt)

time: 228 us -> 226 us (level)
  Pallas kernels: 94.6 us -> 85.8 us
  starting transfers between devices: 65.8 us -> 69.4 us
  waiting for transfers between devices: 47.3 us -> 49.9 us
    pallas_call x4, Pallas kernels: 34.4 us -> 26.4 us  [x_call(): pl.pallas_call(functools.partial(x_kernel, n, q, params_here), grid=(deep...]
    ppermute x30, starting transfers between devices: 64.7 us -> 68.4 us  [exchange(): lax.ppermute(slots[r], 'pencil', [(i, i ^ r) for i in range(n)])]
    ppermute x30, waiting for transfers between devices: 47.3 us -> 49.9 us  [exchange(): lax.ppermute(slots[r], 'pencil', [(i, i ^ r) for i in range(n)])]
  transfers between devices with their start and end apart: 38 -> 38, of which waited for: 6 -> 6; matrix products, arithmetic and copies ran while one was open for 1% -> 1% of each run, Pallas kernels for 39% -> 36%
where the time goes in v2:
time: 226 us; the launch traced here: 221 us
  Pallas kernels  85.8 us (38%)
  starting transfers between devices  69.4 us (31%)
  waiting for transfers between devices  49.9 us (22%)
  local copies, waits for them, and re-layouts  15 us (7%)
    ppermute x30, starting transfers between devices, exchange(): lax.ppermute(slots[r], 'pencil', [(i, i ^ r) for i in range(n)])  68.4 us
    pallas_call x5, Pallas kernels, y_call(): pl.pallas_call(functools.partial(y_kernel, n, q, params_here), out_shape=...  49.9 us
    ppermute x30, waiting for transfers between devices, exchange(): lax.ppermute(slots[r], 'pencil', [(i, i ^ r) for i in range(n)])  49.9 us
    pallas_call x4, Pallas kernels, x_call(): pl.pallas_call(functools.partial(x_kernel, n, q, params_here), grid=(deep...  26.4 us
    unnamed x83, local copies, waits for them, and re-layouts  15 us
  transfers between devices with their start and end apart: 38, of which 6 were waited for; matrix products, arithmetic and copies ran while one was open for 1% of the time, Pallas kernels for 36%

profile of v2, /device:TPU:0, one launch (start us, length us, event | category | flops | bytes accessed | tf_op | source)
XLA Modules:
  0.0 221.4 jit_solution(17960329950273099763)
XLA Ops:
  0.6 4.5 %x_state.1 = (bf16[4,128,128]{2,1,0:T(8,128)(2,1)}, bf16[4,128,128]{2,1,0:T(8,128)(2,1)}, bf16[4,128,128]{2,1,0:T(8,128)(2,1)}, bf16[4,128,128]{2,1,0:T(8,128)(2,1)}) custom-call(f32[8,8]{1,0:T(8,128)} %rates.17, f32[8,8]{1,0:T(8,128)} %coef.17, f32[2,8]{1,0:T(2,128)} %advect.17, f32[8]{0:T(128)} %diffuse.17, bf16[8,1,128,512]{3,2,1,0:T(8,128)(2,1)} %state.7, ...), custom_call_target="tpu_custom_call" | custom-call | flops 805306368 | bytes 1048576 | tf_op jit(solution)/shard_map/x_state/pallas_call | solution.py:327
  5.1 3.1 %collective-permute-start = (bf16[4,128,128]{2,1,0:T(8,128)(2,1)}, bf16[4,128,128]{2,1,0:T(8,128)(2,1)S(1)}, u32[]{:S(2)}, u32[]{:S(2)}) collective-permute-start(bf16[4,128,128]{2,1,0:T(8,128)(2,1)} %get-tuple-element.43), channel_id=1, source_target_pairs={{0,4},{4,0},{8,12},{12,8},{1,5},{5,1},{9,13},{13,9},{2,6},{6,2},{1... | collective-permute-start | bytes 393224 | tf_op jit(solution)/shard_map/ppermute | solution.py:420
  8.3 2.6 %collective-permute-start.1 = (bf16[4,128,128]{2,1,0:T(8,128)(2,1)}, bf16[4,128,128]{2,1,0:T(8,128)(2,1)S(1)}, u32[]{:S(2)}, u32[]{:S(2)}) collective-permute-start(bf16[4,128,128]{2,1,0:T(8,128)(2,1)} %get-tuple-element.44), channel_id=1, source_target_pairs={{0,8},{4,12},{8,0},{12,4},{1,9},{5,13},{9,1},{13,5},{2,10},{6,14},... | collective-permute-start | bytes 393224 | tf_op jit(solution)/shard_map/ppermute | solution.py:420
  10.9 6.7 %shard_map.111 = (bf16[8,128,128]{2,1,0:T(8,128)(2,1)}, bf16[8,128,128]{2,1,0:T(8,128)(2,1)}, bf16[8,128,128]{2,1,0:T(8,128)(2,1)}, bf16[8,128,128]{2,1,0:T(8,128)(2,1)}) custom-call(f32[8,8]{1,0:T(8,128)} %rates.17, f32[8,8]{1,0:T(8,128)} %coef.17, f32[2,8]{1,0:T(2,128)} %advect.17, f32[8]{0:T(128)} %diffuse.17, bf16[8,1,128,512]{3,2,1,0:T(8,128)(2,1)} %state.7, ...), custom_call_target="tpu_custom_call" | custom-call | flops 1610612736 | bytes 2097152 | tf_op jit(solution)/shard_map/pallas_call | solution.py:351
  18.5 3.5 %collective-permute-start.33 = (bf16[8,128,128]{2,1,0:T(8,128)(2,1)}, bf16[8,128,128]{2,1,0:T(8,128)(2,1)S(1)}, u32[]{:S(2)}, u32[]{:S(2)}) collective-permute-start(bf16[8,128,128]{2,1,0:T(8,128)(2,1)} %get-tuple-element.76), channel_id=1, source_target_pairs={{0,8},{4,12},{8,0},{12,4},{1,9},{5,13},{9,1},{13,5},{2,10},{6,14},... | collective-permute-start | bytes 786440 | tf_op jit(solution)/shard_map/ppermute | solution.py:420
  22.1 6.6 %shard_map.109 = (bf16[8,128,128]{2,1,0:T(8,128)(2,1)}, bf16[8,128,128]{2,1,0:T(8,128)(2,1)}, bf16[8,128,128]{2,1,0:T(8,128)(2,1)}, bf16[8,128,128]{2,1,0:T(8,128)(2,1)}) custom-call(f32[8,8]{1,0:T(8,128)} %rates.17, f32[8,8]{1,0:T(8,128)} %coef.17, f32[2,8]{1,0:T(2,128)} %advect.17, f32[8]{0:T(128)} %diffuse.17, bf16[8,1,128,512]{3,2,1,0:T(8,128)(2,1)} %state.7, ...), custom_call_target="tpu_custom_call" | custom-call | flops 1610612736 | bytes 2097152 | tf_op jit(solution)/shard_map/pallas_call | solution.py:351
  30.8 6.5 %shard_map.107 = (bf16[8,128,128]{2,1,0:T(8,128)(2,1)}, bf16[8,128,128]{2,1,0:T(8,128)(2,1)}, bf16[8,128,128]{2,1,0:T(8,128)(2,1)}, bf16[8,128,128]{2,1,0:T(8,128)(2,1)}) custom-call(f32[8,8]{1,0:T(8,128)} %rates.17, f32[8,8]{1,0:T(8,128)} %coef.17, f32[2,8]{1,0:T(2,128)} %advect.17, f32[8]{0:T(128)} %diffuse.17, bf16[8,1,128,512]{3,2,1,0:T(8,128)(2,1)} %state.7, ...), custom_call_target="tpu_custom_call" | custom-call | flops 1610612736 | bytes 2097152 | tf_op jit(solution)/shard_map/pallas_call | solution.py:351
  38.7 2.8 %collective-permute-start.27 = (bf16[8,128,128]{2,1,0:T(8,128)(2,1)}, bf16[8,128,128]{2,1,0:T(8,128)(2,1)S(1)}, u32[]{:S(2)}, u32[]{:S(2)}) collective-permute-start(bf16[8,128,128]{2,1,0:T(8,128)(2,1)} %get-tuple-element.68), channel_id=1, source_target_pairs={{0,8},{4,12},{8,0},{12,4},{1,9},{5,13},{9,1},{13,5},{2,10},{6,14},... | collective-permute-start | bytes 786440 | tf_op jit(solution)/shard_map/ppermute | solution.py:420
  44.0 5.1 %collective-permute-start.21 = (bf16[8,128,128]{2,1,0:T(8,128)(2,1)}, bf16[8,128,128]{2,1,0:T(8,128)(2,1)S(1)}, u32[]{:S(2)}, u32[]{:S(2)}) collective-permute-start(bf16[8,128,128]{2,1,0:T(8,128)(2,1)} %get-tuple-element.60), channel_id=1, source_target_pairs={{0,8},{4,12},{8,0},{12,4},{1,9},{5,13},{9,1},{13,5},{2,10},{6,14},... | collective-permute-start | bytes 786440 | tf_op jit(solution)/shard_map/ppermute | solution.py:420
  49.1 6.6 %shard_map.105 = (bf16[8,128,128]{2,1,0:T(8,128)(2,1)}, bf16[8,128,128]{2,1,0:T(8,128)(2,1)}, bf16[8,128,128]{2,1,0:T(8,128)(2,1)}, bf16[8,128,128]{2,1,0:T(8,128)(2,1)}) custom-call(f32[8,8]{1,0:T(8,128)} %rates.17, f32[8,8]{1,0:T(8,128)} %coef.17, f32[2,8]{1,0:T(2,128)} %advect.17, f32[8]{0:T(128)} %diffuse.17, bf16[8,1,128,512]{3,2,1,0:T(8,128)(2,1)} %state.7, ...), custom_call_target="tpu_custom_call" | custom-call | flops 1610612736 | bytes 2097152 | tf_op jit(solution)/shard_map/pallas_call | solution.py:351
  57.1 5.9 %collective-permute-done.27.rest_10_ = bf16[8,128,128]{2,1,0:T(8,128)(2,1)S(1)} collective-permute-done((bf16[8,128,128]{2,1,0:T(8,128)(2,1)}, bf16[8,128,128]{2,1,0:T(8,128)(2,1)S(1)}, u32[]{:S(2)}, u32[]{:S(2)}) %collective-permute-start.27) | collective-permute-done | bytes 262176 | tf_op jit(solution)/shard_map/ppermute | solution.py:420
  64.4 17.9 %collective-permute-start.15 = (bf16[8,128,128]{2,1,0:T(8,128)(2,1)}, bf16[8,128,128]{2,1,0:T(8,128)(2,1)S(1)}, u32[]{:S(2)}, u32[]{:S(2)}) collective-permute-start(bf16[8,128,128]{2,1,0:T(8,128)(2,1)} %get-tuple-element.52), channel_id=1, source_target_pairs={{0,8},{4,12},{8,0},{12,4},{1,9},{5,13},{9,1},{13,5},{2,10},{6,14},... | collective-permute-start | bytes 786440 | tf_op jit(solution)/shard_map/ppermute | solution.py:420
  91.6 6.9 %shard_map.104 = (bf16[4,128,128]{2,1,0:T(8,128)(2,1)S(1)}, bf16[4,128,128]{2,1,0:T(8,128)(2,1)S(1)}, bf16[4,128,128]{2,1,0:T(8,128)(2,1)S(1)}, bf16[4,128,128]{2,1,0:T(8,128)(2,1)S(1)}) custom-call(f32[8,8]{1,0:T(8,128)S(1)} %copy-done, f32[8,8]{1,0:T(8,128)S(1)} %copy-done.1, f32[2,8]{1,0:T(2,128)S(1)} %copy-done.2, f32[8]{0:T(128)S(1)} %copy-done.3, ...), custom_call_target="tpu_custom_call" | custom-call | flops 805306368 | bytes 1048576 | tf_op jit(solution)/shard_map/pallas_call | solution.py:375
  101.4 10.6 %shard_map.112 = (bf16[8,128,128]{2,1,0:T(8,128)(2,1)S(1)}, bf16[8,128,128]{2,1,0:T(8,128)(2,1)S(1)}, bf16[8,128,128]{2,1,0:T(8,128)(2,1)S(1)}, bf16[8,128,128]{2,1,0:T(8,128)(2,1)S(1)}) custom-call(f32[8,8]{1,0:T(8,128)S(1)} %copy-done, f32[8,8]{1,0:T(8,128)S(1)} %copy-done.1, f32[2,8]{1,0:T(2,128)S(1)} %copy-done.2, f32[8]{0:T(128)S(1)} %copy-done.3, ...), custom_call_target="tpu_custom_call" | custom-call | flops 1610612736 | bytes 2097152 | tf_op jit(solution)/shard_map/pallas_call | solution.py:375
  112.1 2.1 collective-permute-start.35
  117.1 2.7 %collective-permute-start.9 = (bf16[4,128,128]{2,1,0:T(8,128)(2,1)S(1)}, bf16[4,128,128]{2,1,0:T(8,128)(2,1)S(1)}, u32[]{:S(2)}, u32[]{:S(2)}) collective-permute-start(bf16[4,128,128]{2,1,0:T(8,128)(2,1)S(1)} %get-tuple-element.49), channel_id=1, source_target_pairs={{0,12},{4,8},{8,4},{12,0},{1,13},{5,9},{9,5},{13,1},{2,14},{6,10},... | collective-permute-start | bytes 393224 | tf_op jit(solution)/shard_map/ppermute | solution.py:420
  119.8 10.9 %shard_map.110 = (bf16[8,128,128]{2,1,0:T(8,128)(2,1)S(1)}, bf16[8,128,128]{2,1,0:T(8,128)(2,1)S(1)}, bf16[8,128,128]{2,1,0:T(8,128)(2,1)S(1)}, bf16[8,128,128]{2,1,0:T(8,128)(2,1)S(1)}) custom-call(f32[8,8]{1,0:T(8,128)S(1)} %copy-done, f32[8,8]{1,0:T(8,128)S(1)} %copy-done.1, f32[2,8]{1,0:T(2,128)S(1)} %copy-done.2, f32[8]{0:T(128)S(1)} %copy-done.3, ...), custom_call_target="tpu_custom_call" | custom-call | flops 1610612736 | bytes 2097152 | tf_op jit(solution)/shard_map/pallas_call | solution.py:375
  130.7 10.4 %collective-permute-done.8.rest_2_ = bf16[4,128,128]{2,1,0:T(8,128)(2,1)S(1)} collective-permute-done((bf16[4,128,128]{2,1,0:T(8,128)(2,1)S(1)}, bf16[4,128,128]{2,1,0:T(8,128)(2,1)S(1)}, u32[]{:S(2)}, u32[]{:S(2)}) %collective-permute-start.8) | collective-permute-done | bytes 131104 | tf_op jit(solution)/shard_map/ppermute | solution.py:420
  141.1 2.4 %collective-permute-start.37 = (bf16[8,128,128]{2,1,0:T(8,128)(2,1)S(1)}, bf16[8,128,128]{2,1,0:T(8,128)(2,1)S(1)}, u32[]{:S(2)}, u32[]{:S(2)}) collective-permute-start(bf16[8,128,128]{2,1,0:T(8,128)(2,1)S(1)} %get-tuple-element.81), channel_id=1, source_target_pairs={{0,12},{4,8},{8,4},{12,0},{1,13},{5,9},{9,5},{13,1},{2,14},{6,10},... | collective-permute-start | bytes 786440 | tf_op jit(solution)/shard_map/ppermute | solution.py:420
  143.5 6.6 %collective-permute-start.29 = (bf16[8,128,128]{2,1,0:T(8,128)(2,1)S(1)}, bf16[8,128,128]{2,1,0:T(8,128)(2,1)S(1)}, u32[]{:S(2)}, u32[]{:S(2)}) collective-permute-start(bf16[8,128,128]{2,1,0:T(8,128)(2,1)S(1)} %get-tuple-element.71), channel_id=1, source_target_pairs={{0,4},{4,0},{8,12},{12,8},{1,5},{5,1},{9,13},{13,9},{2,6},{6,2},{1... | collective-permute-start | bytes 786440 | tf_op jit(solution)/shard_map/ppermute | solution.py:420
  151.0 10.9 %shard_map.108 = (bf16[8,128,128]{2,1,0:T(8,128)(2,1)S(1)}, bf16[8,128,128]{2,1,0:T(8,128)(2,1)S(1)}, bf16[8,128,128]{2,1,0:T(8,128)(2,1)S(1)}, bf16[8,128,128]{2,1,0:T(8,128)(2,1)S(1)}) custom-call(f32[8,8]{1,0:T(8,128)S(1)} %copy-done, f32[8,8]{1,0:T(8,128)S(1)} %copy-done.1, f32[2,8]{1,0:T(2,128)S(1)} %copy-done.2, f32[8]{0:T(128)S(1)} %copy-done.3, ...), custom_call_target="tpu_custom_call" | custom-call | flops 1610612736 | bytes 2097152 | tf_op jit(solution)/shard_map/pallas_call | solution.py:375
  166.3 10.6 %shard_map.106 = (bf16[8,128,128]{2,1,0:T(8,128)(2,1)S(1)}, bf16[8,128,128]{2,1,0:T(8,128)(2,1)S(1)}, bf16[8,128,128]{2,1,0:T(8,128)(2,1)S(1)}, bf16[8,128,128]{2,1,0:T(8,128)(2,1)S(1)}) custom-call(f32[8,8]{1,0:T(8,128)S(1)} %copy-done, f32[8,8]{1,0:T(8,128)S(1)} %copy-done.1, f32[2,8]{1,0:T(2,128)S(1)} %copy-done.2, f32[8]{0:T(128)S(1)} %copy-done.3, ...), custom_call_target="tpu_custom_call" | custom-call | flops 1610612736 | bytes 2097152 | tf_op jit(solution)/shard_map/pallas_call | solution.py:375
  187.0 10.9 %collective-permute-done.24.rest_2_ = bf16[8,128,128]{2,1,0:T(8,128)(2,1)S(1)} collective-permute-done((bf16[8,128,128]{2,1,0:T(8,128)(2,1)S(1)}, bf16[8,128,128]{2,1,0:T(8,128)(2,1)S(1)}, u32[]{:S(2)}, u32[]{:S(2)}) %collective-permute-start.24) | collective-permute-done | bytes 262176 | tf_op jit(solution)/shard_map/ppermute | solution.py:420
  199.1 21.1 %collective-permute-done.18.rest_2_ = bf16[8,128,128]{2,1,0:T(8,128)(2,1)S(1)} collective-permute-done((bf16[8,128,128]{2,1,0:T(8,128)(2,1)S(1)}, bf16[8,128,128]{2,1,0:T(8,128)(2,1)S(1)}, u32[]{:S(2)}, u32[]{:S(2)}) %collective-permute-start.18) | collective-permute-done | bytes 262176 | tf_op jit(solution)/shard_map/ppermute | solution.py:420
  (150 shorter events, 42.2 us)
Async XLA Ops:
  10.9 19.4 %collective-permute-start.3 = (bf16[4,128,128]{2,1,0:T(8,128)(2,1)}, bf16[4,128,128]{2,1,0:T(8,128)(2,1)S(1)}, u32[]{:S(2)}, u32[]{:S(2)}) collective-permute-start(bf16[4,128,128]{2,1,0:T(8,128)(2,1)} %get-tuple-element.42.rest_0_), channel_id=1, source_target_pairs={{0,1},{1,0},{2,3},{3,2},{4,5},{5,4},{6,7},{7,6},{8,9},{9,8},{10,11... | collective-permute-start | bytes 393224 | tf_op jit(solution)/shard_map/ppermute | solution.py:425
  17.6 24.0 %collective-permute-start.32 = (bf16[8,128,128]{2,1,0:T(8,128)(2,1)}, bf16[8,128,128]{2,1,0:T(8,128)(2,1)S(1)}, u32[]{:S(2)}, u32[]{:S(2)}) collective-permute-start(bf16[8,128,128]{2,1,0:T(8,128)(2,1)} %get-tuple-element.75), channel_id=1, source_target_pairs={{0,4},{4,0},{8,12},{12,8},{1,5},{5,1},{9,13},{13,9},{2,6},{6,2},{1... | collective-permute-start | bytes 786440 | tf_op jit(solution)/shard_map/ppermute | solution.py:420
  18.5 24.6 %collective-permute-start.33 = (bf16[8,128,128]{2,1,0:T(8,128)(2,1)}, bf16[8,128,128]{2,1,0:T(8,128)(2,1)S(1)}, u32[]{:S(2)}, u32[]{:S(2)}) collective-permute-start(bf16[8,128,128]{2,1,0:T(8,128)(2,1)} %get-tuple-element.76), channel_id=1, source_target_pairs={{0,8},{4,12},{8,0},{12,4},{1,9},{5,13},{9,1},{13,5},{2,10},{6,14},... | collective-permute-start | bytes 786440 | tf_op jit(solution)/shard_map/ppermute | solution.py:420
  38.7 24.2 %collective-permute-start.27 = (bf16[8,128,128]{2,1,0:T(8,128)(2,1)}, bf16[8,128,128]{2,1,0:T(8,128)(2,1)S(1)}, u32[]{:S(2)}, u32[]{:S(2)}) collective-permute-start(bf16[8,128,128]{2,1,0:T(8,128)(2,1)} %get-tuple-element.68), channel_id=1, source_target_pairs={{0,8},{4,12},{8,0},{12,4},{1,9},{5,13},{9,1},{13,5},{2,10},{6,14},... | collective-permute-start | bytes 786440 | tf_op jit(solution)/shard_map/ppermute | solution.py:420
  41.5 22.1 %collective-permute-start.28 = (bf16[8,128,128]{2,1,0:T(8,128)(2,1)}, bf16[8,128,128]{2,1,0:T(8,128)(2,1)S(1)}, u32[]{:S(2)}, u32[]{:S(2)}) collective-permute-start(bf16[8,128,128]{2,1,0:T(8,128)(2,1)} %get-tuple-element.69), channel_id=1, source_target_pairs={{0,12},{4,8},{8,4},{12,0},{1,13},{5,9},{9,5},{13,1},{2,14},{6,10},... | collective-permute-start | bytes 786440 | tf_op jit(solution)/shard_map/ppermute | solution.py:420
  43.2 39.2 %collective-permute-start.20 = (bf16[8,128,128]{2,1,0:T(8,128)(2,1)}, bf16[8,128,128]{2,1,0:T(8,128)(2,1)S(1)}, u32[]{:S(2)}, u32[]{:S(2)}) collective-permute-start(bf16[8,128,128]{2,1,0:T(8,128)(2,1)} %get-tuple-element.59), channel_id=1, source_target_pairs={{0,4},{4,0},{8,12},{12,8},{1,5},{5,1},{9,13},{13,9},{2,6},{6,2},{1... | collective-permute-start | bytes 786440 | tf_op jit(solution)/shard_map/ppermute | solution.py:420
  44.0 54.5 %collective-permute-start.21 = (bf16[8,128,128]{2,1,0:T(8,128)(2,1)}, bf16[8,128,128]{2,1,0:T(8,128)(2,1)S(1)}, u32[]{:S(2)}, u32[]{:S(2)}) collective-permute-start(bf16[8,128,128]{2,1,0:T(8,128)(2,1)} %get-tuple-element.60), channel_id=1, source_target_pairs={{0,8},{4,12},{8,0},{12,4},{1,9},{5,13},{9,1},{13,5},{2,10},{6,14},... | collective-permute-start | bytes 786440 | tf_op jit(solution)/shard_map/ppermute | solution.py:420
  56.4 55.7 %collective-permute-start.22 = (bf16[8,128,128]{2,1,0:T(8,128)(2,1)}, bf16[8,128,128]{2,1,0:T(8,128)(2,1)}, u32[]{:S(2)}, u32[]{:S(2)}) collective-permute-start(bf16[8,128,128]{2,1,0:T(8,128)(2,1)} %get-tuple-element.61), channel_id=1, source_target_pairs={{0,12},{4,8},{8,4},{12,0},{1,13},{5,9},{9,5},{13,1},{2,14},{6,10},... | collective-permute-start | bytes 786440 | tf_op jit(solution)/shard_map/ppermute | solution.py:420
  63.7 50.4 %collective-permute-start.14 = (bf16[8,128,128]{2,1,0:T(8,128)(2,1)}, bf16[8,128,128]{2,1,0:T(8,128)(2,1)S(1)}, u32[]{:S(2)}, u32[]{:S(2)}) collective-permute-start(bf16[8,128,128]{2,1,0:T(8,128)(2,1)} %get-tuple-element.51), channel_id=1, source_target_pairs={{0,4},{4,0},{8,12},{12,8},{1,5},{5,1},{9,13},{13,9},{2,6},{6,2},{1... | collective-permute-start | bytes 786440 | tf_op jit(solution)/shard_map/ppermute | solution.py:420
  64.4 51.0 %collective-permute-start.15 = (bf16[8,128,128]{2,1,0:T(8,128)(2,1)}, bf16[8,128,128]{2,1,0:T(8,128)(2,1)S(1)}, u32[]{:S(2)}, u32[]{:S(2)}) collective-permute-start(bf16[8,128,128]{2,1,0:T(8,128)(2,1)} %get-tuple-element.52), channel_id=1, source_target_pairs={{0,8},{4,12},{8,0},{12,4},{1,9},{5,13},{9,1},{13,5},{2,10},{6,14},... | collective-permute-start | bytes 786440 | tf_op jit(solution)/shard_map/ppermute | solution.py:420
  82.3 34.7 %collective-permute-start.16 = (bf16[8,128,128]{2,1,0:T(8,128)(2,1)}, bf16[8,128,128]{2,1,0:T(8,128)(2,1)S(1)}, u32[]{:S(2)}, u32[]{:S(2)}) collective-permute-start(bf16[8,128,128]{2,1,0:T(8,128)(2,1)} %get-tuple-element.53), channel_id=1, source_target_pairs={{0,12},{4,8},{8,4},{12,0},{1,13},{5,9},{9,5},{13,1},{2,14},{6,10},... | collective-permute-start | bytes 786440 | tf_op jit(solution)/shard_map/ppermute | solution.py:420
  98.5 21.3 %collective-permute-start.7 = (bf16[4,128,128]{2,1,0:T(8,128)(2,1)S(1)}, bf16[4,128,128]{2,1,0:T(8,128)(2,1)S(1)}, u32[]{:S(2)}, u32[]{:S(2)}) collective-permute-start(bf16[4,128,128]{2,1,0:T(8,128)(2,1)S(1)} %get-tuple-element.47), channel_id=1, source_target_pairs={{0,4},{4,0},{8,12},{12,8},{1,5},{5,1},{9,13},{13,9},{2,6},{6,2},{1... | collective-permute-start | bytes 393224 | tf_op jit(solution)/shard_map/ppermute | solution.py:420
  112.1 49.9 %collective-permute-start.35 = (bf16[8,128,128]{2,1,0:T(8,128)(2,1)S(1)}, bf16[8,128,128]{2,1,0:T(8,128)(2,1)S(1)}, u32[]{:S(2)}, u32[]{:S(2)}) collective-permute-start(bf16[8,128,128]{2,1,0:T(8,128)(2,1)S(1)} %get-tuple-element.79), channel_id=1, source_target_pairs={{0,4},{4,0},{8,12},{12,8},{1,5},{5,1},{9,13},{13,9},{2,6},{6,2},{1... | collective-permute-start | bytes 786440 | tf_op jit(solution)/shard_map/ppermute | solution.py:420
  114.1 49.4 %collective-permute-start.36 = (bf16[8,128,128]{2,1,0:T(8,128)(2,1)S(1)}, bf16[8,128,128]{2,1,0:T(8,128)(2,1)S(1)}, u32[]{:S(2)}, u32[]{:S(2)}) collective-permute-start(bf16[8,128,128]{2,1,0:T(8,128)(2,1)S(1)} %get-tuple-element.80), channel_id=1, source_target_pairs={{0,8},{4,12},{8,0},{12,4},{1,9},{5,13},{9,1},{13,5},{2,10},{6,14},... | collective-permute-start | bytes 786440 | tf_op jit(solution)/shard_map/ppermute | solution.py:420
  115.4 25.6 %collective-permute-start.8 = (bf16[4,128,128]{2,1,0:T(8,128)(2,1)S(1)}, bf16[4,128,128]{2,1,0:T(8,128)(2,1)S(1)}, u32[]{:S(2)}, u32[]{:S(2)}) collective-permute-start(bf16[4,128,128]{2,1,0:T(8,128)(2,1)S(1)} %get-tuple-element.48), channel_id=1, source_target_pairs={{0,8},{4,12},{8,0},{12,4},{1,9},{5,13},{9,1},{13,5},{2,10},{6,14},... | collective-permute-start | bytes 393224 | tf_op jit(solution)/shard_map/ppermute | solution.py:420
  117.1 26.4 %collective-permute-start.9 = (bf16[4,128,128]{2,1,0:T(8,128)(2,1)S(1)}, bf16[4,128,128]{2,1,0:T(8,128)(2,1)S(1)}, u32[]{:S(2)}, u32[]{:S(2)}) collective-permute-start(bf16[4,128,128]{2,1,0:T(8,128)(2,1)S(1)} %get-tuple-element.49), channel_id=1, source_target_pairs={{0,12},{4,8},{8,4},{12,0},{1,13},{5,9},{9,5},{13,1},{2,14},{6,10},... | collective-permute-start | bytes 393224 | tf_op jit(solution)/shard_map/ppermute | solution.py:420
  119.7 30.3 %collective-permute-start.10 = (bf16[4,128,128]{2,1,0:T(8,128)(2,1)S(1)}, bf16[4,128,128]{2,1,0:T(8,128)(2,1)S(1)}, u32[]{:S(2)}, u32[]{:S(2)}) collective-permute-start(bf16[4,128,128]{2,1,0:T(8,128)(2,1)S(1)} %get-tuple-element.46.rest_0_), channel_id=1, source_target_pairs={{0,1},{1,0},{2,3},{3,2},{4,5},{5,4},{6,7},{7,6},{8,9},{9,8},{10,11... | collective-permute-start | bytes 393224 | tf_op jit(solution)/shard_map/ppermute | solution.py:425
  141.1 23.5 %collective-permute-start.37 = (bf16[8,128,128]{2,1,0:T(8,128)(2,1)S(1)}, bf16[8,128,128]{2,1,0:T(8,128)(2,1)S(1)}, u32[]{:S(2)}, u32[]{:S(2)}) collective-permute-start(bf16[8,128,128]{2,1,0:T(8,128)(2,1)S(1)} %get-tuple-element.81), channel_id=1, source_target_pairs={{0,12},{4,8},{8,4},{12,0},{1,13},{5,9},{9,5},{13,1},{2,14},{6,10},... | collective-permute-start | bytes 786440 | tf_op jit(solution)/shard_map/ppermute | solution.py:420
  143.5 21.1 %collective-permute-start.29 = (bf16[8,128,128]{2,1,0:T(8,128)(2,1)S(1)}, bf16[8,128,128]{2,1,0:T(8,128)(2,1)S(1)}, u32[]{:S(2)}, u32[]{:S(2)}) collective-permute-start(bf16[8,128,128]{2,1,0:T(8,128)(2,1)S(1)} %get-tuple-element.71), channel_id=1, source_target_pairs={{0,4},{4,0},{8,12},{12,8},{1,5},{5,1},{9,13},{13,9},{2,6},{6,2},{1... | collective-permute-start | bytes 786440 | tf_op jit(solution)/shard_map/ppermute | solution.py:420
  177.0 20.9 %collective-permute-start.24 = (bf16[8,128,128]{2,1,0:T(8,128)(2,1)S(1)}, bf16[8,128,128]{2,1,0:T(8,128)(2,1)S(1)}, u32[]{:S(2)}, u32[]{:S(2)}) collective-permute-start(bf16[8,128,128]{2,1,0:T(8,128)(2,1)S(1)} %get-tuple-element.64), channel_id=1, source_target_pairs={{0,8},{4,12},{8,0},{12,4},{1,9},{5,13},{9,1},{13,5},{2,10},{6,14},... | collective-permute-start | bytes 786440 | tf_op jit(solution)/shard_map/ppermute | solution.py:420
  177.7 20.2 %collective-permute-start.25 = (bf16[8,128,128]{2,1,0:T(8,128)(2,1)S(1)}, bf16[8,128,128]{2,1,0:T(8,128)(2,1)S(1)}, u32[]{:S(2)}, u32[]{:S(2)}) collective-permute-start(bf16[8,128,128]{2,1,0:T(8,128)(2,1)S(1)} %get-tuple-element.65), channel_id=1, source_target_pairs={{0,12},{4,8},{8,4},{12,0},{1,13},{5,9},{9,5},{13,1},{2,14},{6,10},... | collective-permute-start | bytes 786440 | tf_op jit(solution)/shard_map/ppermute | solution.py:420
  179.6 19.6 %collective-permute-start.17 = (bf16[8,128,128]{2,1,0:T(8,128)(2,1)S(1)}, bf16[8,128,128]{2,1,0:T(8,128)(2,1)S(1)}, u32[]{:S(2)}, u32[]{:S(2)}) collective-permute-start(bf16[8,128,128]{2,1,0:T(8,128)(2,1)S(1)} %get-tuple-element.55), channel_id=1, source_target_pairs={{0,4},{4,0},{8,12},{12,8},{1,5},{5,1},{9,13},{13,9},{2,6},{6,2},{1... | collective-permute-start | bytes 786440 | tf_op jit(solution)/shard_map/ppermute | solution.py:420
  180.6 39.7 %collective-permute-start.18 = (bf16[8,128,128]{2,1,0:T(8,128)(2,1)S(1)}, bf16[8,128,128]{2,1,0:T(8,128)(2,1)S(1)}, u32[]{:S(2)}, u32[]{:S(2)}) collective-permute-start(bf16[8,128,128]{2,1,0:T(8,128)(2,1)S(1)} %get-tuple-element.56), channel_id=1, source_target_pairs={{0,8},{4,12},{8,0},{12,4},{1,9},{5,13},{9,1},{13,5},{2,10},{6,14},... | collective-permute-start | bytes 786440 | tf_op jit(solution)/shard_map/ppermute | solution.py:420
  182.1 38.1 %collective-permute-start.19 = (bf16[8,128,128]{2,1,0:T(8,128)(2,1)S(1)}, bf16[8,128,128]{2,1,0:T(8,128)(2,1)S(1)}, u32[]{:S(2)}, u32[]{:S(2)}) collective-permute-start(bf16[8,128,128]{2,1,0:T(8,128)(2,1)S(1)} %get-tuple-element.57), channel_id=1, source_target_pairs={{0,12},{4,8},{8,4},{12,0},{1,13},{5,9},{9,5},{13,1},{2,14},{6,10},... | collective-permute-start | bytes 786440 | tf_op jit(solution)/shard_map/ppermute | solution.py:420
  (54 other events, 945.1 us)

commit v3 on v2

--- a/solution.py
+++ b/solution.py
@@ -95,12 +95,6 @@
     )
 
 
-def mixed_float(mixer, values):
-    rounded = values.astype(bf16)
-    left = (values - rounded.astype(f32)).astype(bf16)
-    return mixed(mixer, rounded) + jnp.dot(mixer[0][...], left, preferred_element_type=f32)
-
-
 def weighted(coef, s, channels):
     total = None
     for p in range(coef.shape[0]):
@@ -123,40 +117,39 @@
     far, outs, near, rest = refs[:8], refs[8 : 8 + n], refs[8 + n : 16 + n], refs[16 + n :]
     rates, coef, advect, diffuse, state, d1, d2, filt = near
     filt_own, rates_high, rates_low, rate, middle, ready, sems, out_sems = rest
-    copies = [pltpu.make_async_copy(far[i], near[i], sems.at[i]) for i in range(8)]
+    me, half = lax.axis_index("pencil"), lax.axis_index("field")
+    fields, _, rows, length = state.shape
+    size = length // n
+    sources = list(far)
+    sources[4] = far[4].at[:, :, aligned(half, rows), :]
+    copies = [pltpu.make_async_copy(sources[i], near[i], sems.at[i]) for i in range(8)]
     for copy in copies:
         copy.start()
-    me, half = lax.axis_index("pencil"), lax.axis_index("field")
-    count, _, rows, length = state.shape
-    fields = outs[0].shape[0]
-    size = length // n
-    first = half * fields
     for copy in copies[:4]:
         copy.wait()
     fill_mixer(lambda a, b: rates[a, b], rates_high, rates_low)
     copies[4].wait()
-    for j in range(rows // DEPTH):
-        down = slice(j * DEPTH, (j + 1) * DEPTH)
-        for c in range(length // WIDE):
-            across = slice(c * WIDE, (c + 1) * WIDE)
-            u = state[:, 0, down, across].reshape(count * DEPTH, WIDE)
+    own = state[:, 0].reshape(fields * rows, length)
+    for c in range(length // WIDE):
+        across = slice(c * WIDE, (c + 1) * WIDE)
+        for j in range(rows // DEPTH):
+            u = state[:, 0, j * DEPTH : (j + 1) * DEPTH, across].reshape(fields * DEPTH, WIDE)
             activity = jnp.tanh(mixed((rates_high, rates_low), u))
             for s in range(fields):
                 at = slice(s * rows + j * DEPTH, s * rows + (j + 1) * DEPTH)
-                rate[at, across] = weighted(coef, first + s, activity)
-    own = state[pl.ds(first, fields), 0].reshape(fields * rows, length)
-    copies[5].wait()
-    copies[6].wait()
-    for c in range(length // WIDE):
-        across = slice(c * WIDE, (c + 1) * WIDE)
+                rate[at, across] = weighted(coef, s, activity)
+        if c == 0:
+            for copy in copies[5:]:
+                copy.wait()
         slope = jnp.dot(own, d1[:, across], preferred_element_type=f32)
+        for s in range(fields):
+            at = slice(s * rows, (s + 1) * rows)
+            rate[at, across] = rate[at, across] - advect[0, s] * slope[at]
         curve = jnp.dot(own, d2[:, across], preferred_element_type=f32)
         for s in range(fields):
             at = slice(s * rows, (s + 1) * rows)
-            middle[at, across] = advance(
-                own[at, across], curve[at], slope[at], rate[at, across], diffuse[first + s], advect[0, first + s]
-            )
-    copies[7].wait()
+            moved = own[at, across].astype(f32) + time_step * (diffuse[s] * curve[at] + rate[at, across])
+            middle[at, across] = moved.astype(bf16)
     for r in range(n):
         filt_own[:, r * size : (r + 1) * size] = filt[:, aligned(me ^ r, size)]
     sends = []
@@ -206,60 +199,54 @@
 
 
 def y_kernel(n, q, params_here, rates, coef, advect, diffuse, *rest):
-    own, rest = rest[:n], rest[n:]
-    other, rest = rest[:n], rest[n:]
-    if q is None:
-        arrived = own
-    else:
+    own, other, rest = rest[:n], rest[n : 2 * n], rest[2 * n :]
+    if q is not None:
         arrived, rest = rest[:n], rest[n:]
     d1t, d2t, filtt = rest[:3]
     outs, rest = rest[3 : 3 + n], rest[3 + n :]
-    filt_own, v_full, rate_full, state_high, state_low, coef_high, coef_low = rest[:7]
+    filt_own, u_full, rate_full, rates_high, rates_low = rest[:5]
+    v_full = u_full if q is None else rest[5]
     me, half = lax.axis_index("pencil"), lax.axis_index("field")
-    here = own[0].shape[0]
-    count = rates.shape[1]
-    size = own[0].shape[1]
+    count, rows, size = own[0].shape
     fields = outs[0].shape[0]
-    first = half * here if q is None else 0
-
-    fill_mixer(lambda a, b: rates[a, lax.rem(half * here + b, count)], state_high, state_low)
-    fill_mixer(lambda a, b: coef[b, first + a], coef_high, coef_low)
-    if q is not None:
-        rates_high, rates_low = rest[7:]
-        fill_mixer(lambda a, b: rates[a, b], rates_high, rates_low)
-
-    def tile(refs, down):
-        return jnp.concatenate([ref[:, down, :].reshape(ref.shape[0] * DEPTH, size) for ref in refs], axis=0)
-
-    def pair(refs, j):
-        starts = [(2 * j + k) * DEPTH for k in range(2)]
-        return jnp.concatenate([tile(refs, pl.ds(pl.multiple_of(at, DEPTH), DEPTH)) for at in starts], axis=1)
+    first = half * fields if q is None else 0
+    fill_mixer(lambda a, b: rates[a, b], rates_high, rates_low)
 
     for r in range(n):
         filt_own[r * size : (r + 1) * size, :] = filtt[aligned(me ^ r, size), :]
+        for s in range(count):
+            across = slice(s * size, (s + 1) * size)
+            u_full[aligned(2 * (me ^ r) + half, rows), across] = own[r][s]
+            u_full[aligned(2 * (me ^ r) + 1 - half, rows), across] = other[r][s]
+            if q is not None:
+                v_full[aligned(me ^ r, size), across] = arrived[r][s]
+
+    def pair(full, block):
+        tiles = []
+        for k in range(2):
+            down = aligned(2 * block + k, DEPTH)
+            tiles.append(
+                jnp.concatenate([full[down, s * size : (s + 1) * size] for s in range(count)], axis=0)
+            )
+        return jnp.concatenate(tiles, axis=1)
+
+    def rate_block(block, carry):
+        scaled = jnp.tanh(mixed((rates_high, rates_low), pair(u_full, block)))
+        if q is not None:
+            mixing = mixed((rates_high, rates_low), pair(v_full, block))
+            scaled = tangent_scaled(scaled, mixing, half * params_here + q)
         for s in range(fields):
-            v_full[aligned(me ^ r, size), s * size : (s + 1) * size] = arrived[r][s]
-
-        def rate_block(j, carry, r=r):
-            activity = jnp.tanh(mixed((state_high, state_low), pair((own[r], other[r]), j)))
-            if q is None:
-                scaled = activity
-            else:
-                mixing = mixed((rates_high, rates_low), pair((arrived[r],), j))
-                scaled = tangent_scaled(activity, mixing, half * params_here + q)
-            rate = mixed_float((coef_high, coef_low), scaled)
+            rate = weighted(coef, first + s, scaled)
             for k in range(2):
-                down = pl.ds(pl.multiple_of((me ^ r) * size + (2 * j + k) * DEPTH, DEPTH), DEPTH)
-                for s in range(fields):
-                    rate_full[down, s * size : (s + 1) * size] = rate[
-                        s * DEPTH : (s + 1) * DEPTH, k * size : (k + 1) * size
-                    ]
-            return carry
-
-        lax.fori_loop(0, size // (2 * DEPTH), rate_block, 0)
+                rate_full[aligned(2 * block + k, DEPTH), s * size : (s + 1) * size] = rate[
+                    :, k * size : (k + 1) * size
+                ]
+        return carry
+
+    lax.fori_loop(0, n * size // (2 * DEPTH), rate_block, 0)
 
     def two_fields(f, carry):
-        v = v_full[:, aligned(f, 2 * size)]
+        v = v_full[:, aligned(first // 2 + f, 2 * size)]
         slope = jnp.dot(d1t[...], v, preferred_element_type=f32)
         curve = jnp.dot(d2t[...], v, preferred_element_type=f32)
         columns = []
@@ -286,21 +273,21 @@
     lax.fori_loop(0, fields // 2, two_fields, 0)
 
 
-def place_kernel(n, q, *rest):
+def place_kernel(n, q, some, *rest):
     out, sems = rest[-2:]
     me, half = lax.axis_index("pencil"), lax.axis_index("field")
     groups = 2 if q is None else 1
     copies = []
     for g in range(groups):
-        for r in range(n):
-            slot = rest[g * n + r]
+        for i, r in enumerate(some):
+            slot = rest[g * n + i]
             here, _, size = slot.shape
             across = aligned(me ^ r, size)
             if q is None:
                 target = out.at[aligned(half if g == 0 else 1 - half, here), 0, :, across]
             else:
                 target = out.at[q, :, 0, :, across]
-            copies.append(pltpu.make_async_copy(slot, target, sems.at[g * n + r]))
+            copies.append(pltpu.make_async_copy(slot, target, sems.at[g * n + i]))
     for copy in copies:
         copy.start()
     for copy in copies:
@@ -321,25 +308,26 @@
     return [pltpu.VMEM((fields * DEPTH, count * DEPTH), bf16)] * 2
 
 
-def x_state_call(n, scalars, state, d1, d2, filt, here):
+def x_state_call(n, scalars, state, d1, d2, filt):
     count, _, deep, length = state.shape
+    rows = deep // 2
     square = pltpu.VMEM((length, length), bf16)
     return pl.pallas_call(
         functools.partial(x_state_kernel, n),
-        out_shape=[jax.ShapeDtypeStruct((here, deep, length // n), bf16)] * n,
+        out_shape=[jax.ShapeDtypeStruct((count, rows, length // n), bf16)] * n,
         in_specs=[HBM] * 8,
         out_specs=[HBM] * n,
         scratch_shapes=[pltpu.SMEM(scalar.shape, f32) for scalar in scalars]
-        + [pltpu.VMEM(state.shape, bf16), square, square, square, square]
+        + [pltpu.VMEM((count, 1, rows, length), bf16), square, square, square, square]
         + mixers(count, count)
         + [
-            pltpu.VMEM((here * deep, length), f32),
-            pltpu.VMEM((here * deep, length), bf16),
-            pltpu.VMEM((n, here, deep, length // n), bf16),
+            pltpu.VMEM((count * rows, length), f32),
+            pltpu.VMEM((count * rows, length), bf16),
+            pltpu.VMEM((n, count, rows, length // n), bf16),
             pltpu.SemaphoreType.DMA((8,)),
             pltpu.SemaphoreType.DMA((n,)),
         ],
-        cost_estimate=cost(6 * here * deep * length * length, 4 * here * deep * length),
+        cost_estimate=cost(6 * count * rows * length * length, 4 * count * rows * length),
         name="x_state",
     )(*scalars, state, d1, d2, filt)
 
@@ -367,32 +355,27 @@
 
 
 def y_call(n, q, params_here, scalars, own, other, arrived, turned):
-    here, deep, size = own[0].shape
-    count = scalars[0].shape[1]
-    length = deep * n
-    fields = here if q is None else count
+    count, _, size = own[0].shape
+    length = size * n
+    fields = count // 2 if q is None else count
     arrays = list(own) + list(other) + list(arrived or ())
+    full = pltpu.VMEM((length, count * size), bf16)
     return pl.pallas_call(
         functools.partial(y_kernel, n, q, params_here),
-        out_shape=[jax.ShapeDtypeStruct((fields, deep, size), bf16)] * n,
+        out_shape=[jax.ShapeDtypeStruct((fields, size, size), bf16)] * n,
         in_specs=[SMEM] * 4 + [VMEM] * (len(arrays) + 3),
         out_specs=[VMEM] * n,
-        scratch_shapes=[
-            pltpu.VMEM((length, length), bf16),
-            pltpu.VMEM((length, fields * size), bf16),
-            pltpu.VMEM((length, fields * size), f32),
-        ]
+        scratch_shapes=[pltpu.VMEM((length, length), bf16), full, pltpu.VMEM((length, fields * size), f32)]
         + mixers(count, count)
-        + mixers(fields, count)
-        + ([] if q is None else mixers(count, count)),
+        + ([] if q is None else [full]),
         compiler_params=GRANT,
-        cost_estimate=cost(6 * fields * deep * length * length, 4 * fields * deep * length),
+        cost_estimate=cost(6 * fields * size * length * length, 4 * fields * size * length),
     )(*scalars, *arrays, *turned)
 
 
 def place_state(n, shape, own, other):
     return pl.pallas_call(
-        functools.partial(place_kernel, n, None),
+        functools.partial(place_kernel, n, None, range(n)),
         out_shape=jax.ShapeDtypeStruct(shape, bf16),
         in_specs=[VMEM] * (2 * n),
         out_specs=HBM,
@@ -402,22 +385,25 @@
     )(*own, *other)
 
 
-def place_tangent(n, q, shape, slots, buffer):
+def place_tangent(n, q, some, shape, slots, buffer):
+    slots = [slots[r] for r in some]
     earlier = [] if buffer is None else [buffer]
     return pl.pallas_call(
-        functools.partial(place_kernel, n, q),
+        functools.partial(place_kernel, n, q, some),
         out_shape=jax.ShapeDtypeStruct(shape, bf16),
-        in_specs=[VMEM] * n + [HBM] * len(earlier),
+        in_specs=[VMEM] * len(slots) + [HBM] * len(earlier),
         out_specs=HBM,
-        scratch_shapes=[pltpu.SemaphoreType.DMA((n,))],
-        input_output_aliases={n: 0} if earlier else {},
+        scratch_shapes=[pltpu.SemaphoreType.DMA((len(slots),))],
+        input_output_aliases={len(slots): 0} if earlier else {},
         compiler_params=GRANT,
     )(*slots, *earlier)
 
 
 def exchange(n, slots):
     order = list(range(n // 2, n)) + list(range(1, n // 2))
-    arrived = {r: lax.ppermute(slots[r], "pencil", [(i, i ^ r) for i in range(n)]) for r in order}
+    arrived = {}
+    for r in order:
+        arrived[r] = lax.ppermute(slots[r], "pencil", [(i, i ^ r) for i in range(n)])
     return [slots[0]] + [arrived[r] for r in range(1, n)]
 
 
@@ -427,12 +413,11 @@
 
 def pipelined(n, state, tangents, d1, d2, filt, advect, diffuse, coef, rates):
     params = range(tangents.shape[0])
-    here = state.shape[0] // 2
     scalars = (rates, coef, advect, diffuse)
 
     def forth(q):
         if q is None:
-            return x_state_call(n, scalars, state, d1, d2, filt, here)
+            return x_state_call(n, scalars, state, d1, d2, filt)
         return x_call(n, q, scalars, state, tangents, d1, d2, filt)
 
     own = exchange(n, forth(None))
@@ -448,7 +433,9 @@
     buffer = None
     for q in params:
         back = exchange(n, turn(q))
-        buffer = place_tangent(n, q, tangents.shape, back, buffer)
+        early = range(n if q < params[-1] else n - 1)
+        buffer = place_tangent(n, q, early, tangents.shape, back, buffer)
+    buffer = place_tangent(n, q, range(n - 1, n), tangents.shape, back, buffer)
     return (place_state(n, state.shape, mine, theirs), buffer)
 
 

time: 226 us -> 215 us (0.951); the launches traced: 221 us -> 214 us
  Pallas kernels: 85.8 us -> 76.1 us
  starting transfers between devices: 69.4 us -> 77.7 us
  waiting for transfers between devices: 49.9 us -> 44.4 us
    pallas_call x5, Pallas kernels: 49.9 us -> 40.3 us  [y_call(): pl.pallas_call(functools.partial(y_kernel, n, q, params_here), out_shape=...]
    ppermute x30, starting transfers between devices: 68.4 us -> 76.6 us  [exchange(): lax.ppermute(slots[r], 'pencil', [(i, i ^ r) for i in range(n)])]
    ppermute x30, waiting for transfers between devices: 49.9 us -> 44.4 us  [exchange(): lax.ppermute(slots[r], 'pencil', [(i, i ^ r) for i in range(n)])]
    pallas_call x5 -> x6, Pallas kernels: 5.03 us -> 5.7 us  [the longest x5 4.66 us: place_tangent(): pl.pallas_call(functools.partial(place_kernel, n, q, some), out_shape=jax...]
    unnamed x83 -> x85, local copies, waits for them, and re-layouts: 15 us -> 14.9 us
  transfers between devices with their start and end apart: 38 -> 38, of which waited for: 6 -> 4; matrix products, arithmetic and copies ran while one was open for 1% -> 1% of each run, Pallas kernels for 36% -> 33%
where the time goes in v3:
time: 215 us; the launch traced here: 214 us
  starting transfers between devices  77.7 us (36%)
  Pallas kernels  76.1 us (35%)
  waiting for transfers between devices  44.4 us (21%)
  local copies, waits for them, and re-layouts  14.9 us (7%)
    ppermute x30, starting transfers between devices, exchange(): lax.ppermute(slots[r], 'pencil', [(i, i ^ r) for i in range(n)])  76.6 us
    ppermute x30, waiting for transfers between devices, exchange(): lax.ppermute(slots[r], 'pencil', [(i, i ^ r) for i in range(n)])  44.4 us
    pallas_call x5, Pallas kernels, y_call(): pl.pallas_call(functools.partial(y_kernel, n, q, params_here), out_shape=...  40.3 us
    pallas_call x4, Pallas kernels, x_call(): pl.pallas_call(functools.partial(x_kernel, n, q, params_here), grid=(deep...  26.2 us
    unnamed x85, local copies, waits for them, and re-layouts  14.9 us
    pallas_call x5, Pallas kernels, place_tangent(): pl.pallas_call(functools.partial(place_kernel, n, q, some), out_shape=jax...  4.66 us
  transfers between devices with their start and end apart: 38, of which 4 were waited for; matrix products, arithmetic and copies ran while one was open for 1% of the time, Pallas kernels for 33%

profile of v3, /device:TPU:0, one launch (start us, length us, event | category | flops | bytes accessed | tf_op | source)
XLA Modules:
  0.0 214.4 jit_solution(6648711116933131270)
XLA Ops:
  0.6 3.9 %x_state.1 = (bf16[8,64,128]{2,1,0:T(8,128)(2,1)}, bf16[8,64,128]{2,1,0:T(8,128)(2,1)}, bf16[8,64,128]{2,1,0:T(8,128)(2,1)}, bf16[8,64,128]{2,1,0:T(8,128)(2,1)}) custom-call(f32[8,8]{1,0:T(8,128)} %rates.17, f32[8,8]{1,0:T(8,128)} %coef.17, f32[2,8]{1,0:T(2,128)} %advect.17, f32[8]{0:T(128)} %diffuse.17, bf16[8,1,128,512]{3,2,1,0:T(8,128)(2,1)} %state.7, ...), custom_call_target="tpu_custom_call" | custom-call | flops 805306368 | bytes 1048576 | tf_op jit(solution)/shard_map/x_state/pallas_call | solution.py:315
  4.6 3.1 %collective-permute-start = (bf16[8,64,128]{2,1,0:T(8,128)(2,1)}, bf16[8,64,128]{2,1,0:T(8,128)(2,1)S(1)}, u32[]{:S(2)}, u32[]{:S(2)}) collective-permute-start(bf16[8,64,128]{2,1,0:T(8,128)(2,1)} %get-tuple-element.43), channel_id=1, source_target_pairs={{0,4},{4,0},{8,12},{12,8},{1,5},{5,1},{9,13},{13,9},{2,6},{6,2},{1... | collective-permute-start | bytes 393224 | tf_op jit(solution)/shard_map/ppermute | solution.py:406
  10.3 6.5 %shard_map.111 = (bf16[8,128,128]{2,1,0:T(8,128)(2,1)}, bf16[8,128,128]{2,1,0:T(8,128)(2,1)}, bf16[8,128,128]{2,1,0:T(8,128)(2,1)}, bf16[8,128,128]{2,1,0:T(8,128)(2,1)}) custom-call(f32[8,8]{1,0:T(8,128)} %rates.17, f32[8,8]{1,0:T(8,128)} %coef.17, f32[2,8]{1,0:T(2,128)} %advect.17, f32[8]{0:T(128)} %diffuse.17, bf16[8,1,128,512]{3,2,1,0:T(8,128)(2,1)} %state.7, ...), custom_call_target="tpu_custom_call" | custom-call | flops 1610612736 | bytes 2097152 | tf_op jit(solution)/shard_map/pallas_call | solution.py:339
  17.8 3.5 %collective-permute-start.33 = (bf16[8,128,128]{2,1,0:T(8,128)(2,1)}, bf16[8,128,128]{2,1,0:T(8,128)(2,1)S(1)}, u32[]{:S(2)}, u32[]{:S(2)}) collective-permute-start(bf16[8,128,128]{2,1,0:T(8,128)(2,1)} %get-tuple-element.76), channel_id=1, source_target_pairs={{0,8},{4,12},{8,0},{12,4},{1,9},{5,13},{9,1},{13,5},{2,10},{6,14},... | collective-permute-start | bytes 786440 | tf_op jit(solution)/shard_map/ppermute | solution.py:406
  21.3 6.6 %shard_map.109 = (bf16[8,128,128]{2,1,0:T(8,128)(2,1)}, bf16[8,128,128]{2,1,0:T(8,128)(2,1)}, bf16[8,128,128]{2,1,0:T(8,128)(2,1)}, bf16[8,128,128]{2,1,0:T(8,128)(2,1)}) custom-call(f32[8,8]{1,0:T(8,128)} %rates.17, f32[8,8]{1,0:T(8,128)} %coef.17, f32[2,8]{1,0:T(2,128)} %advect.17, f32[8]{0:T(128)} %diffuse.17, bf16[8,1,128,512]{3,2,1,0:T(8,128)(2,1)} %state.7, ...), custom_call_target="tpu_custom_call" | custom-call | flops 1610612736 | bytes 2097152 | tf_op jit(solution)/shard_map/pallas_call | solution.py:339
  30.3 6.5 %shard_map.107 = (bf16[8,128,128]{2,1,0:T(8,128)(2,1)}, bf16[8,128,128]{2,1,0:T(8,128)(2,1)}, bf16[8,128,128]{2,1,0:T(8,128)(2,1)}, bf16[8,128,128]{2,1,0:T(8,128)(2,1)}) custom-call(f32[8,8]{1,0:T(8,128)} %rates.17, f32[8,8]{1,0:T(8,128)} %coef.17, f32[2,8]{1,0:T(2,128)} %advect.17, f32[8]{0:T(128)} %diffuse.17, bf16[8,1,128,512]{3,2,1,0:T(8,128)(2,1)} %state.7, ...), custom_call_target="tpu_custom_call" | custom-call | flops 1610612736 | bytes 2097152 | tf_op jit(solution)/shard_map/pallas_call | solution.py:339
  38.2 2.6 %collective-permute-start.27 = (bf16[8,128,128]{2,1,0:T(8,128)(2,1)}, bf16[8,128,128]{2,1,0:T(8,128)(2,1)S(1)}, u32[]{:S(2)}, u32[]{:S(2)}) collective-permute-start(bf16[8,128,128]{2,1,0:T(8,128)(2,1)} %get-tuple-element.68), channel_id=1, source_target_pairs={{0,8},{4,12},{8,0},{12,4},{1,9},{5,13},{9,1},{13,5},{2,10},{6,14},... | collective-permute-start | bytes 786440 | tf_op jit(solution)/shard_map/ppermute | solution.py:406
  44.1 4.0 %collective-permute-start.21 = (bf16[8,128,128]{2,1,0:T(8,128)(2,1)}, bf16[8,128,128]{2,1,0:T(8,128)(2,1)S(1)}, u32[]{:S(2)}, u32[]{:S(2)}) collective-permute-start(bf16[8,128,128]{2,1,0:T(8,128)(2,1)} %get-tuple-element.60), channel_id=1, source_target_pairs={{0,8},{4,12},{8,0},{12,4},{1,9},{5,13},{9,1},{13,5},{2,10},{6,14},... | collective-permute-start | bytes 786440 | tf_op jit(solution)/shard_map/ppermute | solution.py:406
  48.2 6.5 %shard_map.105 = (bf16[8,128,128]{2,1,0:T(8,128)(2,1)}, bf16[8,128,128]{2,1,0:T(8,128)(2,1)}, bf16[8,128,128]{2,1,0:T(8,128)(2,1)}, bf16[8,128,128]{2,1,0:T(8,128)(2,1)}) custom-call(f32[8,8]{1,0:T(8,128)} %rates.17, f32[8,8]{1,0:T(8,128)} %coef.17, f32[2,8]{1,0:T(2,128)} %advect.17, f32[8]{0:T(128)} %diffuse.17, bf16[8,1,128,512]{3,2,1,0:T(8,128)(2,1)} %state.7, ...), custom_call_target="tpu_custom_call" | custom-call | flops 1610612736 | bytes 2097152 | tf_op jit(solution)/shard_map/pallas_call | solution.py:339
  56.3 5.9 %collective-permute-done.27.rest_10_ = bf16[8,128,128]{2,1,0:T(8,128)(2,1)S(1)} collective-permute-done((bf16[8,128,128]{2,1,0:T(8,128)(2,1)}, bf16[8,128,128]{2,1,0:T(8,128)(2,1)S(1)}, u32[]{:S(2)}, u32[]{:S(2)}) %collective-permute-start.27) | collective-permute-done | bytes 262176 | tf_op jit(solution)/shard_map/ppermute | solution.py:406
  63.6 17.9 %collective-permute-start.15 = (bf16[8,128,128]{2,1,0:T(8,128)(2,1)}, bf16[8,128,128]{2,1,0:T(8,128)(2,1)S(1)}, u32[]{:S(2)}, u32[]{:S(2)}) collective-permute-start(bf16[8,128,128]{2,1,0:T(8,128)(2,1)} %get-tuple-element.52), channel_id=1, source_target_pairs={{0,8},{4,12},{8,0},{12,4},{1,9},{5,13},{9,1},{13,5},{2,10},{6,14},... | collective-permute-start | bytes 786440 | tf_op jit(solution)/shard_map/ppermute | solution.py:406
  92.7 8.7 %shard_map.112 = (bf16[8,128,128]{2,1,0:T(8,128)(2,1)S(1)}, bf16[8,128,128]{2,1,0:T(8,128)(2,1)S(1)}, bf16[8,128,128]{2,1,0:T(8,128)(2,1)S(1)}, bf16[8,128,128]{2,1,0:T(8,128)(2,1)S(1)}) custom-call(f32[8,8]{1,0:T(8,128)S(1)} %copy-done, f32[8,8]{1,0:T(8,128)S(1)} %copy-done.1, f32[2,8]{1,0:T(2,128)S(1)} %copy-done.2, f32[8]{0:T(128)S(1)} %copy-done.3, ...), custom_call_target="tpu_custom_call" | custom-call | flops 1610612736 | bytes 2097152 | tf_op jit(solution)/shard_map/pallas_call | solution.py:363
  101.6 5.0 %shard_map.104 = (bf16[4,128,128]{2,1,0:T(8,128)(2,1)S(1)}, bf16[4,128,128]{2,1,0:T(8,128)(2,1)S(1)}, bf16[4,128,128]{2,1,0:T(8,128)(2,1)S(1)}, bf16[4,128,128]{2,1,0:T(8,128)(2,1)S(1)}) custom-call(f32[8,8]{1,0:T(8,128)S(1)} %copy-done, f32[8,8]{1,0:T(8,128)S(1)} %copy-done.1, f32[2,8]{1,0:T(2,128)S(1)} %copy-done.2, f32[8]{0:T(128)S(1)} %copy-done.3, ...), custom_call_target="tpu_custom_call" | custom-call | flops 805306368 | bytes 1048576 | tf_op jit(solution)/shard_map/pallas_call | solution.py:363
  106.6 3.3 %collective-permute-start.36 = (bf16[8,128,128]{2,1,0:T(8,128)(2,1)S(1)}, bf16[8,128,128]{2,1,0:T(8,128)(2,1)S(1)}, u32[]{:S(2)}, u32[]{:S(2)}) collective-permute-start(bf16[8,128,128]{2,1,0:T(8,128)(2,1)S(1)} %get-tuple-element.80), channel_id=1, source_target_pairs={{0,8},{4,12},{8,0},{12,4},{1,9},{5,13},{9,1},{13,5},{2,10},{6,14},... | collective-permute-start | bytes 786440 | tf_op jit(solution)/shard_map/ppermute | solution.py:406
  111.6 2.7 %collective-permute-start.9 = (bf16[4,128,128]{2,1,0:T(8,128)(2,1)S(1)}, bf16[4,128,128]{2,1,0:T(8,128)(2,1)S(1)}, u32[]{:S(2)}, u32[]{:S(2)}) collective-permute-start(bf16[4,128,128]{2,1,0:T(8,128)(2,1)S(1)} %get-tuple-element.49), channel_id=1, source_target_pairs={{0,12},{4,8},{8,4},{12,0},{1,13},{5,9},{9,5},{13,1},{2,14},{6,10},... | collective-permute-start | bytes 393224 | tf_op jit(solution)/shard_map/ppermute | solution.py:406
  114.3 8.7 %shard_map.110 = (bf16[8,128,128]{2,1,0:T(8,128)(2,1)S(1)}, bf16[8,128,128]{2,1,0:T(8,128)(2,1)S(1)}, bf16[8,128,128]{2,1,0:T(8,128)(2,1)S(1)}, bf16[8,128,128]{2,1,0:T(8,128)(2,1)S(1)}) custom-call(f32[8,8]{1,0:T(8,128)S(1)} %copy-done, f32[8,8]{1,0:T(8,128)S(1)} %copy-done.1, f32[2,8]{1,0:T(2,128)S(1)} %copy-done.2, f32[8]{0:T(128)S(1)} %copy-done.3, ...), custom_call_target="tpu_custom_call" | custom-call | flops 1610612736 | bytes 2097152 | tf_op jit(solution)/shard_map/pallas_call | solution.py:363
  124.3 13.8 %collective-permute-done.8.rest_2_ = bf16[4,128,128]{2,1,0:T(8,128)(2,1)S(1)} collective-permute-done((bf16[4,128,128]{2,1,0:T(8,128)(2,1)S(1)}, bf16[4,128,128]{2,1,0:T(8,128)(2,1)S(1)}, u32[]{:S(2)}, u32[]{:S(2)}) %collective-permute-start.8) | collective-permute-done | bytes 131104 | tf_op jit(solution)/shard_map/ppermute | solution.py:406
  138.1 4.6 %collective-permute-start.30 = (bf16[8,128,128]{2,1,0:T(8,128)(2,1)S(1)}, bf16[8,128,128]{2,1,0:T(8,128)(2,1)S(1)}, u32[]{:S(2)}, u32[]{:S(2)}) collective-permute-start(bf16[8,128,128]{2,1,0:T(8,128)(2,1)S(1)} %get-tuple-element.72), channel_id=1, source_target_pairs={{0,8},{4,12},{8,0},{12,4},{1,9},{5,13},{9,1},{13,5},{2,10},{6,14},... | collective-permute-start | bytes 786440 | tf_op jit(solution)/shard_map/ppermute | solution.py:406
  143.8 9.1 %shard_map.108 = (bf16[8,128,128]{2,1,0:T(8,128)(2,1)S(1)}, bf16[8,128,128]{2,1,0:T(8,128)(2,1)S(1)}, bf16[8,128,128]{2,1,0:T(8,128)(2,1)S(1)}, bf16[8,128,128]{2,1,0:T(8,128)(2,1)S(1)}) custom-call(f32[8,8]{1,0:T(8,128)S(1)} %copy-done, f32[8,8]{1,0:T(8,128)S(1)} %copy-done.1, f32[2,8]{1,0:T(2,128)S(1)} %copy-done.2, f32[8]{0:T(128)S(1)} %copy-done.3, ...), custom_call_target="tpu_custom_call" | custom-call | flops 1610612736 | bytes 2097152 | tf_op jit(solution)/shard_map/pallas_call | solution.py:363
  153.1 8.7 %shard_map.106 = (bf16[8,128,128]{2,1,0:T(8,128)(2,1)S(1)}, bf16[8,128,128]{2,1,0:T(8,128)(2,1)S(1)}, bf16[8,128,128]{2,1,0:T(8,128)(2,1)S(1)}, bf16[8,128,128]{2,1,0:T(8,128)(2,1)S(1)}) custom-call(f32[8,8]{1,0:T(8,128)S(1)} %copy-done, f32[8,8]{1,0:T(8,128)S(1)} %copy-done.1, f32[2,8]{1,0:T(2,128)S(1)} %copy-done.2, f32[8]{0:T(128)S(1)} %copy-done.3, ...), custom_call_target="tpu_custom_call" | custom-call | flops 1610612736 | bytes 2097152 | tf_op jit(solution)/shard_map/pallas_call | solution.py:363
  161.8 3.3 %collective-permute-start.24 = (bf16[8,128,128]{2,1,0:T(8,128)(2,1)S(1)}, bf16[8,128,128]{2,1,0:T(8,128)(2,1)S(1)}, u32[]{:S(2)}, u32[]{:S(2)}) collective-permute-start(bf16[8,128,128]{2,1,0:T(8,128)(2,1)S(1)} %get-tuple-element.64), channel_id=1, source_target_pairs={{0,8},{4,12},{8,0},{12,4},{1,9},{5,13},{9,1},{13,5},{2,10},{6,14},... | collective-permute-start | bytes 786440 | tf_op jit(solution)/shard_map/ppermute | solution.py:406
  166.2 15.8 %collective-permute-start.19 = (bf16[8,128,128]{2,1,0:T(8,128)(2,1)S(1)}, bf16[8,128,128]{2,1,0:T(8,128)(2,1)S(1)}, u32[]{:S(2)}, u32[]{:S(2)}) collective-permute-start(bf16[8,128,128]{2,1,0:T(8,128)(2,1)S(1)} %get-tuple-element.57), channel_id=1, source_target_pairs={{0,8},{4,12},{8,0},{12,4},{1,9},{5,13},{9,1},{13,5},{2,10},{6,14},... | collective-permute-start | bytes 786440 | tf_op jit(solution)/shard_map/ppermute | solution.py:406
  183.3 13.9 %collective-permute-done.24.rest_2_ = bf16[8,128,128]{2,1,0:T(8,128)(2,1)S(1)} collective-permute-done((bf16[8,128,128]{2,1,0:T(8,128)(2,1)S(1)}, bf16[8,128,128]{2,1,0:T(8,128)(2,1)S(1)}, u32[]{:S(2)}, u32[]{:S(2)}) %collective-permute-start.24) | collective-permute-done | bytes 262176 | tf_op jit(solution)/shard_map/ppermute | solution.py:406
  197.8 10.6 %collective-permute-done.19.rest_2_ = bf16[8,128,128]{2,1,0:T(8,128)(2,1)S(1)} collective-permute-done((bf16[8,128,128]{2,1,0:T(8,128)(2,1)S(1)}, bf16[8,128,128]{2,1,0:T(8,128)(2,1)S(1)}, u32[]{:S(2)}, u32[]{:S(2)}) %collective-permute-start.19) | collective-permute-done | bytes 262176 | tf_op jit(solution)/shard_map/ppermute | solution.py:406
  (153 shorter events, 37.6 us)
Async XLA Ops:
  16.8 24.0 %collective-permute-start.32 = (bf16[8,128,128]{2,1,0:T(8,128)(2,1)}, bf16[8,128,128]{2,1,0:T(8,128)(2,1)S(1)}, u32[]{:S(2)}, u32[]{:S(2)}) collective-permute-start(bf16[8,128,128]{2,1,0:T(8,128)(2,1)} %get-tuple-element.75), channel_id=1, source_target_pairs={{0,4},{4,0},{8,12},{12,8},{1,5},{5,1},{9,13},{13,9},{2,6},{6,2},{1... | collective-permute-start | bytes 786440 | tf_op jit(solution)/shard_map/ppermute | solution.py:406
  17.8 24.9 %collective-permute-start.33 = (bf16[8,128,128]{2,1,0:T(8,128)(2,1)}, bf16[8,128,128]{2,1,0:T(8,128)(2,1)S(1)}, u32[]{:S(2)}, u32[]{:S(2)}) collective-permute-start(bf16[8,128,128]{2,1,0:T(8,128)(2,1)} %get-tuple-element.76), channel_id=1, source_target_pairs={{0,8},{4,12},{8,0},{12,4},{1,9},{5,13},{9,1},{13,5},{2,10},{6,14},... | collective-permute-start | bytes 786440 | tf_op jit(solution)/shard_map/ppermute | solution.py:406
  38.2 24.0 %collective-permute-start.27 = (bf16[8,128,128]{2,1,0:T(8,128)(2,1)}, bf16[8,128,128]{2,1,0:T(8,128)(2,1)S(1)}, u32[]{:S(2)}, u32[]{:S(2)}) collective-permute-start(bf16[8,128,128]{2,1,0:T(8,128)(2,1)} %get-tuple-element.68), channel_id=1, source_target_pairs={{0,8},{4,12},{8,0},{12,4},{1,9},{5,13},{9,1},{13,5},{2,10},{6,14},... | collective-permute-start | bytes 786440 | tf_op jit(solution)/shard_map/ppermute | solution.py:406
  40.8 22.1 %collective-permute-start.28 = (bf16[8,128,128]{2,1,0:T(8,128)(2,1)}, bf16[8,128,128]{2,1,0:T(8,128)(2,1)S(1)}, u32[]{:S(2)}, u32[]{:S(2)}) collective-permute-start(bf16[8,128,128]{2,1,0:T(8,128)(2,1)} %get-tuple-element.69), channel_id=1, source_target_pairs={{0,12},{4,8},{8,4},{12,0},{1,13},{5,9},{9,5},{13,1},{2,14},{6,10},... | collective-permute-start | bytes 786440 | tf_op jit(solution)/shard_map/ppermute | solution.py:406
  43.4 38.2 %collective-permute-start.20 = (bf16[8,128,128]{2,1,0:T(8,128)(2,1)}, bf16[8,128,128]{2,1,0:T(8,128)(2,1)S(1)}, u32[]{:S(2)}, u32[]{:S(2)}) collective-permute-start(bf16[8,128,128]{2,1,0:T(8,128)(2,1)} %get-tuple-element.59), channel_id=1, source_target_pairs={{0,4},{4,0},{8,12},{12,8},{1,5},{5,1},{9,13},{13,9},{2,6},{6,2},{1... | collective-permute-start | bytes 786440 | tf_op jit(solution)/shard_map/ppermute | solution.py:406
  44.1 57.3 %collective-permute-start.21 = (bf16[8,128,128]{2,1,0:T(8,128)(2,1)}, bf16[8,128,128]{2,1,0:T(8,128)(2,1)S(1)}, u32[]{:S(2)}, u32[]{:S(2)}) collective-permute-start(bf16[8,128,128]{2,1,0:T(8,128)(2,1)} %get-tuple-element.60), channel_id=1, source_target_pairs={{0,8},{4,12},{8,0},{12,4},{1,9},{5,13},{9,1},{13,5},{2,10},{6,14},... | collective-permute-start | bytes 786440 | tf_op jit(solution)/shard_map/ppermute | solution.py:406
  55.4 51.2 %collective-permute-start.22 = (bf16[8,128,128]{2,1,0:T(8,128)(2,1)}, bf16[8,128,128]{2,1,0:T(8,128)(2,1)}, u32[]{:S(2)}, u32[]{:S(2)}) collective-permute-start(bf16[8,128,128]{2,1,0:T(8,128)(2,1)} %get-tuple-element.61), channel_id=1, source_target_pairs={{0,12},{4,8},{8,4},{12,0},{1,13},{5,9},{9,5},{13,1},{2,14},{6,10},... | collective-permute-start | bytes 786440 | tf_op jit(solution)/shard_map/ppermute | solution.py:406
  62.9 47.0 %collective-permute-start.14 = (bf16[8,128,128]{2,1,0:T(8,128)(2,1)}, bf16[8,128,128]{2,1,0:T(8,128)(2,1)S(1)}, u32[]{:S(2)}, u32[]{:S(2)}) collective-permute-start(bf16[8,128,128]{2,1,0:T(8,128)(2,1)} %get-tuple-element.51), channel_id=1, source_target_pairs={{0,4},{4,0},{8,12},{12,8},{1,5},{5,1},{9,13},{13,9},{2,6},{6,2},{1... | collective-permute-start | bytes 786440 | tf_op jit(solution)/shard_map/ppermute | solution.py:406
  63.6 46.3 %collective-permute-start.15 = (bf16[8,128,128]{2,1,0:T(8,128)(2,1)}, bf16[8,128,128]{2,1,0:T(8,128)(2,1)S(1)}, u32[]{:S(2)}, u32[]{:S(2)}) collective-permute-start(bf16[8,128,128]{2,1,0:T(8,128)(2,1)} %get-tuple-element.52), channel_id=1, source_target_pairs={{0,8},{4,12},{8,0},{12,4},{1,9},{5,13},{9,1},{13,5},{2,10},{6,14},... | collective-permute-start | bytes 786440 | tf_op jit(solution)/shard_map/ppermute | solution.py:406
  81.6 30.0 %collective-permute-start.16 = (bf16[8,128,128]{2,1,0:T(8,128)(2,1)}, bf16[8,128,128]{2,1,0:T(8,128)(2,1)S(1)}, u32[]{:S(2)}, u32[]{:S(2)}) collective-permute-start(bf16[8,128,128]{2,1,0:T(8,128)(2,1)} %get-tuple-element.53), channel_id=1, source_target_pairs={{0,12},{4,8},{8,4},{12,0},{1,13},{5,9},{9,5},{13,1},{2,14},{6,10},... | collective-permute-start | bytes 786440 | tf_op jit(solution)/shard_map/ppermute | solution.py:406
  101.5 41.2 %collective-permute-start.35 = (bf16[8,128,128]{2,1,0:T(8,128)(2,1)S(1)}, bf16[8,128,128]{2,1,0:T(8,128)(2,1)S(1)}, u32[]{:S(2)}, u32[]{:S(2)}) collective-permute-start(bf16[8,128,128]{2,1,0:T(8,128)(2,1)S(1)} %get-tuple-element.79), channel_id=1, source_target_pairs={{0,4},{4,0},{8,12},{12,8},{1,5},{5,1},{9,13},{13,9},{2,6},{6,2},{1... | collective-permute-start | bytes 786440 | tf_op jit(solution)/shard_map/ppermute | solution.py:406
  106.6 46.3 %collective-permute-start.36 = (bf16[8,128,128]{2,1,0:T(8,128)(2,1)S(1)}, bf16[8,128,128]{2,1,0:T(8,128)(2,1)S(1)}, u32[]{:S(2)}, u32[]{:S(2)}) collective-permute-start(bf16[8,128,128]{2,1,0:T(8,128)(2,1)S(1)} %get-tuple-element.80), channel_id=1, source_target_pairs={{0,8},{4,12},{8,0},{12,4},{1,9},{5,13},{9,1},{13,5},{2,10},{6,14},... | collective-permute-start | bytes 786440 | tf_op jit(solution)/shard_map/ppermute | solution.py:406
  109.9 28.1 %collective-permute-start.8 = (bf16[4,128,128]{2,1,0:T(8,128)(2,1)S(1)}, bf16[4,128,128]{2,1,0:T(8,128)(2,1)S(1)}, u32[]{:S(2)}, u32[]{:S(2)}) collective-permute-start(bf16[4,128,128]{2,1,0:T(8,128)(2,1)S(1)} %get-tuple-element.48), channel_id=1, source_target_pairs={{0,8},{4,12},{8,0},{12,4},{1,9},{5,13},{9,1},{13,5},{2,10},{6,14},... | collective-permute-start | bytes 393224 | tf_op jit(solution)/shard_map/ppermute | solution.py:406
  111.6 26.5 %collective-permute-start.9 = (bf16[4,128,128]{2,1,0:T(8,128)(2,1)S(1)}, bf16[4,128,128]{2,1,0:T(8,128)(2,1)S(1)}, u32[]{:S(2)}, u32[]{:S(2)}) collective-permute-start(bf16[4,128,128]{2,1,0:T(8,128)(2,1)S(1)} %get-tuple-element.49), channel_id=1, source_target_pairs={{0,12},{4,8},{8,4},{12,0},{1,13},{5,9},{9,5},{13,1},{2,14},{6,10},... | collective-permute-start | bytes 393224 | tf_op jit(solution)/shard_map/ppermute | solution.py:406
  123.1 38.7 %collective-permute-start.37 = (bf16[8,128,128]{2,1,0:T(8,128)(2,1)S(1)}, bf16[8,128,128]{2,1,0:T(8,128)(2,1)S(1)}, u32[]{:S(2)}, u32[]{:S(2)}) collective-permute-start(bf16[8,128,128]{2,1,0:T(8,128)(2,1)S(1)} %get-tuple-element.81), channel_id=1, source_target_pairs={{0,12},{4,8},{8,4},{12,0},{1,13},{5,9},{9,5},{13,1},{2,14},{6,10},... | collective-permute-start | bytes 786440 | tf_op jit(solution)/shard_map/ppermute | solution.py:406
  138.1 27.0 %collective-permute-start.29 = (bf16[8,128,128]{2,1,0:T(8,128)(2,1)S(1)}, bf16[8,128,128]{2,1,0:T(8,128)(2,1)S(1)}, u32[]{:S(2)}, u32[]{:S(2)}) collective-permute-start(bf16[8,128,128]{2,1,0:T(8,128)(2,1)S(1)} %get-tuple-element.71), channel_id=1, source_target_pairs={{0,4},{4,0},{8,12},{12,8},{1,5},{5,1},{9,13},{13,9},{2,6},{6,2},{1... | collective-permute-start | bytes 786440 | tf_op jit(solution)/shard_map/ppermute | solution.py:406
  138.1 28.1 %collective-permute-start.30 = (bf16[8,128,128]{2,1,0:T(8,128)(2,1)S(1)}, bf16[8,128,128]{2,1,0:T(8,128)(2,1)S(1)}, u32[]{:S(2)}, u32[]{:S(2)}) collective-permute-start(bf16[8,128,128]{2,1,0:T(8,128)(2,1)S(1)} %get-tuple-element.72), channel_id=1, source_target_pairs={{0,8},{4,12},{8,0},{12,4},{1,9},{5,13},{9,1},{13,5},{2,10},{6,14},... | collective-permute-start | bytes 786440 | tf_op jit(solution)/shard_map/ppermute | solution.py:406
  142.7 23.5 %collective-permute-start.31 = (bf16[8,128,128]{2,1,0:T(8,128)(2,1)S(1)}, bf16[8,128,128]{2,1,0:T(8,128)(2,1)S(1)}, u32[]{:S(2)}, u32[]{:S(2)}) collective-permute-start(bf16[8,128,128]{2,1,0:T(8,128)(2,1)S(1)} %get-tuple-element.73), channel_id=1, source_target_pairs={{0,12},{4,8},{8,4},{12,0},{1,13},{5,9},{9,5},{13,1},{2,14},{6,10},... | collective-permute-start | bytes 786440 | tf_op jit(solution)/shard_map/ppermute | solution.py:406
  152.9 29.1 %collective-permute-start.23 = (bf16[8,128,128]{2,1,0:T(8,128)(2,1)S(1)}, bf16[8,128,128]{2,1,0:T(8,128)(2,1)S(1)}, u32[]{:S(2)}, u32[]{:S(2)}) collective-permute-start(bf16[8,128,128]{2,1,0:T(8,128)(2,1)S(1)} %get-tuple-element.63), channel_id=1, source_target_pairs={{0,4},{4,0},{8,12},{12,8},{1,5},{5,1},{9,13},{13,9},{2,6},{6,2},{1... | collective-permute-start | bytes 786440 | tf_op jit(solution)/shard_map/ppermute | solution.py:406
  161.8 35.4 %collective-permute-start.24 = (bf16[8,128,128]{2,1,0:T(8,128)(2,1)S(1)}, bf16[8,128,128]{2,1,0:T(8,128)(2,1)S(1)}, u32[]{:S(2)}, u32[]{:S(2)}) collective-permute-start(bf16[8,128,128]{2,1,0:T(8,128)(2,1)S(1)} %get-tuple-element.64), channel_id=1, source_target_pairs={{0,8},{4,12},{8,0},{12,4},{1,9},{5,13},{9,1},{13,5},{2,10},{6,14},... | collective-permute-start | bytes 786440 | tf_op jit(solution)/shard_map/ppermute | solution.py:406
  165.1 32.1 %collective-permute-start.25 = (bf16[8,128,128]{2,1,0:T(8,128)(2,1)S(1)}, bf16[8,128,128]{2,1,0:T(8,128)(2,1)S(1)}, u32[]{:S(2)}, u32[]{:S(2)}) collective-permute-start(bf16[8,128,128]{2,1,0:T(8,128)(2,1)S(1)} %get-tuple-element.65), channel_id=1, source_target_pairs={{0,12},{4,8},{8,4},{12,0},{1,13},{5,9},{9,5},{13,1},{2,14},{6,10},... | collective-permute-start | bytes 786440 | tf_op jit(solution)/shard_map/ppermute | solution.py:406
  166.2 31.5 %collective-permute-start.18 = (bf16[8,128,128]{2,1,0:T(8,128)(2,1)S(1)}, bf16[8,128,128]{2,1,0:T(8,128)(2,1)S(1)}, u32[]{:S(2)}, u32[]{:S(2)}) collective-permute-start(bf16[8,128,128]{2,1,0:T(8,128)(2,1)S(1)} %get-tuple-element.56), channel_id=1, source_target_pairs={{0,4},{4,0},{8,12},{12,8},{1,5},{5,1},{9,13},{13,9},{2,6},{6,2},{1... | collective-permute-start | bytes 786440 | tf_op jit(solution)/shard_map/ppermute | solution.py:406
  166.2 42.2 %collective-permute-start.19 = (bf16[8,128,128]{2,1,0:T(8,128)(2,1)S(1)}, bf16[8,128,128]{2,1,0:T(8,128)(2,1)S(1)}, u32[]{:S(2)}, u32[]{:S(2)}) collective-permute-start(bf16[8,128,128]{2,1,0:T(8,128)(2,1)S(1)} %get-tuple-element.57), channel_id=1, source_target_pairs={{0,8},{4,12},{8,0},{12,4},{1,9},{5,13},{9,1},{13,5},{2,10},{6,14},... | collective-permute-start | bytes 786440 | tf_op jit(solution)/shard_map/ppermute | solution.py:406
  182.0 30.4 %collective-permute-start.17 = (bf16[8,128,128]{2,1,0:T(8,128)(2,1)S(1)}, bf16[8,128,128]{2,1,0:T(8,128)(2,1)S(1)}, u32[]{:S(2)}, u32[]{:S(2)}) collective-permute-start(bf16[8,128,128]{2,1,0:T(8,128)(2,1)S(1)} %get-tuple-element.54), channel_id=1, source_target_pairs={{0,12},{4,8},{8,4},{12,0},{1,13},{5,9},{9,5},{13,1},{2,14},{6,10},... | collective-permute-start | bytes 786440 | tf_op jit(solution)/shard_map/ppermute | solution.py:406
  (55 other events, 905.3 us)

commit v4 on v3

--- a/solution.py
+++ b/solution.py
@@ -15,6 +15,7 @@
 LANES = 128
 WIDE = 2 * LANES
 DEPTH = 32
+PARTS = 1
 
 
 def spread(values, fields):
@@ -113,15 +114,16 @@
     return (v.astype(f32) + time_step * (diffusivity * curve - speed * slope + rate)).astype(bf16)
 
 
-def x_state_kernel(n, *refs):
-    far, outs, near, rest = refs[:8], refs[8 : 8 + n], refs[8 + n : 16 + n], refs[16 + n :]
+def x_state_kernel(n, part, *refs):
+    kept = n // 2
+    far, outs, near, rest = refs[:8], refs[8 : 9 + kept], refs[9 + kept : 17 + kept], refs[17 + kept :]
     rates, coef, advect, diffuse, state, d1, d2, filt = near
     filt_own, rates_high, rates_low, rate, middle, ready, sems, out_sems = rest
     me, half = lax.axis_index("pencil"), lax.axis_index("field")
     fields, _, rows, length = state.shape
     size = length // n
     sources = list(far)
-    sources[4] = far[4].at[:, :, aligned(half, rows), :]
+    sources[4] = far[4].at[:, :, aligned(PARTS * half + part, rows), :]
     copies = [pltpu.make_async_copy(sources[i], near[i], sems.at[i]) for i in range(8)]
     for copy in copies:
         copy.start()
@@ -152,15 +154,18 @@
             middle[at, across] = moved.astype(bf16)
     for r in range(n):
         filt_own[:, r * size : (r + 1) * size] = filt[:, aligned(me ^ r, size)]
-    sends = []
     for c in reversed(range(length // WIDE)):
         across = slice(c * WIDE, (c + 1) * WIDE)
         result = jnp.dot(middle[...], filt_own[:, across], preferred_element_type=f32).astype(bf16)
         for k in range(WIDE // size):
             r = c * (WIDE // size) + k
             ready[r] = result[:, k * size : (k + 1) * size].reshape(fields, rows, size)
-            sends.append(pltpu.make_async_copy(ready.at[r], outs[r], out_sems.at[r]))
-            sends[-1].start()
+        if c * (WIDE // size) == kept:
+            sends = [pltpu.make_async_copy(ready.at[pl.ds(kept, n - kept)], outs[kept], out_sems.at[kept])]
+            sends[0].start()
+    for r in range(kept):
+        sends.append(pltpu.make_async_copy(ready.at[r], outs[r], out_sems.at[r]))
+        sends[-1].start()
     for send in sends:
         send.wait()
 
@@ -199,7 +204,8 @@
 
 
 def y_kernel(n, q, params_here, rates, coef, advect, diffuse, *rest):
-    own, other, rest = rest[:n], rest[n : 2 * n], rest[2 * n :]
+    pieces = PARTS * n
+    own, other, rest = rest[:pieces], rest[pieces : 2 * pieces], rest[2 * pieces :]
     if q is not None:
         arrived, rest = rest[:n], rest[n:]
     d1t, d2t, filtt = rest[:3]
@@ -216,8 +222,10 @@
         filt_own[r * size : (r + 1) * size, :] = filtt[aligned(me ^ r, size), :]
         for s in range(count):
             across = slice(s * size, (s + 1) * size)
-            u_full[aligned(2 * (me ^ r) + half, rows), across] = own[r][s]
-            u_full[aligned(2 * (me ^ r) + 1 - half, rows), across] = other[r][s]
+            for part in range(PARTS):
+                here, there = PARTS * half + part, PARTS * (1 - half) + part
+                u_full[aligned(2 * PARTS * (me ^ r) + here, rows), across] = own[part * n + r][s]
+                u_full[aligned(2 * PARTS * (me ^ r) + there, rows), across] = other[part * n + r][s]
             if q is not None:
                 v_full[aligned(me ^ r, size), across] = arrived[r][s]
 
@@ -308,15 +316,18 @@
     return [pltpu.VMEM((fields * DEPTH, count * DEPTH), bf16)] * 2
 
 
-def x_state_call(n, scalars, state, d1, d2, filt):
+def x_state_call(n, part, scalars, state, d1, d2, filt):
     count, _, deep, length = state.shape
-    rows = deep // 2
+    rows = deep // (2 * PARTS)
+    kept = n // 2
+    block = (count, rows, length // n)
     square = pltpu.VMEM((length, length), bf16)
     return pl.pallas_call(
-        functools.partial(x_state_kernel, n),
-        out_shape=[jax.ShapeDtypeStruct((count, rows, length // n), bf16)] * n,
+        functools.partial(x_state_kernel, n, part),
+        out_shape=[jax.ShapeDtypeStruct(block, bf16)] * kept
+        + [jax.ShapeDtypeStruct((n - kept,) + block, bf16)],
         in_specs=[HBM] * 8,
-        out_specs=[HBM] * n,
+        out_specs=[HBM] * (kept + 1),
         scratch_shapes=[pltpu.SMEM(scalar.shape, f32) for scalar in scalars]
         + [pltpu.VMEM((count, 1, rows, length), bf16), square, square, square, square]
         + mixers(count, count)
@@ -325,10 +336,9 @@
             pltpu.VMEM((count * rows, length), bf16),
             pltpu.VMEM((n, count, rows, length // n), bf16),
             pltpu.SemaphoreType.DMA((8,)),
-            pltpu.SemaphoreType.DMA((n,)),
+            pltpu.SemaphoreType.DMA((kept + 1,)),
         ],
         cost_estimate=cost(6 * count * rows * length * length, 4 * count * rows * length),
-        name="x_state",
     )(*scalars, state, d1, d2, filt)
 
 
@@ -407,6 +417,17 @@
     return [slots[0]] + [arrived[r] for r in range(1, n)]
 
 
+def exchange_state(n, made):
+    kept = n // 2
+    landed = lax.ppermute(made[kept], "pencil", [(i, i ^ kept) for i in range(n)])
+    slots = [made[0]] + [None] * (kept - 1) + [landed[0]] + [None] * (kept - 1)
+    for r in range(1, kept):
+        pairs = [(i, i ^ r) for i in range(n)]
+        slots[r] = lax.ppermute(made[r], "pencil", pairs)
+        slots[kept + r] = lax.ppermute(landed[r], "pencil", pairs)
+    return slots
+
+
 def swap(slots):
     return [lax.ppermute(slot, "field", [(0, 1), (1, 0)]) for slot in slots]
 
@@ -415,12 +436,15 @@
     params = range(tangents.shape[0])
     scalars = (rates, coef, advect, diffuse)
 
+    def forth_state(part):
+        return x_state_call(n, part, scalars, state, d1, d2, filt)
+
     def forth(q):
-        if q is None:
-            return x_state_call(n, scalars, state, d1, d2, filt)
         return x_call(n, q, scalars, state, tangents, d1, d2, filt)
 
-    own = exchange(n, forth(None))
+    own = []
+    for part in range(PARTS):
+        own += exchange_state(n, forth_state(part))
     sent = [exchange(n, forth(q)) for q in params]
     turned = (d1.T, d2.T, filt.T)
     other = swap(own)
@@ -470,6 +494,7 @@
             and planes == mesh.shape["slab"]
             and n * LANES == length == state.shape[2]
             and length % WIDE == 0
+            and n == 2 * (WIDE // LANES)
         )
         local = functools.partial(pipelined, n) if fits else plain
         call = jax.shard_map(local, mesh=mesh, in_specs=in_specs, out_specs=out_specs, check_vma=False)

time: 215 us -> 214 us (level)
  starting transfers between devices: 77.7 us -> 68.8 us
  waiting for transfers between devices: 44.4 us -> 53.2 us
    ppermute x30 -> x27, starting transfers between devices: 76.6 us -> 61.9 us  [exchange(): lax.ppermute(slots[r], 'pencil', [(i, i ^ r) for i in range(n)])]
    ppermute x30 -> x27, waiting for transfers between devices: 44.4 us -> 51.9 us  [exchange(): lax.ppermute(slots[r], 'pencil', [(i, i ^ r) for i in range(n)])]
    ppermute x0 -> x3, starting transfers between devices: none -> 5.7 us  [the longest x1 4.12 us: exchange_state(): lax.ppermute(made[kept], 'pencil', [(i, i ^ kept) for i in range(n)])]
    unnamed x85 -> x63, local copies, waits for them, and re-layouts: 14.9 us -> 14 us
  transfers between devices with their start and end apart: 38 -> 38, of which waited for: 4 -> 8; matrix products, arithmetic and copies ran while one was open for 1% -> 1% of each run, Pallas kernels for 33% -> 33%
where the time goes in v4:
time: 214 us
  Pallas kernels  76.3 us (36%)
  starting transfers between devices  68.8 us (32%)
  waiting for transfers between devices  53.2 us (25%)
  local copies, waits for them, and re-layouts  14 us (7%)
    ppermute x27, starting transfers between devices, exchange(): lax.ppermute(slots[r], 'pencil', [(i, i ^ r) for i in range(n)])  61.9 us
    ppermute x27, waiting for transfers between devices, exchange(): lax.ppermute(slots[r], 'pencil', [(i, i ^ r) for i in range(n)])  51.9 us
    pallas_call x5, Pallas kernels, y_call(): pl.pallas_call(functools.partial(y_kernel, n, q, params_here), out_shape=...  40.6 us
    pallas_call x4, Pallas kernels, x_call(): pl.pallas_call(functools.partial(x_kernel, n, q, params_here), grid=(deep...  26.2 us
    unnamed x63, local copies, waits for them, and re-layouts  14 us
    pallas_call x5, Pallas kernels, place_tangent(): pl.pallas_call(functools.partial(place_kernel, n, q, some), out_shape=jax...  4.66 us
  transfers between devices with their start and end apart: 38, of which 8 were waited for; matrix products, arithmetic and copies ran while one was open for 1% of the time, Pallas kernels for 33%

profile of v4, /device:TPU:0, one launch (start us, length us, event | category | flops | bytes accessed | tf_op | source)
XLA Modules:
  0.0 213.5 jit_solution(18395523670413426739)
XLA Ops:
  0.6 3.9 %shard_map.104 = (bf16[8,64,128]{2,1,0:T(8,128)(2,1)}, bf16[8,64,128]{2,1,0:T(8,128)(2,1)}, bf16[2,8,64,128]{3,2,1,0:T(8,128)(2,1)}) custom-call(f32[8,8]{1,0:T(8,128)} %rates.17, f32[8,8]{1,0:T(8,128)} %coef.17, f32[2,8]{1,0:T(2,128)} %advect.17, f32[8]{0:T(128)} %diffuse.17, bf16[8,1,128,512]{3,2,1,0:T(8,128)(2,1)} %state.7, bf16[512,512]{1,0:T(8,128)(2,1)} %d1.7, ...), custom_call_target="tpu_custom_call" | custom-call | flops 805306368 | bytes 1048576 | tf_op jit(solution)/shard_map/pallas_call | solution.py:325
  4.5 4.1 %collective-permute-start.1 = (bf16[2,8,64,128]{3,2,1,0:T(8,128)(2,1)}, bf16[2,8,64,128]{3,2,1,0:T(8,128)(2,1)S(1)}, u32[]{:S(2)}, u32[]{:S(2)}) collective-permute-start(bf16[2,8,64,128]{3,2,1,0:T(8,128)(2,1)} %get-tuple-element.43), channel_id=1, source_target_pairs={{0,8},{4,12},{8,0},{12,4},{1,9},{5,13},{9,1},{13,5},{2,10},{6,14},... | collective-permute-start | bytes 786440 | tf_op jit(solution)/shard_map/ppermute | solution.py:422
  10.2 6.6 %shard_map.112 = (bf16[8,128,128]{2,1,0:T(8,128)(2,1)}, bf16[8,128,128]{2,1,0:T(8,128)(2,1)}, bf16[8,128,128]{2,1,0:T(8,128)(2,1)}, bf16[8,128,128]{2,1,0:T(8,128)(2,1)}) custom-call(f32[8,8]{1,0:T(8,128)} %rates.17, f32[8,8]{1,0:T(8,128)} %coef.17, f32[2,8]{1,0:T(2,128)} %advect.17, f32[8]{0:T(128)} %diffuse.17, bf16[8,1,128,512]{3,2,1,0:T(8,128)(2,1)} %state.7, ...), custom_call_target="tpu_custom_call" | custom-call | flops 1610612736 | bytes 2097152 | tf_op jit(solution)/shard_map/pallas_call | solution.py:349
  17.4 6.5 %shard_map.110 = (bf16[8,128,128]{2,1,0:T(8,128)(2,1)}, bf16[8,128,128]{2,1,0:T(8,128)(2,1)}, bf16[8,128,128]{2,1,0:T(8,128)(2,1)}, bf16[8,128,128]{2,1,0:T(8,128)(2,1)}) custom-call(f32[8,8]{1,0:T(8,128)} %rates.17, f32[8,8]{1,0:T(8,128)} %coef.17, f32[2,8]{1,0:T(2,128)} %advect.17, f32[8]{0:T(128)} %diffuse.17, bf16[8,1,128,512]{3,2,1,0:T(8,128)(2,1)} %state.7, ...), custom_call_target="tpu_custom_call" | custom-call | flops 1610612736 | bytes 2097152 | tf_op jit(solution)/shard_map/pallas_call | solution.py:349
  23.9 3.9 %collective-permute-start.34 = (bf16[8,128,128]{2,1,0:T(8,128)(2,1)S(1)}, bf16[8,128,128]{2,1,0:T(8,128)(2,1)S(1)}, u32[]{:S(2)}, u32[]{:S(2)}) collective-permute-start(bf16[8,128,128]{2,1,0:T(8,128)(2,1)S(1)} %copy-done.29), channel_id=1, source_target_pairs={{0,12},{4,8},{8,4},{12,0},{1,13},{5,9},{9,5},{13,1},{2,14},{6,10},... | collective-permute-start | bytes 786440 | tf_op jit(solution)/shard_map/ppermute | solution.py:416
  30.8 6.6 %shard_map.108 = (bf16[8,128,128]{2,1,0:T(8,128)(2,1)}, bf16[8,128,128]{2,1,0:T(8,128)(2,1)}, bf16[8,128,128]{2,1,0:T(8,128)(2,1)}, bf16[8,128,128]{2,1,0:T(8,128)(2,1)}) custom-call(f32[8,8]{1,0:T(8,128)} %rates.17, f32[8,8]{1,0:T(8,128)} %coef.17, f32[2,8]{1,0:T(2,128)} %advect.17, f32[8]{0:T(128)} %diffuse.17, bf16[8,1,128,512]{3,2,1,0:T(8,128)(2,1)} %state.7, ...), custom_call_target="tpu_custom_call" | custom-call | flops 1610612736 | bytes 2097152 | tf_op jit(solution)/shard_map/pallas_call | solution.py:349
  39.6 2.5 %collective-permute-start.28 = (bf16[8,128,128]{2,1,0:T(8,128)(2,1)}, bf16[8,128,128]{2,1,0:T(8,128)(2,1)S(1)}, u32[]{:S(2)}, u32[]{:S(2)}) collective-permute-start(bf16[8,128,128]{2,1,0:T(8,128)(2,1)} %get-tuple-element.67), channel_id=1, source_target_pairs={{0,12},{4,8},{8,4},{12,0},{1,13},{5,9},{9,5},{13,1},{2,14},{6,10},... | collective-permute-start | bytes 786440 | tf_op jit(solution)/shard_map/ppermute | solution.py:416
  42.7 8.6 %collective-permute-start.20 = (bf16[8,128,128]{2,1,0:T(8,128)(2,1)}, bf16[8,128,128]{2,1,0:T(8,128)(2,1)S(1)}, u32[]{:S(2)}, u32[]{:S(2)}) collective-permute-start(bf16[8,128,128]{2,1,0:T(8,128)(2,1)} %get-tuple-element.57), channel_id=1, source_target_pairs={{0,4},{4,0},{8,12},{12,8},{1,5},{5,1},{9,13},{13,9},{2,6},{6,2},{1... | collective-permute-start | bytes 786440 | tf_op jit(solution)/shard_map/ppermute | solution.py:416
  52.4 9.0 %collective-permute-done.27.rest_10_ = bf16[8,128,128]{2,1,0:T(8,128)(2,1)S(1)} collective-permute-done((bf16[8,128,128]{2,1,0:T(8,128)(2,1)}, bf16[8,128,128]{2,1,0:T(8,128)(2,1)S(1)}, u32[]{:S(2)}, u32[]{:S(2)}) %collective-permute-start.27) | collective-permute-done | bytes 262176 | tf_op jit(solution)/shard_map/ppermute | solution.py:416
  62.0 6.5 %shard_map.106 = (bf16[8,128,128]{2,1,0:T(8,128)(2,1)}, bf16[8,128,128]{2,1,0:T(8,128)(2,1)}, bf16[8,128,128]{2,1,0:T(8,128)(2,1)}, bf16[8,128,128]{2,1,0:T(8,128)(2,1)}) custom-call(f32[8,8]{1,0:T(8,128)} %rates.17, f32[8,8]{1,0:T(8,128)} %coef.17, f32[2,8]{1,0:T(2,128)} %advect.17, f32[8]{0:T(128)} %diffuse.17, bf16[8,1,128,512]{3,2,1,0:T(8,128)(2,1)} %state.7, ...), custom_call_target="tpu_custom_call" | custom-call | flops 1610612736 | bytes 2097152 | tf_op jit(solution)/shard_map/pallas_call | solution.py:349
  69.2 2.5 %collective-permute-start.22 = (bf16[8,128,128]{2,1,0:T(8,128)(2,1)}, bf16[8,128,128]{2,1,0:T(8,128)(2,1)}, u32[]{:S(2)}, u32[]{:S(2)}) collective-permute-start(bf16[8,128,128]{2,1,0:T(8,128)(2,1)} %get-tuple-element.59), channel_id=1, source_target_pairs={{0,12},{4,8},{8,4},{12,0},{1,13},{5,9},{9,5},{13,1},{2,14},{6,10},... | collective-permute-start | bytes 786440 | tf_op jit(solution)/shard_map/ppermute | solution.py:416
  71.7 3.8 %collective-permute-start.14 = (bf16[8,128,128]{2,1,0:T(8,128)(2,1)}, bf16[8,128,128]{2,1,0:T(8,128)(2,1)S(1)}, u32[]{:S(2)}, u32[]{:S(2)}) collective-permute-start(bf16[8,128,128]{2,1,0:T(8,128)(2,1)} %get-tuple-element.49), channel_id=1, source_target_pairs={{0,4},{4,0},{8,12},{12,8},{1,5},{5,1},{9,13},{13,9},{2,6},{6,2},{1... | collective-permute-start | bytes 786440 | tf_op jit(solution)/shard_map/ppermute | solution.py:416
  89.1 8.7 %shard_map.113 = (bf16[8,128,128]{2,1,0:T(8,128)(2,1)S(1)}, bf16[8,128,128]{2,1,0:T(8,128)(2,1)S(1)}, bf16[8,128,128]{2,1,0:T(8,128)(2,1)S(1)}, bf16[8,128,128]{2,1,0:T(8,128)(2,1)S(1)}) custom-call(f32[8,8]{1,0:T(8,128)S(1)} %copy-done, f32[8,8]{1,0:T(8,128)S(1)} %copy-done.1, f32[2,8]{1,0:T(2,128)S(1)} %copy-done.2, f32[8]{0:T(128)S(1)} %copy-done.3, ...), custom_call_target="tpu_custom_call" | custom-call | flops 1610612736 | bytes 2097152 | tf_op jit(solution)/shard_map/pallas_call | solution.py:373
  99.1 5.0 %shard_map.105 = (bf16[4,128,128]{2,1,0:T(8,128)(2,1)S(1)}, bf16[4,128,128]{2,1,0:T(8,128)(2,1)S(1)}, bf16[4,128,128]{2,1,0:T(8,128)(2,1)S(1)}, bf16[4,128,128]{2,1,0:T(8,128)(2,1)S(1)}) custom-call(f32[8,8]{1,0:T(8,128)S(1)} %copy-done, f32[8,8]{1,0:T(8,128)S(1)} %copy-done.1, f32[2,8]{1,0:T(2,128)S(1)} %copy-done.2, f32[8]{0:T(128)S(1)} %copy-done.3, ...), custom_call_target="tpu_custom_call" | custom-call | flops 805306368 | bytes 1048576 | tf_op jit(solution)/shard_map/pallas_call | solution.py:373
  108.0 5.1 %collective-permute-start.9 = (bf16[4,128,128]{2,1,0:T(8,128)(2,1)S(1)}, bf16[4,128,128]{2,1,0:T(8,128)(2,1)S(1)}, u32[]{:S(2)}, u32[]{:S(2)}) collective-permute-start(bf16[4,128,128]{2,1,0:T(8,128)(2,1)S(1)} %get-tuple-element.47), channel_id=1, source_target_pairs={{0,12},{4,8},{8,4},{12,0},{1,13},{5,9},{9,5},{13,1},{2,14},{6,10},... | collective-permute-start | bytes 393224 | tf_op jit(solution)/shard_map/ppermute | solution.py:416
  113.1 8.7 %shard_map.111 = (bf16[8,128,128]{2,1,0:T(8,128)(2,1)S(1)}, bf16[8,128,128]{2,1,0:T(8,128)(2,1)S(1)}, bf16[8,128,128]{2,1,0:T(8,128)(2,1)S(1)}, bf16[8,128,128]{2,1,0:T(8,128)(2,1)S(1)}) custom-call(f32[8,8]{1,0:T(8,128)S(1)} %copy-done, f32[8,8]{1,0:T(8,128)S(1)} %copy-done.1, f32[2,8]{1,0:T(2,128)S(1)} %copy-done.2, f32[8]{0:T(128)S(1)} %copy-done.3, ...), custom_call_target="tpu_custom_call" | custom-call | flops 1610612736 | bytes 2097152 | tf_op jit(solution)/shard_map/pallas_call | solution.py:373
  121.9 15.4 %collective-permute-done.8.rest_2_ = bf16[4,128,128]{2,1,0:T(8,128)(2,1)S(1)} collective-permute-done((bf16[4,128,128]{2,1,0:T(8,128)(2,1)S(1)}, bf16[4,128,128]{2,1,0:T(8,128)(2,1)S(1)}, u32[]{:S(2)}, u32[]{:S(2)}) %collective-permute-start.8) | collective-permute-done | bytes 131104 | tf_op jit(solution)/shard_map/ppermute | solution.py:416
  137.3 4.4 %collective-permute-start.30 = (bf16[8,128,128]{2,1,0:T(8,128)(2,1)S(1)}, bf16[8,128,128]{2,1,0:T(8,128)(2,1)S(1)}, u32[]{:S(2)}, u32[]{:S(2)}) collective-permute-start(bf16[8,128,128]{2,1,0:T(8,128)(2,1)S(1)} %get-tuple-element.70), channel_id=1, source_target_pairs={{0,8},{4,12},{8,0},{12,4},{1,9},{5,13},{9,1},{13,5},{2,10},{6,14},... | collective-permute-start | bytes 786440 | tf_op jit(solution)/shard_map/ppermute | solution.py:416
  143.1 9.1 %shard_map.109 = (bf16[8,128,128]{2,1,0:T(8,128)(2,1)S(1)}, bf16[8,128,128]{2,1,0:T(8,128)(2,1)S(1)}, bf16[8,128,128]{2,1,0:T(8,128)(2,1)S(1)}, bf16[8,128,128]{2,1,0:T(8,128)(2,1)S(1)}) custom-call(f32[8,8]{1,0:T(8,128)S(1)} %copy-done, f32[8,8]{1,0:T(8,128)S(1)} %copy-done.1, f32[2,8]{1,0:T(2,128)S(1)} %copy-done.2, f32[8]{0:T(128)S(1)} %copy-done.3, ...), custom_call_target="tpu_custom_call" | custom-call | flops 1610612736 | bytes 2097152 | tf_op jit(solution)/shard_map/pallas_call | solution.py:373
  152.3 9.1 %shard_map.107 = (bf16[8,128,128]{2,1,0:T(8,128)(2,1)S(1)}, bf16[8,128,128]{2,1,0:T(8,128)(2,1)S(1)}, bf16[8,128,128]{2,1,0:T(8,128)(2,1)S(1)}, bf16[8,128,128]{2,1,0:T(8,128)(2,1)S(1)}) custom-call(f32[8,8]{1,0:T(8,128)S(1)} %copy-done, f32[8,8]{1,0:T(8,128)S(1)} %copy-done.1, f32[2,8]{1,0:T(2,128)S(1)} %copy-done.2, f32[8]{0:T(128)S(1)} %copy-done.3, ...), custom_call_target="tpu_custom_call" | custom-call | flops 1610612736 | bytes 2097152 | tf_op jit(solution)/shard_map/pallas_call | solution.py:373
  161.4 3.1 %collective-permute-start.24 = (bf16[8,128,128]{2,1,0:T(8,128)(2,1)S(1)}, bf16[8,128,128]{2,1,0:T(8,128)(2,1)S(1)}, u32[]{:S(2)}, u32[]{:S(2)}) collective-permute-start(bf16[8,128,128]{2,1,0:T(8,128)(2,1)S(1)} %get-tuple-element.62), channel_id=1, source_target_pairs={{0,8},{4,12},{8,0},{12,4},{1,9},{5,13},{9,1},{13,5},{2,10},{6,14},... | collective-permute-start | bytes 786440 | tf_op jit(solution)/shard_map/ppermute | solution.py:416
  165.8 15.2 %collective-permute-start.19 = (bf16[8,128,128]{2,1,0:T(8,128)(2,1)S(1)}, bf16[8,128,128]{2,1,0:T(8,128)(2,1)S(1)}, u32[]{:S(2)}, u32[]{:S(2)}) collective-permute-start(bf16[8,128,128]{2,1,0:T(8,128)(2,1)S(1)} %get-tuple-element.55), channel_id=1, source_target_pairs={{0,8},{4,12},{8,0},{12,4},{1,9},{5,13},{9,1},{13,5},{2,10},{6,14},... | collective-permute-start | bytes 786440 | tf_op jit(solution)/shard_map/ppermute | solution.py:416
  182.4 13.9 %collective-permute-done.24.rest_2_ = bf16[8,128,128]{2,1,0:T(8,128)(2,1)S(1)} collective-permute-done((bf16[8,128,128]{2,1,0:T(8,128)(2,1)S(1)}, bf16[8,128,128]{2,1,0:T(8,128)(2,1)S(1)}, u32[]{:S(2)}, u32[]{:S(2)}) %collective-permute-start.24) | collective-permute-done | bytes 262176 | tf_op jit(solution)/shard_map/ppermute | solution.py:416
  196.9 10.6 %collective-permute-done.19.rest_2_ = bf16[8,128,128]{2,1,0:T(8,128)(2,1)S(1)} collective-permute-done((bf16[8,128,128]{2,1,0:T(8,128)(2,1)S(1)}, bf16[8,128,128]{2,1,0:T(8,128)(2,1)S(1)}, u32[]{:S(2)}, u32[]{:S(2)}) %collective-permute-start.19) | collective-permute-done | bytes 262176 | tf_op jit(solution)/shard_map/ppermute | solution.py:416
  (132 shorter events, 39.6 us)
Async XLA Ops:
  27.9 23.5 %collective-permute-start.26 = (bf16[8,128,128]{2,1,0:T(8,128)(2,1)}, bf16[8,128,128]{2,1,0:T(8,128)(2,1)S(1)}, u32[]{:S(2)}, u32[]{:S(2)}) collective-permute-start(bf16[8,128,128]{2,1,0:T(8,128)(2,1)} %get-tuple-element.65), channel_id=1, source_target_pairs={{0,4},{4,0},{8,12},{12,8},{1,5},{5,1},{9,13},{13,9},{2,6},{6,2},{1... | collective-permute-start | bytes 786440 | tf_op jit(solution)/shard_map/ppermute | solution.py:416
  29.9 31.5 %collective-permute-start.27 = (bf16[8,128,128]{2,1,0:T(8,128)(2,1)}, bf16[8,128,128]{2,1,0:T(8,128)(2,1)S(1)}, u32[]{:S(2)}, u32[]{:S(2)}) collective-permute-start(bf16[8,128,128]{2,1,0:T(8,128)(2,1)} %get-tuple-element.66), channel_id=1, source_target_pairs={{0,8},{4,12},{8,0},{12,4},{1,9},{5,13},{9,1},{13,5},{2,10},{6,14},... | collective-permute-start | bytes 786440 | tf_op jit(solution)/shard_map/ppermute | solution.py:416
  30.8 30.7 %collective-permute-start.2 = (bf16[8,64,128]{2,1,0:T(8,128)(2,1)S(1)}, bf16[8,64,128]{2,1,0:T(8,128)(2,1)S(1)}, u32[]{:S(2)}, u32[]{:S(2)}) collective-permute-start(bf16[8,64,128]{2,1,0:T(8,128)(2,1)S(1)} %get-tuple-element.80), channel_id=1, source_target_pairs={{0,4},{4,0},{8,12},{12,8},{1,5},{5,1},{9,13},{13,9},{2,6},{6,2},{1... | collective-permute-start | bytes 393224 | tf_op jit(solution)/shard_map/ppermute | solution.py:427
  39.6 28.9 %collective-permute-start.28 = (bf16[8,128,128]{2,1,0:T(8,128)(2,1)}, bf16[8,128,128]{2,1,0:T(8,128)(2,1)S(1)}, u32[]{:S(2)}, u32[]{:S(2)}) collective-permute-start(bf16[8,128,128]{2,1,0:T(8,128)(2,1)} %get-tuple-element.67), channel_id=1, source_target_pairs={{0,12},{4,8},{8,4},{12,0},{1,13},{5,9},{9,5},{13,1},{2,14},{6,10},... | collective-permute-start | bytes 786440 | tf_op jit(solution)/shard_map/ppermute | solution.py:416
  42.7 28.9 %collective-permute-start.20 = (bf16[8,128,128]{2,1,0:T(8,128)(2,1)}, bf16[8,128,128]{2,1,0:T(8,128)(2,1)S(1)}, u32[]{:S(2)}, u32[]{:S(2)}) collective-permute-start(bf16[8,128,128]{2,1,0:T(8,128)(2,1)} %get-tuple-element.57), channel_id=1, source_target_pairs={{0,4},{4,0},{8,12},{12,8},{1,5},{5,1},{9,13},{13,9},{2,6},{6,2},{1... | collective-permute-start | bytes 786440 | tf_op jit(solution)/shard_map/ppermute | solution.py:416
  51.4 46.5 %collective-permute-start.21 = (bf16[8,128,128]{2,1,0:T(8,128)(2,1)}, bf16[8,128,128]{2,1,0:T(8,128)(2,1)S(1)}, u32[]{:S(2)}, u32[]{:S(2)}) collective-permute-start(bf16[8,128,128]{2,1,0:T(8,128)(2,1)} %get-tuple-element.58), channel_id=1, source_target_pairs={{0,8},{4,12},{8,0},{12,4},{1,9},{5,13},{9,1},{13,5},{2,10},{6,14},... | collective-permute-start | bytes 786440 | tf_op jit(solution)/shard_map/ppermute | solution.py:416
  69.2 34.9 %collective-permute-start.22 = (bf16[8,128,128]{2,1,0:T(8,128)(2,1)}, bf16[8,128,128]{2,1,0:T(8,128)(2,1)}, u32[]{:S(2)}, u32[]{:S(2)}) collective-permute-start(bf16[8,128,128]{2,1,0:T(8,128)(2,1)} %get-tuple-element.59), channel_id=1, source_target_pairs={{0,12},{4,8},{8,4},{12,0},{1,13},{5,9},{9,5},{13,1},{2,14},{6,10},... | collective-permute-start | bytes 786440 | tf_op jit(solution)/shard_map/ppermute | solution.py:416
  71.7 33.4 %collective-permute-start.14 = (bf16[8,128,128]{2,1,0:T(8,128)(2,1)}, bf16[8,128,128]{2,1,0:T(8,128)(2,1)S(1)}, u32[]{:S(2)}, u32[]{:S(2)}) collective-permute-start(bf16[8,128,128]{2,1,0:T(8,128)(2,1)} %get-tuple-element.49), channel_id=1, source_target_pairs={{0,4},{4,0},{8,12},{12,8},{1,5},{5,1},{9,13},{13,9},{2,6},{6,2},{1... | collective-permute-start | bytes 786440 | tf_op jit(solution)/shard_map/ppermute | solution.py:416
  76.1 30.4 %collective-permute-start.15 = (bf16[8,128,128]{2,1,0:T(8,128)(2,1)}, bf16[8,128,128]{2,1,0:T(8,128)(2,1)}, u32[]{:S(2)}, u32[]{:S(2)}) collective-permute-start(bf16[8,128,128]{2,1,0:T(8,128)(2,1)} %get-tuple-element.50), channel_id=1, source_target_pairs={{0,8},{4,12},{8,0},{12,4},{1,9},{5,13},{9,1},{13,5},{2,10},{6,14},... | collective-permute-start | bytes 786440 | tf_op jit(solution)/shard_map/ppermute | solution.py:416
  76.8 31.2 %collective-permute-start.16 = (bf16[8,128,128]{2,1,0:T(8,128)(2,1)}, bf16[8,128,128]{2,1,0:T(8,128)(2,1)}, u32[]{:S(2)}, u32[]{:S(2)}) collective-permute-start(bf16[8,128,128]{2,1,0:T(8,128)(2,1)} %get-tuple-element.51), channel_id=1, source_target_pairs={{0,12},{4,8},{8,4},{12,0},{1,13},{5,9},{9,5},{13,1},{2,14},{6,10},... | collective-permute-start | bytes 786440 | tf_op jit(solution)/shard_map/ppermute | solution.py:416
  97.9 43.8 %collective-permute-start.35 = (bf16[8,128,128]{2,1,0:T(8,128)(2,1)S(1)}, bf16[8,128,128]{2,1,0:T(8,128)(2,1)S(1)}, u32[]{:S(2)}, u32[]{:S(2)}) collective-permute-start(bf16[8,128,128]{2,1,0:T(8,128)(2,1)S(1)} %get-tuple-element.77), channel_id=1, source_target_pairs={{0,4},{4,0},{8,12},{12,8},{1,5},{5,1},{9,13},{13,9},{2,6},{6,2},{1... | collective-permute-start | bytes 786440 | tf_op jit(solution)/shard_map/ppermute | solution.py:416
  104.1 48.1 %collective-permute-start.36 = (bf16[8,128,128]{2,1,0:T(8,128)(2,1)S(1)}, bf16[8,128,128]{2,1,0:T(8,128)(2,1)S(1)}, u32[]{:S(2)}, u32[]{:S(2)}) collective-permute-start(bf16[8,128,128]{2,1,0:T(8,128)(2,1)S(1)} %get-tuple-element.78), channel_id=1, source_target_pairs={{0,8},{4,12},{8,0},{12,4},{1,9},{5,13},{9,1},{13,5},{2,10},{6,14},... | collective-permute-start | bytes 786440 | tf_op jit(solution)/shard_map/ppermute | solution.py:416
  106.5 30.8 %collective-permute-start.8 = (bf16[4,128,128]{2,1,0:T(8,128)(2,1)S(1)}, bf16[4,128,128]{2,1,0:T(8,128)(2,1)S(1)}, u32[]{:S(2)}, u32[]{:S(2)}) collective-permute-start(bf16[4,128,128]{2,1,0:T(8,128)(2,1)S(1)} %get-tuple-element.46), channel_id=1, source_target_pairs={{0,8},{4,12},{8,0},{12,4},{1,9},{5,13},{9,1},{13,5},{2,10},{6,14},... | collective-permute-start | bytes 393224 | tf_op jit(solution)/shard_map/ppermute | solution.py:416
  108.0 29.3 %collective-permute-start.9 = (bf16[4,128,128]{2,1,0:T(8,128)(2,1)S(1)}, bf16[4,128,128]{2,1,0:T(8,128)(2,1)S(1)}, u32[]{:S(2)}, u32[]{:S(2)}) collective-permute-start(bf16[4,128,128]{2,1,0:T(8,128)(2,1)S(1)} %get-tuple-element.47), channel_id=1, source_target_pairs={{0,12},{4,8},{8,4},{12,0},{1,13},{5,9},{9,5},{13,1},{2,14},{6,10},... | collective-permute-start | bytes 393224 | tf_op jit(solution)/shard_map/ppermute | solution.py:416
  121.8 39.6 %collective-permute-start.37 = (bf16[8,128,128]{2,1,0:T(8,128)(2,1)S(1)}, bf16[8,128,128]{2,1,0:T(8,128)(2,1)S(1)}, u32[]{:S(2)}, u32[]{:S(2)}) collective-permute-start(bf16[8,128,128]{2,1,0:T(8,128)(2,1)S(1)} %get-tuple-element.79), channel_id=1, source_target_pairs={{0,12},{4,8},{8,4},{12,0},{1,13},{5,9},{9,5},{13,1},{2,14},{6,10},... | collective-permute-start | bytes 786440 | tf_op jit(solution)/shard_map/ppermute | solution.py:416
  137.3 27.1 %collective-permute-start.29 = (bf16[8,128,128]{2,1,0:T(8,128)(2,1)S(1)}, bf16[8,128,128]{2,1,0:T(8,128)(2,1)S(1)}, u32[]{:S(2)}, u32[]{:S(2)}) collective-permute-start(bf16[8,128,128]{2,1,0:T(8,128)(2,1)S(1)} %get-tuple-element.69), channel_id=1, source_target_pairs={{0,4},{4,0},{8,12},{12,8},{1,5},{5,1},{9,13},{13,9},{2,6},{6,2},{1... | collective-permute-start | bytes 786440 | tf_op jit(solution)/shard_map/ppermute | solution.py:416
  137.3 28.5 %collective-permute-start.30 = (bf16[8,128,128]{2,1,0:T(8,128)(2,1)S(1)}, bf16[8,128,128]{2,1,0:T(8,128)(2,1)S(1)}, u32[]{:S(2)}, u32[]{:S(2)}) collective-permute-start(bf16[8,128,128]{2,1,0:T(8,128)(2,1)S(1)} %get-tuple-element.70), channel_id=1, source_target_pairs={{0,8},{4,12},{8,0},{12,4},{1,9},{5,13},{9,1},{13,5},{2,10},{6,14},... | collective-permute-start | bytes 786440 | tf_op jit(solution)/shard_map/ppermute | solution.py:416
  141.7 24.1 %collective-permute-start.31 = (bf16[8,128,128]{2,1,0:T(8,128)(2,1)S(1)}, bf16[8,128,128]{2,1,0:T(8,128)(2,1)S(1)}, u32[]{:S(2)}, u32[]{:S(2)}) collective-permute-start(bf16[8,128,128]{2,1,0:T(8,128)(2,1)S(1)} %get-tuple-element.71), channel_id=1, source_target_pairs={{0,12},{4,8},{8,4},{12,0},{1,13},{5,9},{9,5},{13,1},{2,14},{6,10},... | collective-permute-start | bytes 786440 | tf_op jit(solution)/shard_map/ppermute | solution.py:416
  152.2 28.8 %collective-permute-start.23 = (bf16[8,128,128]{2,1,0:T(8,128)(2,1)S(1)}, bf16[8,128,128]{2,1,0:T(8,128)(2,1)S(1)}, u32[]{:S(2)}, u32[]{:S(2)}) collective-permute-start(bf16[8,128,128]{2,1,0:T(8,128)(2,1)S(1)} %get-tuple-element.61), channel_id=1, source_target_pairs={{0,4},{4,0},{8,12},{12,8},{1,5},{5,1},{9,13},{13,9},{2,6},{6,2},{1... | collective-permute-start | bytes 786440 | tf_op jit(solution)/shard_map/ppermute | solution.py:416
  161.4 35.0 %collective-permute-start.24 = (bf16[8,128,128]{2,1,0:T(8,128)(2,1)S(1)}, bf16[8,128,128]{2,1,0:T(8,128)(2,1)S(1)}, u32[]{:S(2)}, u32[]{:S(2)}) collective-permute-start(bf16[8,128,128]{2,1,0:T(8,128)(2,1)S(1)} %get-tuple-element.62), channel_id=1, source_target_pairs={{0,8},{4,12},{8,0},{12,4},{1,9},{5,13},{9,1},{13,5},{2,10},{6,14},... | collective-permute-start | bytes 786440 | tf_op jit(solution)/shard_map/ppermute | solution.py:416
  164.4 31.9 %collective-permute-start.25 = (bf16[8,128,128]{2,1,0:T(8,128)(2,1)S(1)}, bf16[8,128,128]{2,1,0:T(8,128)(2,1)S(1)}, u32[]{:S(2)}, u32[]{:S(2)}) collective-permute-start(bf16[8,128,128]{2,1,0:T(8,128)(2,1)S(1)} %get-tuple-element.63), channel_id=1, source_target_pairs={{0,12},{4,8},{8,4},{12,0},{1,13},{5,9},{9,5},{13,1},{2,14},{6,10},... | collective-permute-start | bytes 786440 | tf_op jit(solution)/shard_map/ppermute | solution.py:416
  165.8 31.1 %collective-permute-start.18 = (bf16[8,128,128]{2,1,0:T(8,128)(2,1)S(1)}, bf16[8,128,128]{2,1,0:T(8,128)(2,1)S(1)}, u32[]{:S(2)}, u32[]{:S(2)}) collective-permute-start(bf16[8,128,128]{2,1,0:T(8,128)(2,1)S(1)} %get-tuple-element.54), channel_id=1, source_target_pairs={{0,4},{4,0},{8,12},{12,8},{1,5},{5,1},{9,13},{13,9},{2,6},{6,2},{1... | collective-permute-start | bytes 786440 | tf_op jit(solution)/shard_map/ppermute | solution.py:416
  165.8 41.8 %collective-permute-start.19 = (bf16[8,128,128]{2,1,0:T(8,128)(2,1)S(1)}, bf16[8,128,128]{2,1,0:T(8,128)(2,1)S(1)}, u32[]{:S(2)}, u32[]{:S(2)}) collective-permute-start(bf16[8,128,128]{2,1,0:T(8,128)(2,1)S(1)} %get-tuple-element.55), channel_id=1, source_target_pairs={{0,8},{4,12},{8,0},{12,4},{1,9},{5,13},{9,1},{13,5},{2,10},{6,14},... | collective-permute-start | bytes 786440 | tf_op jit(solution)/shard_map/ppermute | solution.py:416
  181.0 30.5 %collective-permute-start.17 = (bf16[8,128,128]{2,1,0:T(8,128)(2,1)S(1)}, bf16[8,128,128]{2,1,0:T(8,128)(2,1)S(1)}, u32[]{:S(2)}, u32[]{:S(2)}) collective-permute-start(bf16[8,128,128]{2,1,0:T(8,128)(2,1)S(1)} %get-tuple-element.52), channel_id=1, source_target_pairs={{0,12},{4,8},{8,4},{12,0},{1,13},{5,9},{9,5},{13,1},{2,14},{6,10},... | collective-permute-start | bytes 786440 | tf_op jit(solution)/shard_map/ppermute | solution.py:416
  (44 other events, 580.6 us)

commit v5 on v4

--- a/solution.py
+++ b/solution.py
@@ -130,7 +130,8 @@
     for copy in copies[:4]:
         copy.wait()
     fill_mixer(lambda a, b: rates[a, b], rates_high, rates_low)
-    copies[4].wait()
+    for copy in copies[4:]:
+        copy.wait()
     own = state[:, 0].reshape(fields * rows, length)
     for c in range(length // WIDE):
         across = slice(c * WIDE, (c + 1) * WIDE)
@@ -140,9 +141,6 @@
             for s in range(fields):
                 at = slice(s * rows + j * DEPTH, s * rows + (j + 1) * DEPTH)
                 rate[at, across] = weighted(coef, s, activity)
-        if c == 0:
-            for copy in copies[5:]:
-                copy.wait()
         slope = jnp.dot(own, d1[:, across], preferred_element_type=f32)
         for s in range(fields):
             at = slice(s * rows, (s + 1) * rows)
@@ -419,12 +417,12 @@
 
 def exchange_state(n, made):
     kept = n // 2
-    landed = lax.ppermute(made[kept], "pencil", [(i, i ^ kept) for i in range(n)])
-    slots = [made[0]] + [None] * (kept - 1) + [landed[0]] + [None] * (kept - 1)
+    landed = lax.ppermute(made[kept], "pencil", [(i, i ^ (n - 1)) for i in range(n)])
+    slots = list(made[:kept]) + [None] * (kept - 1) + [landed[kept - 1]]
     for r in range(1, kept):
         pairs = [(i, i ^ r) for i in range(n)]
         slots[r] = lax.ppermute(made[r], "pencil", pairs)
-        slots[kept + r] = lax.ppermute(landed[r], "pencil", pairs)
+        slots[n - 1 - r] = lax.ppermute(landed[kept - 1 - r], "pencil", pairs)
     return slots
 
 

time: 214 us -> 215 us (level)
    ppermute x2, starting transfers between devices: 4.12 us -> 6.37 us  [the longest x1 5.14 us: exchange_state(): lax.ppermute(made[kept], 'pencil', [(i, i ^ n - 1) for i in range(n)])]
  transfers between devices with their start and end apart: 38 -> 38, of which waited for: 8 -> 6; matrix products, arithmetic and copies ran while one was open for 1% -> 1% of each run, Pallas kernels for 33% -> 33%
where the time goes in v5:
time: 215 us
  Pallas kernels  76.4 us (36%)
  starting transfers between devices  70.8 us (33%)
  waiting for transfers between devices  52.1 us (24%)
  local copies, waits for them, and re-layouts  14 us (7%)
    ppermute x27, starting transfers between devices, exchange(): lax.ppermute(slots[r], 'pencil', [(i, i ^ r) for i in range(n)])  63.3 us
    ppermute x27, waiting for transfers between devices, exchange(): lax.ppermute(slots[r], 'pencil', [(i, i ^ r) for i in range(n)])  51.9 us
    pallas_call x5, Pallas kernels, y_call(): pl.pallas_call(functools.partial(y_kernel, n, q, params_here), out_shape=...  40.5 us
    pallas_call x4, Pallas kernels, x_call(): pl.pallas_call(functools.partial(x_kernel, n, q, params_here), grid=(deep...  26.2 us
    unnamed x63, local copies, waits for them, and re-layouts  14 us
    ppermute x1, starting transfers between devices, exchange_state(): lax.ppermute(made[kept], 'pencil', [(i, i ^ n - 1) for i in range(n)])  5.14 us
    pallas_call x5, Pallas kernels, place_tangent(): pl.pallas_call(functools.partial(place_kernel, n, q, some), out_shape=jax...  4.66 us
  transfers between devices with their start and end apart: 38, of which 6 were waited for; matrix products, arithmetic and copies ran while one was open for 1% of the time, Pallas kernels for 33%

profile of v5, /device:TPU:0, one launch (start us, length us, event | category | flops | bytes accessed | tf_op | source)
XLA Modules:
  0.0 214.6 jit_solution(1573343238011953874)
XLA Ops:
  0.6 4.0 %shard_map.104 = (bf16[8,64,128]{2,1,0:T(8,128)(2,1)}, bf16[8,64,128]{2,1,0:T(8,128)(2,1)}, bf16[2,8,64,128]{3,2,1,0:T(8,128)(2,1)}) custom-call(f32[8,8]{1,0:T(8,128)} %rates.17, f32[8,8]{1,0:T(8,128)} %coef.17, f32[2,8]{1,0:T(2,128)} %advect.17, f32[8]{0:T(128)} %diffuse.17, bf16[8,1,128,512]{3,2,1,0:T(8,128)(2,1)} %state.7, bf16[512,512]{1,0:T(8,128)(2,1)} %d1.7, ...), custom_call_target="tpu_custom_call" | custom-call | flops 805306368 | bytes 1048576 | tf_op jit(solution)/shard_map/pallas_call | solution.py:323
  4.6 5.1 %collective-permute-start.1 = (bf16[2,8,64,128]{3,2,1,0:T(8,128)(2,1)}, bf16[2,8,64,128]{3,2,1,0:T(8,128)(2,1)S(1)}, u32[]{:S(2)}, u32[]{:S(2)}) collective-permute-start(bf16[2,8,64,128]{3,2,1,0:T(8,128)(2,1)} %get-tuple-element.43), channel_id=1, source_target_pairs={{0,12},{4,8},{8,4},{12,0},{1,13},{5,9},{9,5},{13,1},{2,14},{6,10},... | collective-permute-start | bytes 786440 | tf_op jit(solution)/shard_map/ppermute | solution.py:420
  9.8 6.6 %shard_map.112 = (bf16[8,128,128]{2,1,0:T(8,128)(2,1)}, bf16[8,128,128]{2,1,0:T(8,128)(2,1)}, bf16[8,128,128]{2,1,0:T(8,128)(2,1)}, bf16[8,128,128]{2,1,0:T(8,128)(2,1)}) custom-call(f32[8,8]{1,0:T(8,128)} %rates.17, f32[8,8]{1,0:T(8,128)} %coef.17, f32[2,8]{1,0:T(2,128)} %advect.17, f32[8]{0:T(128)} %diffuse.17, bf16[8,1,128,512]{3,2,1,0:T(8,128)(2,1)} %state.7, ...), custom_call_target="tpu_custom_call" | custom-call | flops 1610612736 | bytes 2097152 | tf_op jit(solution)/shard_map/pallas_call | solution.py:347
  18.4 6.5 %shard_map.110 = (bf16[8,128,128]{2,1,0:T(8,128)(2,1)}, bf16[8,128,128]{2,1,0:T(8,128)(2,1)}, bf16[8,128,128]{2,1,0:T(8,128)(2,1)}, bf16[8,128,128]{2,1,0:T(8,128)(2,1)}) custom-call(f32[8,8]{1,0:T(8,128)} %rates.17, f32[8,8]{1,0:T(8,128)} %coef.17, f32[2,8]{1,0:T(2,128)} %advect.17, f32[8]{0:T(128)} %diffuse.17, bf16[8,1,128,512]{3,2,1,0:T(8,128)(2,1)} %state.7, ...), custom_call_target="tpu_custom_call" | custom-call | flops 1610612736 | bytes 2097152 | tf_op jit(solution)/shard_map/pallas_call | solution.py:347
  25.0 2.5 %collective-permute-start.34 = (bf16[8,128,128]{2,1,0:T(8,128)(2,1)S(1)}, bf16[8,128,128]{2,1,0:T(8,128)(2,1)S(1)}, u32[]{:S(2)}, u32[]{:S(2)}) collective-permute-start(bf16[8,128,128]{2,1,0:T(8,128)(2,1)S(1)} %copy-done.29), channel_id=1, source_target_pairs={{0,12},{4,8},{8,4},{12,0},{1,13},{5,9},{9,5},{13,1},{2,14},{6,10},... | collective-permute-start | bytes 786440 | tf_op jit(solution)/shard_map/ppermute | solution.py:414
  31.4 6.6 %shard_map.108 = (bf16[8,128,128]{2,1,0:T(8,128)(2,1)}, bf16[8,128,128]{2,1,0:T(8,128)(2,1)}, bf16[8,128,128]{2,1,0:T(8,128)(2,1)}, bf16[8,128,128]{2,1,0:T(8,128)(2,1)}) custom-call(f32[8,8]{1,0:T(8,128)} %rates.17, f32[8,8]{1,0:T(8,128)} %coef.17, f32[2,8]{1,0:T(2,128)} %advect.17, f32[8]{0:T(128)} %diffuse.17, bf16[8,1,128,512]{3,2,1,0:T(8,128)(2,1)} %state.7, ...), custom_call_target="tpu_custom_call" | custom-call | flops 1610612736 | bytes 2097152 | tf_op jit(solution)/shard_map/pallas_call | solution.py:347
  41.9 16.3 %collective-permute-start.20 = (bf16[8,128,128]{2,1,0:T(8,128)(2,1)}, bf16[8,128,128]{2,1,0:T(8,128)(2,1)S(1)}, u32[]{:S(2)}, u32[]{:S(2)}) collective-permute-start(bf16[8,128,128]{2,1,0:T(8,128)(2,1)} %get-tuple-element.57), channel_id=1, source_target_pairs={{0,4},{4,0},{8,12},{12,8},{1,5},{5,1},{9,13},{13,9},{2,6},{6,2},{1... | collective-permute-start | bytes 786440 | tf_op jit(solution)/shard_map/ppermute | solution.py:414
  58.2 10.0 %collective-permute-done.27.rest_10_ = bf16[8,128,128]{2,1,0:T(8,128)(2,1)S(1)} collective-permute-done((bf16[8,128,128]{2,1,0:T(8,128)(2,1)}, bf16[8,128,128]{2,1,0:T(8,128)(2,1)S(1)}, u32[]{:S(2)}, u32[]{:S(2)}) %collective-permute-start.27) | collective-permute-done | bytes 262176 | tf_op jit(solution)/shard_map/ppermute | solution.py:414
  68.8 6.5 %shard_map.106 = (bf16[8,128,128]{2,1,0:T(8,128)(2,1)}, bf16[8,128,128]{2,1,0:T(8,128)(2,1)}, bf16[8,128,128]{2,1,0:T(8,128)(2,1)}, bf16[8,128,128]{2,1,0:T(8,128)(2,1)}) custom-call(f32[8,8]{1,0:T(8,128)} %rates.17, f32[8,8]{1,0:T(8,128)} %coef.17, f32[2,8]{1,0:T(2,128)} %advect.17, f32[8]{0:T(128)} %diffuse.17, bf16[8,1,128,512]{3,2,1,0:T(8,128)(2,1)} %state.7, ...), custom_call_target="tpu_custom_call" | custom-call | flops 1610612736 | bytes 2097152 | tf_op jit(solution)/shard_map/pallas_call | solution.py:347
  76.7 4.4 %collective-permute-start.15 = (bf16[8,128,128]{2,1,0:T(8,128)(2,1)}, bf16[8,128,128]{2,1,0:T(8,128)(2,1)}, u32[]{:S(2)}, u32[]{:S(2)}) collective-permute-start(bf16[8,128,128]{2,1,0:T(8,128)(2,1)} %get-tuple-element.50), channel_id=1, source_target_pairs={{0,8},{4,12},{8,0},{12,4},{1,9},{5,13},{9,1},{13,5},{2,10},{6,14},... | collective-permute-start | bytes 786440 | tf_op jit(solution)/shard_map/ppermute | solution.py:414
  91.7 8.7 %shard_map.113 = (bf16[8,128,128]{2,1,0:T(8,128)(2,1)S(1)}, bf16[8,128,128]{2,1,0:T(8,128)(2,1)S(1)}, bf16[8,128,128]{2,1,0:T(8,128)(2,1)S(1)}, bf16[8,128,128]{2,1,0:T(8,128)(2,1)S(1)}) custom-call(f32[8,8]{1,0:T(8,128)S(1)} %copy-done, f32[8,8]{1,0:T(8,128)S(1)} %copy-done.1, f32[2,8]{1,0:T(2,128)S(1)} %copy-done.2, f32[8]{0:T(128)S(1)} %copy-done.3, ...), custom_call_target="tpu_custom_call" | custom-call | flops 1610612736 | bytes 2097152 | tf_op jit(solution)/shard_map/pallas_call | solution.py:371
  101.1 5.0 %shard_map.105 = (bf16[4,128,128]{2,1,0:T(8,128)(2,1)S(1)}, bf16[4,128,128]{2,1,0:T(8,128)(2,1)S(1)}, bf16[4,128,128]{2,1,0:T(8,128)(2,1)S(1)}, bf16[4,128,128]{2,1,0:T(8,128)(2,1)S(1)}) custom-call(f32[8,8]{1,0:T(8,128)S(1)} %copy-done, f32[8,8]{1,0:T(8,128)S(1)} %copy-done.1, f32[2,8]{1,0:T(2,128)S(1)} %copy-done.2, f32[8]{0:T(128)S(1)} %copy-done.3, ...), custom_call_target="tpu_custom_call" | custom-call | flops 805306368 | bytes 1048576 | tf_op jit(solution)/shard_map/pallas_call | solution.py:371
  106.1 3.9 %collective-permute-start.36 = (bf16[8,128,128]{2,1,0:T(8,128)(2,1)S(1)}, bf16[8,128,128]{2,1,0:T(8,128)(2,1)S(1)}, u32[]{:S(2)}, u32[]{:S(2)}) collective-permute-start(bf16[8,128,128]{2,1,0:T(8,128)(2,1)S(1)} %get-tuple-element.78), channel_id=1, source_target_pairs={{0,8},{4,12},{8,0},{12,4},{1,9},{5,13},{9,1},{13,5},{2,10},{6,14},... | collective-permute-start | bytes 786440 | tf_op jit(solution)/shard_map/ppermute | solution.py:414
  110.6 3.8 %collective-permute-start.9 = (bf16[4,128,128]{2,1,0:T(8,128)(2,1)S(1)}, bf16[4,128,128]{2,1,0:T(8,128)(2,1)S(1)}, u32[]{:S(2)}, u32[]{:S(2)}) collective-permute-start(bf16[4,128,128]{2,1,0:T(8,128)(2,1)S(1)} %get-tuple-element.47), channel_id=1, source_target_pairs={{0,12},{4,8},{8,4},{12,0},{1,13},{5,9},{9,5},{13,1},{2,14},{6,10},... | collective-permute-start | bytes 393224 | tf_op jit(solution)/shard_map/ppermute | solution.py:414
  114.4 8.7 %shard_map.111 = (bf16[8,128,128]{2,1,0:T(8,128)(2,1)S(1)}, bf16[8,128,128]{2,1,0:T(8,128)(2,1)S(1)}, bf16[8,128,128]{2,1,0:T(8,128)(2,1)S(1)}, bf16[8,128,128]{2,1,0:T(8,128)(2,1)S(1)}) custom-call(f32[8,8]{1,0:T(8,128)S(1)} %copy-done, f32[8,8]{1,0:T(8,128)S(1)} %copy-done.1, f32[2,8]{1,0:T(2,128)S(1)} %copy-done.2, f32[8]{0:T(128)S(1)} %copy-done.3, ...), custom_call_target="tpu_custom_call" | custom-call | flops 1610612736 | bytes 2097152 | tf_op jit(solution)/shard_map/pallas_call | solution.py:371
  123.2 15.2 %collective-permute-done.8.rest_2_ = bf16[4,128,128]{2,1,0:T(8,128)(2,1)S(1)} collective-permute-done((bf16[4,128,128]{2,1,0:T(8,128)(2,1)S(1)}, bf16[4,128,128]{2,1,0:T(8,128)(2,1)S(1)}, u32[]{:S(2)}, u32[]{:S(2)}) %collective-permute-start.8) | collective-permute-done | bytes 131104 | tf_op jit(solution)/shard_map/ppermute | solution.py:414
  140.8 3.4 %collective-permute-start.31 = (bf16[8,128,128]{2,1,0:T(8,128)(2,1)S(1)}, bf16[8,128,128]{2,1,0:T(8,128)(2,1)S(1)}, u32[]{:S(2)}, u32[]{:S(2)}) collective-permute-start(bf16[8,128,128]{2,1,0:T(8,128)(2,1)S(1)} %get-tuple-element.71), channel_id=1, source_target_pairs={{0,12},{4,8},{8,4},{12,0},{1,13},{5,9},{9,5},{13,1},{2,14},{6,10},... | collective-permute-start | bytes 786440 | tf_op jit(solution)/shard_map/ppermute | solution.py:414
  144.2 9.1 %shard_map.109 = (bf16[8,128,128]{2,1,0:T(8,128)(2,1)S(1)}, bf16[8,128,128]{2,1,0:T(8,128)(2,1)S(1)}, bf16[8,128,128]{2,1,0:T(8,128)(2,1)S(1)}, bf16[8,128,128]{2,1,0:T(8,128)(2,1)S(1)}) custom-call(f32[8,8]{1,0:T(8,128)S(1)} %copy-done, f32[8,8]{1,0:T(8,128)S(1)} %copy-done.1, f32[2,8]{1,0:T(2,128)S(1)} %copy-done.2, f32[8]{0:T(128)S(1)} %copy-done.3, ...), custom_call_target="tpu_custom_call" | custom-call | flops 1610612736 | bytes 2097152 | tf_op jit(solution)/shard_map/pallas_call | solution.py:371
  153.4 9.1 %shard_map.107 = (bf16[8,128,128]{2,1,0:T(8,128)(2,1)S(1)}, bf16[8,128,128]{2,1,0:T(8,128)(2,1)S(1)}, bf16[8,128,128]{2,1,0:T(8,128)(2,1)S(1)}, bf16[8,128,128]{2,1,0:T(8,128)(2,1)S(1)}) custom-call(f32[8,8]{1,0:T(8,128)S(1)} %copy-done, f32[8,8]{1,0:T(8,128)S(1)} %copy-done.1, f32[2,8]{1,0:T(2,128)S(1)} %copy-done.2, f32[8]{0:T(128)S(1)} %copy-done.3, ...), custom_call_target="tpu_custom_call" | custom-call | flops 1610612736 | bytes 2097152 | tf_op jit(solution)/shard_map/pallas_call | solution.py:371
  163.5 3.3 %collective-permute-start.25 = (bf16[8,128,128]{2,1,0:T(8,128)(2,1)S(1)}, bf16[8,128,128]{2,1,0:T(8,128)(2,1)S(1)}, u32[]{:S(2)}, u32[]{:S(2)}) collective-permute-start(bf16[8,128,128]{2,1,0:T(8,128)(2,1)S(1)} %get-tuple-element.63), channel_id=1, source_target_pairs={{0,12},{4,8},{8,4},{12,0},{1,13},{5,9},{9,5},{13,1},{2,14},{6,10},... | collective-permute-start | bytes 786440 | tf_op jit(solution)/shard_map/ppermute | solution.py:414
  166.9 13.3 %collective-permute-start.19 = (bf16[8,128,128]{2,1,0:T(8,128)(2,1)S(1)}, bf16[8,128,128]{2,1,0:T(8,128)(2,1)S(1)}, u32[]{:S(2)}, u32[]{:S(2)}) collective-permute-start(bf16[8,128,128]{2,1,0:T(8,128)(2,1)S(1)} %get-tuple-element.55), channel_id=1, source_target_pairs={{0,8},{4,12},{8,0},{12,4},{1,9},{5,13},{9,1},{13,5},{2,10},{6,14},... | collective-permute-start | bytes 786440 | tf_op jit(solution)/shard_map/ppermute | solution.py:414
  180.1 3.3 %collective-permute-start.17 = (bf16[8,128,128]{2,1,0:T(8,128)(2,1)S(1)}, bf16[8,128,128]{2,1,0:T(8,128)(2,1)S(1)}, u32[]{:S(2)}, u32[]{:S(2)}) collective-permute-start(bf16[8,128,128]{2,1,0:T(8,128)(2,1)S(1)} %get-tuple-element.52), channel_id=1, source_target_pairs={{0,12},{4,8},{8,4},{12,0},{1,13},{5,9},{9,5},{13,1},{2,14},{6,10},... | collective-permute-start | bytes 786440 | tf_op jit(solution)/shard_map/ppermute | solution.py:414
  183.5 13.9 %collective-permute-done.24.rest_2_ = bf16[8,128,128]{2,1,0:T(8,128)(2,1)S(1)} collective-permute-done((bf16[8,128,128]{2,1,0:T(8,128)(2,1)S(1)}, bf16[8,128,128]{2,1,0:T(8,128)(2,1)S(1)}, u32[]{:S(2)}, u32[]{:S(2)}) %collective-permute-start.24) | collective-permute-done | bytes 262176 | tf_op jit(solution)/shard_map/ppermute | solution.py:414
  198.0 10.6 %collective-permute-done.19.rest_2_ = bf16[8,128,128]{2,1,0:T(8,128)(2,1)S(1)} collective-permute-done((bf16[8,128,128]{2,1,0:T(8,128)(2,1)S(1)}, bf16[8,128,128]{2,1,0:T(8,128)(2,1)S(1)}, u32[]{:S(2)}, u32[]{:S(2)}) %collective-permute-start.19) | collective-permute-done | bytes 262176 | tf_op jit(solution)/shard_map/ppermute | solution.py:414
  (132 shorter events, 33.5 us)
Async XLA Ops:
  27.5 30.6 %collective-permute-start.26 = (bf16[8,128,128]{2,1,0:T(8,128)(2,1)}, bf16[8,128,128]{2,1,0:T(8,128)(2,1)S(1)}, u32[]{:S(2)}, u32[]{:S(2)}) collective-permute-start(bf16[8,128,128]{2,1,0:T(8,128)(2,1)} %get-tuple-element.65), channel_id=1, source_target_pairs={{0,4},{4,0},{8,12},{12,8},{1,5},{5,1},{9,13},{13,9},{2,6},{6,2},{1... | collective-permute-start | bytes 786440 | tf_op jit(solution)/shard_map/ppermute | solution.py:414
  29.5 38.7 %collective-permute-start.27 = (bf16[8,128,128]{2,1,0:T(8,128)(2,1)}, bf16[8,128,128]{2,1,0:T(8,128)(2,1)S(1)}, u32[]{:S(2)}, u32[]{:S(2)}) collective-permute-start(bf16[8,128,128]{2,1,0:T(8,128)(2,1)} %get-tuple-element.66), channel_id=1, source_target_pairs={{0,8},{4,12},{8,0},{12,4},{1,9},{5,13},{9,1},{13,5},{2,10},{6,14},... | collective-permute-start | bytes 786440 | tf_op jit(solution)/shard_map/ppermute | solution.py:414
  30.2 38.1 %collective-permute-start.2 = (bf16[8,64,128]{2,1,0:T(8,128)(2,1)S(1)}, bf16[8,64,128]{2,1,0:T(8,128)(2,1)S(1)}, u32[]{:S(2)}, u32[]{:S(2)}) collective-permute-start(bf16[8,64,128]{2,1,0:T(8,128)(2,1)S(1)} %get-tuple-element.81), channel_id=1, source_target_pairs={{0,4},{4,0},{8,12},{12,8},{1,5},{5,1},{9,13},{13,9},{2,6},{6,2},{1... | collective-permute-start | bytes 393224 | tf_op jit(solution)/shard_map/ppermute | solution.py:425
  40.7 34.6 %collective-permute-start.28 = (bf16[8,128,128]{2,1,0:T(8,128)(2,1)}, bf16[8,128,128]{2,1,0:T(8,128)(2,1)S(1)}, u32[]{:S(2)}, u32[]{:S(2)}) collective-permute-start(bf16[8,128,128]{2,1,0:T(8,128)(2,1)} %get-tuple-element.67), channel_id=1, source_target_pairs={{0,12},{4,8},{8,4},{12,0},{1,13},{5,9},{9,5},{13,1},{2,14},{6,10},... | collective-permute-start | bytes 786440 | tf_op jit(solution)/shard_map/ppermute | solution.py:414
  41.9 34.1 %collective-permute-start.20 = (bf16[8,128,128]{2,1,0:T(8,128)(2,1)}, bf16[8,128,128]{2,1,0:T(8,128)(2,1)S(1)}, u32[]{:S(2)}, u32[]{:S(2)}) collective-permute-start(bf16[8,128,128]{2,1,0:T(8,128)(2,1)} %get-tuple-element.57), channel_id=1, source_target_pairs={{0,4},{4,0},{8,12},{12,8},{1,5},{5,1},{9,13},{13,9},{2,6},{6,2},{1... | collective-permute-start | bytes 786440 | tf_op jit(solution)/shard_map/ppermute | solution.py:414
  58.2 42.2 %collective-permute-start.21 = (bf16[8,128,128]{2,1,0:T(8,128)(2,1)}, bf16[8,128,128]{2,1,0:T(8,128)(2,1)S(1)}, u32[]{:S(2)}, u32[]{:S(2)}) collective-permute-start(bf16[8,128,128]{2,1,0:T(8,128)(2,1)} %get-tuple-element.58), channel_id=1, source_target_pairs={{0,8},{4,12},{8,0},{12,4},{1,9},{5,13},{9,1},{13,5},{2,10},{6,14},... | collective-permute-start | bytes 786440 | tf_op jit(solution)/shard_map/ppermute | solution.py:414
  76.0 30.1 %collective-permute-start.22 = (bf16[8,128,128]{2,1,0:T(8,128)(2,1)}, bf16[8,128,128]{2,1,0:T(8,128)(2,1)}, u32[]{:S(2)}, u32[]{:S(2)}) collective-permute-start(bf16[8,128,128]{2,1,0:T(8,128)(2,1)} %get-tuple-element.59), channel_id=1, source_target_pairs={{0,12},{4,8},{8,4},{12,0},{1,13},{5,9},{9,5},{13,1},{2,14},{6,10},... | collective-permute-start | bytes 786440 | tf_op jit(solution)/shard_map/ppermute | solution.py:414
  76.0 34.0 %collective-permute-start.14 = (bf16[8,128,128]{2,1,0:T(8,128)(2,1)}, bf16[8,128,128]{2,1,0:T(8,128)(2,1)S(1)}, u32[]{:S(2)}, u32[]{:S(2)}) collective-permute-start(bf16[8,128,128]{2,1,0:T(8,128)(2,1)} %get-tuple-element.49), channel_id=1, source_target_pairs={{0,4},{4,0},{8,12},{12,8},{1,5},{5,1},{9,13},{13,9},{2,6},{6,2},{1... | collective-permute-start | bytes 786440 | tf_op jit(solution)/shard_map/ppermute | solution.py:414
  76.7 33.3 %collective-permute-start.15 = (bf16[8,128,128]{2,1,0:T(8,128)(2,1)}, bf16[8,128,128]{2,1,0:T(8,128)(2,1)}, u32[]{:S(2)}, u32[]{:S(2)}) collective-permute-start(bf16[8,128,128]{2,1,0:T(8,128)(2,1)} %get-tuple-element.50), channel_id=1, source_target_pairs={{0,8},{4,12},{8,0},{12,4},{1,9},{5,13},{9,1},{13,5},{2,10},{6,14},... | collective-permute-start | bytes 786440 | tf_op jit(solution)/shard_map/ppermute | solution.py:414
  81.7 28.8 %collective-permute-start.16 = (bf16[8,128,128]{2,1,0:T(8,128)(2,1)}, bf16[8,128,128]{2,1,0:T(8,128)(2,1)}, u32[]{:S(2)}, u32[]{:S(2)}) collective-permute-start(bf16[8,128,128]{2,1,0:T(8,128)(2,1)} %get-tuple-element.51), channel_id=1, source_target_pairs={{0,12},{4,8},{8,4},{12,0},{1,13},{5,9},{9,5},{13,1},{2,14},{6,10},... | collective-permute-start | bytes 786440 | tf_op jit(solution)/shard_map/ppermute | solution.py:414
  100.4 40.4 %collective-permute-start.35 = (bf16[8,128,128]{2,1,0:T(8,128)(2,1)S(1)}, bf16[8,128,128]{2,1,0:T(8,128)(2,1)S(1)}, u32[]{:S(2)}, u32[]{:S(2)}) collective-permute-start(bf16[8,128,128]{2,1,0:T(8,128)(2,1)S(1)} %get-tuple-element.77), channel_id=1, source_target_pairs={{0,4},{4,0},{8,12},{12,8},{1,5},{5,1},{9,13},{13,9},{2,6},{6,2},{1... | collective-permute-start | bytes 786440 | tf_op jit(solution)/shard_map/ppermute | solution.py:414
  106.1 47.2 %collective-permute-start.36 = (bf16[8,128,128]{2,1,0:T(8,128)(2,1)S(1)}, bf16[8,128,128]{2,1,0:T(8,128)(2,1)S(1)}, u32[]{:S(2)}, u32[]{:S(2)}) collective-permute-start(bf16[8,128,128]{2,1,0:T(8,128)(2,1)S(1)} %get-tuple-element.78), channel_id=1, source_target_pairs={{0,8},{4,12},{8,0},{12,4},{1,9},{5,13},{9,1},{13,5},{2,10},{6,14},... | collective-permute-start | bytes 786440 | tf_op jit(solution)/shard_map/ppermute | solution.py:414
  110.0 28.4 %collective-permute-start.8 = (bf16[4,128,128]{2,1,0:T(8,128)(2,1)S(1)}, bf16[4,128,128]{2,1,0:T(8,128)(2,1)S(1)}, u32[]{:S(2)}, u32[]{:S(2)}) collective-permute-start(bf16[4,128,128]{2,1,0:T(8,128)(2,1)S(1)} %get-tuple-element.46), channel_id=1, source_target_pairs={{0,8},{4,12},{8,0},{12,4},{1,9},{5,13},{9,1},{13,5},{2,10},{6,14},... | collective-permute-start | bytes 393224 | tf_op jit(solution)/shard_map/ppermute | solution.py:414
  110.6 27.9 %collective-permute-start.9 = (bf16[4,128,128]{2,1,0:T(8,128)(2,1)S(1)}, bf16[4,128,128]{2,1,0:T(8,128)(2,1)S(1)}, u32[]{:S(2)}, u32[]{:S(2)}) collective-permute-start(bf16[4,128,128]{2,1,0:T(8,128)(2,1)S(1)} %get-tuple-element.47), channel_id=1, source_target_pairs={{0,12},{4,8},{8,4},{12,0},{1,13},{5,9},{9,5},{13,1},{2,14},{6,10},... | collective-permute-start | bytes 393224 | tf_op jit(solution)/shard_map/ppermute | solution.py:414
  123.1 39.4 %collective-permute-start.37 = (bf16[8,128,128]{2,1,0:T(8,128)(2,1)S(1)}, bf16[8,128,128]{2,1,0:T(8,128)(2,1)S(1)}, u32[]{:S(2)}, u32[]{:S(2)}) collective-permute-start(bf16[8,128,128]{2,1,0:T(8,128)(2,1)S(1)} %get-tuple-element.79), channel_id=1, source_target_pairs={{0,12},{4,8},{8,4},{12,0},{1,13},{5,9},{9,5},{13,1},{2,14},{6,10},... | collective-permute-start | bytes 786440 | tf_op jit(solution)/shard_map/ppermute | solution.py:414
  138.4 25.1 %collective-permute-start.29 = (bf16[8,128,128]{2,1,0:T(8,128)(2,1)S(1)}, bf16[8,128,128]{2,1,0:T(8,128)(2,1)S(1)}, u32[]{:S(2)}, u32[]{:S(2)}) collective-permute-start(bf16[8,128,128]{2,1,0:T(8,128)(2,1)S(1)} %get-tuple-element.69), channel_id=1, source_target_pairs={{0,4},{4,0},{8,12},{12,8},{1,5},{5,1},{9,13},{13,9},{2,6},{6,2},{1... | collective-permute-start | bytes 786440 | tf_op jit(solution)/shard_map/ppermute | solution.py:414
  138.4 28.4 %collective-permute-start.30 = (bf16[8,128,128]{2,1,0:T(8,128)(2,1)S(1)}, bf16[8,128,128]{2,1,0:T(8,128)(2,1)S(1)}, u32[]{:S(2)}, u32[]{:S(2)}) collective-permute-start(bf16[8,128,128]{2,1,0:T(8,128)(2,1)S(1)} %get-tuple-element.70), channel_id=1, source_target_pairs={{0,8},{4,12},{8,0},{12,4},{1,9},{5,13},{9,1},{13,5},{2,10},{6,14},... | collective-permute-start | bytes 786440 | tf_op jit(solution)/shard_map/ppermute | solution.py:414
  140.8 26.1 %collective-permute-start.31 = (bf16[8,128,128]{2,1,0:T(8,128)(2,1)S(1)}, bf16[8,128,128]{2,1,0:T(8,128)(2,1)S(1)}, u32[]{:S(2)}, u32[]{:S(2)}) collective-permute-start(bf16[8,128,128]{2,1,0:T(8,128)(2,1)S(1)} %get-tuple-element.71), channel_id=1, source_target_pairs={{0,12},{4,8},{8,4},{12,0},{1,13},{5,9},{9,5},{13,1},{2,14},{6,10},... | collective-permute-start | bytes 786440 | tf_op jit(solution)/shard_map/ppermute | solution.py:414
  153.3 26.9 %collective-permute-start.23 = (bf16[8,128,128]{2,1,0:T(8,128)(2,1)S(1)}, bf16[8,128,128]{2,1,0:T(8,128)(2,1)S(1)}, u32[]{:S(2)}, u32[]{:S(2)}) collective-permute-start(bf16[8,128,128]{2,1,0:T(8,128)(2,1)S(1)} %get-tuple-element.61), channel_id=1, source_target_pairs={{0,4},{4,0},{8,12},{12,8},{1,5},{5,1},{9,13},{13,9},{2,6},{6,2},{1... | collective-permute-start | bytes 786440 | tf_op jit(solution)/shard_map/ppermute | solution.py:414
  162.5 35.0 %collective-permute-start.24 = (bf16[8,128,128]{2,1,0:T(8,128)(2,1)S(1)}, bf16[8,128,128]{2,1,0:T(8,128)(2,1)S(1)}, u32[]{:S(2)}, u32[]{:S(2)}) collective-permute-start(bf16[8,128,128]{2,1,0:T(8,128)(2,1)S(1)} %get-tuple-element.62), channel_id=1, source_target_pairs={{0,8},{4,12},{8,0},{12,4},{1,9},{5,13},{9,1},{13,5},{2,10},{6,14},... | collective-permute-start | bytes 786440 | tf_op jit(solution)/shard_map/ppermute | solution.py:414
  163.5 33.9 %collective-permute-start.25 = (bf16[8,128,128]{2,1,0:T(8,128)(2,1)S(1)}, bf16[8,128,128]{2,1,0:T(8,128)(2,1)S(1)}, u32[]{:S(2)}, u32[]{:S(2)}) collective-permute-start(bf16[8,128,128]{2,1,0:T(8,128)(2,1)S(1)} %get-tuple-element.63), channel_id=1, source_target_pairs={{0,12},{4,8},{8,4},{12,0},{1,13},{5,9},{9,5},{13,1},{2,14},{6,10},... | collective-permute-start | bytes 786440 | tf_op jit(solution)/shard_map/ppermute | solution.py:414
  166.9 31.1 %collective-permute-start.18 = (bf16[8,128,128]{2,1,0:T(8,128)(2,1)S(1)}, bf16[8,128,128]{2,1,0:T(8,128)(2,1)S(1)}, u32[]{:S(2)}, u32[]{:S(2)}) collective-permute-start(bf16[8,128,128]{2,1,0:T(8,128)(2,1)S(1)} %get-tuple-element.54), channel_id=1, source_target_pairs={{0,4},{4,0},{8,12},{12,8},{1,5},{5,1},{9,13},{13,9},{2,6},{6,2},{1... | collective-permute-start | bytes 786440 | tf_op jit(solution)/shard_map/ppermute | solution.py:414
  166.9 41.8 %collective-permute-start.19 = (bf16[8,128,128]{2,1,0:T(8,128)(2,1)S(1)}, bf16[8,128,128]{2,1,0:T(8,128)(2,1)S(1)}, u32[]{:S(2)}, u32[]{:S(2)}) collective-permute-start(bf16[8,128,128]{2,1,0:T(8,128)(2,1)S(1)} %get-tuple-element.55), channel_id=1, source_target_pairs={{0,8},{4,12},{8,0},{12,4},{1,9},{5,13},{9,1},{13,5},{2,10},{6,14},... | collective-permute-start | bytes 786440 | tf_op jit(solution)/shard_map/ppermute | solution.py:414
  180.1 32.5 %collective-permute-start.17 = (bf16[8,128,128]{2,1,0:T(8,128)(2,1)S(1)}, bf16[8,128,128]{2,1,0:T(8,128)(2,1)S(1)}, u32[]{:S(2)}, u32[]{:S(2)}) collective-permute-start(bf16[8,128,128]{2,1,0:T(8,128)(2,1)S(1)} %get-tuple-element.52), channel_id=1, source_target_pairs={{0,12},{4,8},{8,4},{12,0},{1,13},{5,9},{9,5},{13,1},{2,14},{6,10},... | collective-permute-start | bytes 786440 | tf_op jit(solution)/shard_map/ppermute | solution.py:414
  (44 other events, 542.4 us)

commit v6 on v5

--- a/solution.py
+++ b/solution.py
@@ -125,12 +125,11 @@
     sources = list(far)
     sources[4] = far[4].at[:, :, aligned(PARTS * half + part, rows), :]
     copies = [pltpu.make_async_copy(sources[i], near[i], sems.at[i]) for i in range(8)]
-    for copy in copies:
-        copy.start()
-    for copy in copies[:4]:
-        copy.wait()
+    for i in (0, 4, 5, 6, 7, 1, 2, 3):
+        copies[i].start()
+    copies[0].wait()
     fill_mixer(lambda a, b: rates[a, b], rates_high, rates_low)
-    for copy in copies[4:]:
+    for copy in copies[1:]:
         copy.wait()
     own = state[:, 0].reshape(fields * rows, length)
     for c in range(length // WIDE):

time: 215 us -> 215 us (level)
  no operation moved by 1% of the time
where the time goes in v6:
time: 215 us
  Pallas kernels  76.4 us (36%)
  starting transfers between devices  70.8 us (33%)
  waiting for transfers between devices  52.1 us (24%)
  local copies, waits for them, and re-layouts  14 us (7%)
    ppermute x27, starting transfers between devices, exchange(): lax.ppermute(slots[r], 'pencil', [(i, i ^ r) for i in range(n)])  63.3 us
    ppermute x27, waiting for transfers between devices, exchange(): lax.ppermute(slots[r], 'pencil', [(i, i ^ r) for i in range(n)])  51.9 us
    pallas_call x5, Pallas kernels, y_call(): pl.pallas_call(functools.partial(y_kernel, n, q, params_here), out_shape=...  40.5 us
    pallas_call x4, Pallas kernels, x_call(): pl.pallas_call(functools.partial(x_kernel, n, q, params_here), grid=(deep...  26.2 us
    unnamed x63, local copies, waits for them, and re-layouts  14 us
    ppermute x1, starting transfers between devices, exchange_state(): lax.ppermute(made[kept], 'pencil', [(i, i ^ n - 1) for i in range(n)])  5.14 us
    pallas_call x5, Pallas kernels, place_tangent(): pl.pallas_call(functools.partial(place_kernel, n, q, some), out_shape=jax...  4.66 us
  transfers between devices with their start and end apart: 38, of which 6 were waited for; matrix products, arithmetic and copies ran while one was open for 1% of the time, Pallas kernels for 33%

profile of v6, /device:TPU:0, one launch (start us, length us, event | category | flops | bytes accessed | tf_op | source)
XLA Modules:
  0.0 214.6 jit_solution(778885008985717941)
XLA Ops:
  0.6 4.0 %shard_map.104 = (bf16[8,64,128]{2,1,0:T(8,128)(2,1)}, bf16[8,64,128]{2,1,0:T(8,128)(2,1)}, bf16[2,8,64,128]{3,2,1,0:T(8,128)(2,1)}) custom-call(f32[8,8]{1,0:T(8,128)} %rates.17, f32[8,8]{1,0:T(8,128)} %coef.17, f32[2,8]{1,0:T(2,128)} %advect.17, f32[8]{0:T(128)} %diffuse.17, bf16[8,1,128,512]{3,2,1,0:T(8,128)(2,1)} %state.7, bf16[512,512]{1,0:T(8,128)(2,1)} %d1.7, ...), custom_call_target="tpu_custom_call" | custom-call | flops 805306368 | bytes 1048576 | tf_op jit(solution)/shard_map/pallas_call | solution.py:322
  4.6 5.1 %collective-permute-start.1 = (bf16[2,8,64,128]{3,2,1,0:T(8,128)(2,1)}, bf16[2,8,64,128]{3,2,1,0:T(8,128)(2,1)S(1)}, u32[]{:S(2)}, u32[]{:S(2)}) collective-permute-start(bf16[2,8,64,128]{3,2,1,0:T(8,128)(2,1)} %get-tuple-element.43), channel_id=1, source_target_pairs={{0,12},{4,8},{8,4},{12,0},{1,13},{5,9},{9,5},{13,1},{2,14},{6,10},... | collective-permute-start | bytes 786440 | tf_op jit(solution)/shard_map/ppermute | solution.py:419
  9.8 6.6 %shard_map.112 = (bf16[8,128,128]{2,1,0:T(8,128)(2,1)}, bf16[8,128,128]{2,1,0:T(8,128)(2,1)}, bf16[8,128,128]{2,1,0:T(8,128)(2,1)}, bf16[8,128,128]{2,1,0:T(8,128)(2,1)}) custom-call(f32[8,8]{1,0:T(8,128)} %rates.17, f32[8,8]{1,0:T(8,128)} %coef.17, f32[2,8]{1,0:T(2,128)} %advect.17, f32[8]{0:T(128)} %diffuse.17, bf16[8,1,128,512]{3,2,1,0:T(8,128)(2,1)} %state.7, ...), custom_call_target="tpu_custom_call" | custom-call | flops 1610612736 | bytes 2097152 | tf_op jit(solution)/shard_map/pallas_call | solution.py:346
  18.4 6.5 %shard_map.110 = (bf16[8,128,128]{2,1,0:T(8,128)(2,1)}, bf16[8,128,128]{2,1,0:T(8,128)(2,1)}, bf16[8,128,128]{2,1,0:T(8,128)(2,1)}, bf16[8,128,128]{2,1,0:T(8,128)(2,1)}) custom-call(f32[8,8]{1,0:T(8,128)} %rates.17, f32[8,8]{1,0:T(8,128)} %coef.17, f32[2,8]{1,0:T(2,128)} %advect.17, f32[8]{0:T(128)} %diffuse.17, bf16[8,1,128,512]{3,2,1,0:T(8,128)(2,1)} %state.7, ...), custom_call_target="tpu_custom_call" | custom-call | flops 1610612736 | bytes 2097152 | tf_op jit(solution)/shard_map/pallas_call | solution.py:346
  25.0 2.5 %collective-permute-start.34 = (bf16[8,128,128]{2,1,0:T(8,128)(2,1)S(1)}, bf16[8,128,128]{2,1,0:T(8,128)(2,1)S(1)}, u32[]{:S(2)}, u32[]{:S(2)}) collective-permute-start(bf16[8,128,128]{2,1,0:T(8,128)(2,1)S(1)} %copy-done.29), channel_id=1, source_target_pairs={{0,12},{4,8},{8,4},{12,0},{1,13},{5,9},{9,5},{13,1},{2,14},{6,10},... | collective-permute-start | bytes 786440 | tf_op jit(solution)/shard_map/ppermute | solution.py:413
  31.4 6.6 %shard_map.108 = (bf16[8,128,128]{2,1,0:T(8,128)(2,1)}, bf16[8,128,128]{2,1,0:T(8,128)(2,1)}, bf16[8,128,128]{2,1,0:T(8,128)(2,1)}, bf16[8,128,128]{2,1,0:T(8,128)(2,1)}) custom-call(f32[8,8]{1,0:T(8,128)} %rates.17, f32[8,8]{1,0:T(8,128)} %coef.17, f32[2,8]{1,0:T(2,128)} %advect.17, f32[8]{0:T(128)} %diffuse.17, bf16[8,1,128,512]{3,2,1,0:T(8,128)(2,1)} %state.7, ...), custom_call_target="tpu_custom_call" | custom-call | flops 1610612736 | bytes 2097152 | tf_op jit(solution)/shard_map/pallas_call | solution.py:346
  41.9 16.3 %collective-permute-start.20 = (bf16[8,128,128]{2,1,0:T(8,128)(2,1)}, bf16[8,128,128]{2,1,0:T(8,128)(2,1)S(1)}, u32[]{:S(2)}, u32[]{:S(2)}) collective-permute-start(bf16[8,128,128]{2,1,0:T(8,128)(2,1)} %get-tuple-element.57), channel_id=1, source_target_pairs={{0,4},{4,0},{8,12},{12,8},{1,5},{5,1},{9,13},{13,9},{2,6},{6,2},{1... | collective-permute-start | bytes 786440 | tf_op jit(solution)/shard_map/ppermute | solution.py:413
  58.2 10.0 %collective-permute-done.27.rest_10_ = bf16[8,128,128]{2,1,0:T(8,128)(2,1)S(1)} collective-permute-done((bf16[8,128,128]{2,1,0:T(8,128)(2,1)}, bf16[8,128,128]{2,1,0:T(8,128)(2,1)S(1)}, u32[]{:S(2)}, u32[]{:S(2)}) %collective-permute-start.27) | collective-permute-done | bytes 262176 | tf_op jit(solution)/shard_map/ppermute | solution.py:413
  68.8 6.5 %shard_map.106 = (bf16[8,128,128]{2,1,0:T(8,128)(2,1)}, bf16[8,128,128]{2,1,0:T(8,128)(2,1)}, bf16[8,128,128]{2,1,0:T(8,128)(2,1)}, bf16[8,128,128]{2,1,0:T(8,128)(2,1)}) custom-call(f32[8,8]{1,0:T(8,128)} %rates.17, f32[8,8]{1,0:T(8,128)} %coef.17, f32[2,8]{1,0:T(2,128)} %advect.17, f32[8]{0:T(128)} %diffuse.17, bf16[8,1,128,512]{3,2,1,0:T(8,128)(2,1)} %state.7, ...), custom_call_target="tpu_custom_call" | custom-call | flops 1610612736 | bytes 2097152 | tf_op jit(solution)/shard_map/pallas_call | solution.py:346
  76.7 4.4 %collective-permute-start.15 = (bf16[8,128,128]{2,1,0:T(8,128)(2,1)}, bf16[8,128,128]{2,1,0:T(8,128)(2,1)}, u32[]{:S(2)}, u32[]{:S(2)}) collective-permute-start(bf16[8,128,128]{2,1,0:T(8,128)(2,1)} %get-tuple-element.50), channel_id=1, source_target_pairs={{0,8},{4,12},{8,0},{12,4},{1,9},{5,13},{9,1},{13,5},{2,10},{6,14},... | collective-permute-start | bytes 786440 | tf_op jit(solution)/shard_map/ppermute | solution.py:413
  91.7 8.7 %shard_map.113 = (bf16[8,128,128]{2,1,0:T(8,128)(2,1)S(1)}, bf16[8,128,128]{2,1,0:T(8,128)(2,1)S(1)}, bf16[8,128,128]{2,1,0:T(8,128)(2,1)S(1)}, bf16[8,128,128]{2,1,0:T(8,128)(2,1)S(1)}) custom-call(f32[8,8]{1,0:T(8,128)S(1)} %copy-done, f32[8,8]{1,0:T(8,128)S(1)} %copy-done.1, f32[2,8]{1,0:T(2,128)S(1)} %copy-done.2, f32[8]{0:T(128)S(1)} %copy-done.3, ...), custom_call_target="tpu_custom_call" | custom-call | flops 1610612736 | bytes 2097152 | tf_op jit(solution)/shard_map/pallas_call | solution.py:370
  101.1 5.0 %shard_map.105 = (bf16[4,128,128]{2,1,0:T(8,128)(2,1)S(1)}, bf16[4,128,128]{2,1,0:T(8,128)(2,1)S(1)}, bf16[4,128,128]{2,1,0:T(8,128)(2,1)S(1)}, bf16[4,128,128]{2,1,0:T(8,128)(2,1)S(1)}) custom-call(f32[8,8]{1,0:T(8,128)S(1)} %copy-done, f32[8,8]{1,0:T(8,128)S(1)} %copy-done.1, f32[2,8]{1,0:T(2,128)S(1)} %copy-done.2, f32[8]{0:T(128)S(1)} %copy-done.3, ...), custom_call_target="tpu_custom_call" | custom-call | flops 805306368 | bytes 1048576 | tf_op jit(solution)/shard_map/pallas_call | solution.py:370
  106.1 3.9 %collective-permute-start.36 = (bf16[8,128,128]{2,1,0:T(8,128)(2,1)S(1)}, bf16[8,128,128]{2,1,0:T(8,128)(2,1)S(1)}, u32[]{:S(2)}, u32[]{:S(2)}) collective-permute-start(bf16[8,128,128]{2,1,0:T(8,128)(2,1)S(1)} %get-tuple-element.78), channel_id=1, source_target_pairs={{0,8},{4,12},{8,0},{12,4},{1,9},{5,13},{9,1},{13,5},{2,10},{6,14},... | collective-permute-start | bytes 786440 | tf_op jit(solution)/shard_map/ppermute | solution.py:413
  110.6 3.8 %collective-permute-start.9 = (bf16[4,128,128]{2,1,0:T(8,128)(2,1)S(1)}, bf16[4,128,128]{2,1,0:T(8,128)(2,1)S(1)}, u32[]{:S(2)}, u32[]{:S(2)}) collective-permute-start(bf16[4,128,128]{2,1,0:T(8,128)(2,1)S(1)} %get-tuple-element.47), channel_id=1, source_target_pairs={{0,12},{4,8},{8,4},{12,0},{1,13},{5,9},{9,5},{13,1},{2,14},{6,10},... | collective-permute-start | bytes 393224 | tf_op jit(solution)/shard_map/ppermute | solution.py:413
  114.4 8.7 %shard_map.111 = (bf16[8,128,128]{2,1,0:T(8,128)(2,1)S(1)}, bf16[8,128,128]{2,1,0:T(8,128)(2,1)S(1)}, bf16[8,128,128]{2,1,0:T(8,128)(2,1)S(1)}, bf16[8,128,128]{2,1,0:T(8,128)(2,1)S(1)}) custom-call(f32[8,8]{1,0:T(8,128)S(1)} %copy-done, f32[8,8]{1,0:T(8,128)S(1)} %copy-done.1, f32[2,8]{1,0:T(2,128)S(1)} %copy-done.2, f32[8]{0:T(128)S(1)} %copy-done.3, ...), custom_call_target="tpu_custom_call" | custom-call | flops 1610612736 | bytes 2097152 | tf_op jit(solution)/shard_map/pallas_call | solution.py:370
  123.2 15.2 %collective-permute-done.8.rest_2_ = bf16[4,128,128]{2,1,0:T(8,128)(2,1)S(1)} collective-permute-done((bf16[4,128,128]{2,1,0:T(8,128)(2,1)S(1)}, bf16[4,128,128]{2,1,0:T(8,128)(2,1)S(1)}, u32[]{:S(2)}, u32[]{:S(2)}) %collective-permute-start.8) | collective-permute-done | bytes 131104 | tf_op jit(solution)/shard_map/ppermute | solution.py:413
  140.8 3.4 %collective-permute-start.31 = (bf16[8,128,128]{2,1,0:T(8,128)(2,1)S(1)}, bf16[8,128,128]{2,1,0:T(8,128)(2,1)S(1)}, u32[]{:S(2)}, u32[]{:S(2)}) collective-permute-start(bf16[8,128,128]{2,1,0:T(8,128)(2,1)S(1)} %get-tuple-element.71), channel_id=1, source_target_pairs={{0,12},{4,8},{8,4},{12,0},{1,13},{5,9},{9,5},{13,1},{2,14},{6,10},... | collective-permute-start | bytes 786440 | tf_op jit(solution)/shard_map/ppermute | solution.py:413
  144.2 9.1 %shard_map.109 = (bf16[8,128,128]{2,1,0:T(8,128)(2,1)S(1)}, bf16[8,128,128]{2,1,0:T(8,128)(2,1)S(1)}, bf16[8,128,128]{2,1,0:T(8,128)(2,1)S(1)}, bf16[8,128,128]{2,1,0:T(8,128)(2,1)S(1)}) custom-call(f32[8,8]{1,0:T(8,128)S(1)} %copy-done, f32[8,8]{1,0:T(8,128)S(1)} %copy-done.1, f32[2,8]{1,0:T(2,128)S(1)} %copy-done.2, f32[8]{0:T(128)S(1)} %copy-done.3, ...), custom_call_target="tpu_custom_call" | custom-call | flops 1610612736 | bytes 2097152 | tf_op jit(solution)/shard_map/pallas_call | solution.py:370
  153.4 9.1 %shard_map.107 = (bf16[8,128,128]{2,1,0:T(8,128)(2,1)S(1)}, bf16[8,128,128]{2,1,0:T(8,128)(2,1)S(1)}, bf16[8,128,128]{2,1,0:T(8,128)(2,1)S(1)}, bf16[8,128,128]{2,1,0:T(8,128)(2,1)S(1)}) custom-call(f32[8,8]{1,0:T(8,128)S(1)} %copy-done, f32[8,8]{1,0:T(8,128)S(1)} %copy-done.1, f32[2,8]{1,0:T(2,128)S(1)} %copy-done.2, f32[8]{0:T(128)S(1)} %copy-done.3, ...), custom_call_target="tpu_custom_call" | custom-call | flops 1610612736 | bytes 2097152 | tf_op jit(solution)/shard_map/pallas_call | solution.py:370
  163.5 3.3 %collective-permute-start.25 = (bf16[8,128,128]{2,1,0:T(8,128)(2,1)S(1)}, bf16[8,128,128]{2,1,0:T(8,128)(2,1)S(1)}, u32[]{:S(2)}, u32[]{:S(2)}) collective-permute-start(bf16[8,128,128]{2,1,0:T(8,128)(2,1)S(1)} %get-tuple-element.63), channel_id=1, source_target_pairs={{0,12},{4,8},{8,4},{12,0},{1,13},{5,9},{9,5},{13,1},{2,14},{6,10},... | collective-permute-start | bytes 786440 | tf_op jit(solution)/shard_map/ppermute | solution.py:413
  166.9 13.3 %collective-permute-start.19 = (bf16[8,128,128]{2,1,0:T(8,128)(2,1)S(1)}, bf16[8,128,128]{2,1,0:T(8,128)(2,1)S(1)}, u32[]{:S(2)}, u32[]{:S(2)}) collective-permute-start(bf16[8,128,128]{2,1,0:T(8,128)(2,1)S(1)} %get-tuple-element.55), channel_id=1, source_target_pairs={{0,8},{4,12},{8,0},{12,4},{1,9},{5,13},{9,1},{13,5},{2,10},{6,14},... | collective-permute-start | bytes 786440 | tf_op jit(solution)/shard_map/ppermute | solution.py:413
  180.1 3.3 %collective-permute-start.17 = (bf16[8,128,128]{2,1,0:T(8,128)(2,1)S(1)}, bf16[8,128,128]{2,1,0:T(8,128)(2,1)S(1)}, u32[]{:S(2)}, u32[]{:S(2)}) collective-permute-start(bf16[8,128,128]{2,1,0:T(8,128)(2,1)S(1)} %get-tuple-element.52), channel_id=1, source_target_pairs={{0,12},{4,8},{8,4},{12,0},{1,13},{5,9},{9,5},{13,1},{2,14},{6,10},... | collective-permute-start | bytes 786440 | tf_op jit(solution)/shard_map/ppermute | solution.py:413
  183.5 13.9 %collective-permute-done.24.rest_2_ = bf16[8,128,128]{2,1,0:T(8,128)(2,1)S(1)} collective-permute-done((bf16[8,128,128]{2,1,0:T(8,128)(2,1)S(1)}, bf16[8,128,128]{2,1,0:T(8,128)(2,1)S(1)}, u32[]{:S(2)}, u32[]{:S(2)}) %collective-permute-start.24) | collective-permute-done | bytes 262176 | tf_op jit(solution)/shard_map/ppermute | solution.py:413
  198.0 10.6 %collective-permute-done.19.rest_2_ = bf16[8,128,128]{2,1,0:T(8,128)(2,1)S(1)} collective-permute-done((bf16[8,128,128]{2,1,0:T(8,128)(2,1)S(1)}, bf16[8,128,128]{2,1,0:T(8,128)(2,1)S(1)}, u32[]{:S(2)}, u32[]{:S(2)}) %collective-permute-start.19) | collective-permute-done | bytes 262176 | tf_op jit(solution)/shard_map/ppermute | solution.py:413
  (132 shorter events, 33.5 us)
Async XLA Ops:
  27.5 30.6 %collective-permute-start.26 = (bf16[8,128,128]{2,1,0:T(8,128)(2,1)}, bf16[8,128,128]{2,1,0:T(8,128)(2,1)S(1)}, u32[]{:S(2)}, u32[]{:S(2)}) collective-permute-start(bf16[8,128,128]{2,1,0:T(8,128)(2,1)} %get-tuple-element.65), channel_id=1, source_target_pairs={{0,4},{4,0},{8,12},{12,8},{1,5},{5,1},{9,13},{13,9},{2,6},{6,2},{1... | collective-permute-start | bytes 786440 | tf_op jit(solution)/shard_map/ppermute | solution.py:413
  29.5 38.7 %collective-permute-start.27 = (bf16[8,128,128]{2,1,0:T(8,128)(2,1)}, bf16[8,128,128]{2,1,0:T(8,128)(2,1)S(1)}, u32[]{:S(2)}, u32[]{:S(2)}) collective-permute-start(bf16[8,128,128]{2,1,0:T(8,128)(2,1)} %get-tuple-element.66), channel_id=1, source_target_pairs={{0,8},{4,12},{8,0},{12,4},{1,9},{5,13},{9,1},{13,5},{2,10},{6,14},... | collective-permute-start | bytes 786440 | tf_op jit(solution)/shard_map/ppermute | solution.py:413
  30.2 38.1 %collective-permute-start.2 = (bf16[8,64,128]{2,1,0:T(8,128)(2,1)S(1)}, bf16[8,64,128]{2,1,0:T(8,128)(2,1)S(1)}, u32[]{:S(2)}, u32[]{:S(2)}) collective-permute-start(bf16[8,64,128]{2,1,0:T(8,128)(2,1)S(1)} %get-tuple-element.81), channel_id=1, source_target_pairs={{0,4},{4,0},{8,12},{12,8},{1,5},{5,1},{9,13},{13,9},{2,6},{6,2},{1... | collective-permute-start | bytes 393224 | tf_op jit(solution)/shard_map/ppermute | solution.py:424
  40.7 34.6 %collective-permute-start.28 = (bf16[8,128,128]{2,1,0:T(8,128)(2,1)}, bf16[8,128,128]{2,1,0:T(8,128)(2,1)S(1)}, u32[]{:S(2)}, u32[]{:S(2)}) collective-permute-start(bf16[8,128,128]{2,1,0:T(8,128)(2,1)} %get-tuple-element.67), channel_id=1, source_target_pairs={{0,12},{4,8},{8,4},{12,0},{1,13},{5,9},{9,5},{13,1},{2,14},{6,10},... | collective-permute-start | bytes 786440 | tf_op jit(solution)/shard_map/ppermute | solution.py:413
  41.9 34.1 %collective-permute-start.20 = (bf16[8,128,128]{2,1,0:T(8,128)(2,1)}, bf16[8,128,128]{2,1,0:T(8,128)(2,1)S(1)}, u32[]{:S(2)}, u32[]{:S(2)}) collective-permute-start(bf16[8,128,128]{2,1,0:T(8,128)(2,1)} %get-tuple-element.57), channel_id=1, source_target_pairs={{0,4},{4,0},{8,12},{12,8},{1,5},{5,1},{9,13},{13,9},{2,6},{6,2},{1... | collective-permute-start | bytes 786440 | tf_op jit(solution)/shard_map/ppermute | solution.py:413
  58.2 42.2 %collective-permute-start.21 = (bf16[8,128,128]{2,1,0:T(8,128)(2,1)}, bf16[8,128,128]{2,1,0:T(8,128)(2,1)S(1)}, u32[]{:S(2)}, u32[]{:S(2)}) collective-permute-start(bf16[8,128,128]{2,1,0:T(8,128)(2,1)} %get-tuple-element.58), channel_id=1, source_target_pairs={{0,8},{4,12},{8,0},{12,4},{1,9},{5,13},{9,1},{13,5},{2,10},{6,14},... | collective-permute-start | bytes 786440 | tf_op jit(solution)/shard_map/ppermute | solution.py:413
  76.0 30.1 %collective-permute-start.22 = (bf16[8,128,128]{2,1,0:T(8,128)(2,1)}, bf16[8,128,128]{2,1,0:T(8,128)(2,1)}, u32[]{:S(2)}, u32[]{:S(2)}) collective-permute-start(bf16[8,128,128]{2,1,0:T(8,128)(2,1)} %get-tuple-element.59), channel_id=1, source_target_pairs={{0,12},{4,8},{8,4},{12,0},{1,13},{5,9},{9,5},{13,1},{2,14},{6,10},... | collective-permute-start | bytes 786440 | tf_op jit(solution)/shard_map/ppermute | solution.py:413
  76.0 34.0 %collective-permute-start.14 = (bf16[8,128,128]{2,1,0:T(8,128)(2,1)}, bf16[8,128,128]{2,1,0:T(8,128)(2,1)S(1)}, u32[]{:S(2)}, u32[]{:S(2)}) collective-permute-start(bf16[8,128,128]{2,1,0:T(8,128)(2,1)} %get-tuple-element.49), channel_id=1, source_target_pairs={{0,4},{4,0},{8,12},{12,8},{1,5},{5,1},{9,13},{13,9},{2,6},{6,2},{1... | collective-permute-start | bytes 786440 | tf_op jit(solution)/shard_map/ppermute | solution.py:413
  76.7 33.3 %collective-permute-start.15 = (bf16[8,128,128]{2,1,0:T(8,128)(2,1)}, bf16[8,128,128]{2,1,0:T(8,128)(2,1)}, u32[]{:S(2)}, u32[]{:S(2)}) collective-permute-start(bf16[8,128,128]{2,1,0:T(8,128)(2,1)} %get-tuple-element.50), channel_id=1, source_target_pairs={{0,8},{4,12},{8,0},{12,4},{1,9},{5,13},{9,1},{13,5},{2,10},{6,14},... | collective-permute-start | bytes 786440 | tf_op jit(solution)/shard_map/ppermute | solution.py:413
  81.7 28.8 %collective-permute-start.16 = (bf16[8,128,128]{2,1,0:T(8,128)(2,1)}, bf16[8,128,128]{2,1,0:T(8,128)(2,1)}, u32[]{:S(2)}, u32[]{:S(2)}) collective-permute-start(bf16[8,128,128]{2,1,0:T(8,128)(2,1)} %get-tuple-element.51), channel_id=1, source_target_pairs={{0,12},{4,8},{8,4},{12,0},{1,13},{5,9},{9,5},{13,1},{2,14},{6,10},... | collective-permute-start | bytes 786440 | tf_op jit(solution)/shard_map/ppermute | solution.py:413
  100.4 40.4 %collective-permute-start.35 = (bf16[8,128,128]{2,1,0:T(8,128)(2,1)S(1)}, bf16[8,128,128]{2,1,0:T(8,128)(2,1)S(1)}, u32[]{:S(2)}, u32[]{:S(2)}) collective-permute-start(bf16[8,128,128]{2,1,0:T(8,128)(2,1)S(1)} %get-tuple-element.77), channel_id=1, source_target_pairs={{0,4},{4,0},{8,12},{12,8},{1,5},{5,1},{9,13},{13,9},{2,6},{6,2},{1... | collective-permute-start | bytes 786440 | tf_op jit(solution)/shard_map/ppermute | solution.py:413
  106.1 47.2 %collective-permute-start.36 = (bf16[8,128,128]{2,1,0:T(8,128)(2,1)S(1)}, bf16[8,128,128]{2,1,0:T(8,128)(2,1)S(1)}, u32[]{:S(2)}, u32[]{:S(2)}) collective-permute-start(bf16[8,128,128]{2,1,0:T(8,128)(2,1)S(1)} %get-tuple-element.78), channel_id=1, source_target_pairs={{0,8},{4,12},{8,0},{12,4},{1,9},{5,13},{9,1},{13,5},{2,10},{6,14},... | collective-permute-start | bytes 786440 | tf_op jit(solution)/shard_map/ppermute | solution.py:413
  110.0 28.4 %collective-permute-start.8 = (bf16[4,128,128]{2,1,0:T(8,128)(2,1)S(1)}, bf16[4,128,128]{2,1,0:T(8,128)(2,1)S(1)}, u32[]{:S(2)}, u32[]{:S(2)}) collective-permute-start(bf16[4,128,128]{2,1,0:T(8,128)(2,1)S(1)} %get-tuple-element.46), channel_id=1, source_target_pairs={{0,8},{4,12},{8,0},{12,4},{1,9},{5,13},{9,1},{13,5},{2,10},{6,14},... | collective-permute-start | bytes 393224 | tf_op jit(solution)/shard_map/ppermute | solution.py:413
  110.6 27.9 %collective-permute-start.9 = (bf16[4,128,128]{2,1,0:T(8,128)(2,1)S(1)}, bf16[4,128,128]{2,1,0:T(8,128)(2,1)S(1)}, u32[]{:S(2)}, u32[]{:S(2)}) collective-permute-start(bf16[4,128,128]{2,1,0:T(8,128)(2,1)S(1)} %get-tuple-element.47), channel_id=1, source_target_pairs={{0,12},{4,8},{8,4},{12,0},{1,13},{5,9},{9,5},{13,1},{2,14},{6,10},... | collective-permute-start | bytes 393224 | tf_op jit(solution)/shard_map/ppermute | solution.py:413
  123.1 39.4 %collective-permute-start.37 = (bf16[8,128,128]{2,1,0:T(8,128)(2,1)S(1)}, bf16[8,128,128]{2,1,0:T(8,128)(2,1)S(1)}, u32[]{:S(2)}, u32[]{:S(2)}) collective-permute-start(bf16[8,128,128]{2,1,0:T(8,128)(2,1)S(1)} %get-tuple-element.79), channel_id=1, source_target_pairs={{0,12},{4,8},{8,4},{12,0},{1,13},{5,9},{9,5},{13,1},{2,14},{6,10},... | collective-permute-start | bytes 786440 | tf_op jit(solution)/shard_map/ppermute | solution.py:413
  138.4 25.1 %collective-permute-start.29 = (bf16[8,128,128]{2,1,0:T(8,128)(2,1)S(1)}, bf16[8,128,128]{2,1,0:T(8,128)(2,1)S(1)}, u32[]{:S(2)}, u32[]{:S(2)}) collective-permute-start(bf16[8,128,128]{2,1,0:T(8,128)(2,1)S(1)} %get-tuple-element.69), channel_id=1, source_target_pairs={{0,4},{4,0},{8,12},{12,8},{1,5},{5,1},{9,13},{13,9},{2,6},{6,2},{1... | collective-permute-start | bytes 786440 | tf_op jit(solution)/shard_map/ppermute | solution.py:413
  138.4 28.4 %collective-permute-start.30 = (bf16[8,128,128]{2,1,0:T(8,128)(2,1)S(1)}, bf16[8,128,128]{2,1,0:T(8,128)(2,1)S(1)}, u32[]{:S(2)}, u32[]{:S(2)}) collective-permute-start(bf16[8,128,128]{2,1,0:T(8,128)(2,1)S(1)} %get-tuple-element.70), channel_id=1, source_target_pairs={{0,8},{4,12},{8,0},{12,4},{1,9},{5,13},{9,1},{13,5},{2,10},{6,14},... | collective-permute-start | bytes 786440 | tf_op jit(solution)/shard_map/ppermute | solution.py:413
  140.8 26.1 %collective-permute-start.31 = (bf16[8,128,128]{2,1,0:T(8,128)(2,1)S(1)}, bf16[8,128,128]{2,1,0:T(8,128)(2,1)S(1)}, u32[]{:S(2)}, u32[]{:S(2)}) collective-permute-start(bf16[8,128,128]{2,1,0:T(8,128)(2,1)S(1)} %get-tuple-element.71), channel_id=1, source_target_pairs={{0,12},{4,8},{8,4},{12,0},{1,13},{5,9},{9,5},{13,1},{2,14},{6,10},... | collective-permute-start | bytes 786440 | tf_op jit(solution)/shard_map/ppermute | solution.py:413
  153.3 26.9 %collective-permute-start.23 = (bf16[8,128,128]{2,1,0:T(8,128)(2,1)S(1)}, bf16[8,128,128]{2,1,0:T(8,128)(2,1)S(1)}, u32[]{:S(2)}, u32[]{:S(2)}) collective-permute-start(bf16[8,128,128]{2,1,0:T(8,128)(2,1)S(1)} %get-tuple-element.61), channel_id=1, source_target_pairs={{0,4},{4,0},{8,12},{12,8},{1,5},{5,1},{9,13},{13,9},{2,6},{6,2},{1... | collective-permute-start | bytes 786440 | tf_op jit(solution)/shard_map/ppermute | solution.py:413
  162.5 35.0 %collective-permute-start.24 = (bf16[8,128,128]{2,1,0:T(8,128)(2,1)S(1)}, bf16[8,128,128]{2,1,0:T(8,128)(2,1)S(1)}, u32[]{:S(2)}, u32[]{:S(2)}) collective-permute-start(bf16[8,128,128]{2,1,0:T(8,128)(2,1)S(1)} %get-tuple-element.62), channel_id=1, source_target_pairs={{0,8},{4,12},{8,0},{12,4},{1,9},{5,13},{9,1},{13,5},{2,10},{6,14},... | collective-permute-start | bytes 786440 | tf_op jit(solution)/shard_map/ppermute | solution.py:413
  163.5 33.9 %collective-permute-start.25 = (bf16[8,128,128]{2,1,0:T(8,128)(2,1)S(1)}, bf16[8,128,128]{2,1,0:T(8,128)(2,1)S(1)}, u32[]{:S(2)}, u32[]{:S(2)}) collective-permute-start(bf16[8,128,128]{2,1,0:T(8,128)(2,1)S(1)} %get-tuple-element.63), channel_id=1, source_target_pairs={{0,12},{4,8},{8,4},{12,0},{1,13},{5,9},{9,5},{13,1},{2,14},{6,10},... | collective-permute-start | bytes 786440 | tf_op jit(solution)/shard_map/ppermute | solution.py:413
  166.9 31.1 %collective-permute-start.18 = (bf16[8,128,128]{2,1,0:T(8,128)(2,1)S(1)}, bf16[8,128,128]{2,1,0:T(8,128)(2,1)S(1)}, u32[]{:S(2)}, u32[]{:S(2)}) collective-permute-start(bf16[8,128,128]{2,1,0:T(8,128)(2,1)S(1)} %get-tuple-element.54), channel_id=1, source_target_pairs={{0,4},{4,0},{8,12},{12,8},{1,5},{5,1},{9,13},{13,9},{2,6},{6,2},{1... | collective-permute-start | bytes 786440 | tf_op jit(solution)/shard_map/ppermute | solution.py:413
  166.9 41.8 %collective-permute-start.19 = (bf16[8,128,128]{2,1,0:T(8,128)(2,1)S(1)}, bf16[8,128,128]{2,1,0:T(8,128)(2,1)S(1)}, u32[]{:S(2)}, u32[]{:S(2)}) collective-permute-start(bf16[8,128,128]{2,1,0:T(8,128)(2,1)S(1)} %get-tuple-element.55), channel_id=1, source_target_pairs={{0,8},{4,12},{8,0},{12,4},{1,9},{5,13},{9,1},{13,5},{2,10},{6,14},... | collective-permute-start | bytes 786440 | tf_op jit(solution)/shard_map/ppermute | solution.py:413
  180.1 32.5 %collective-permute-start.17 = (bf16[8,128,128]{2,1,0:T(8,128)(2,1)S(1)}, bf16[8,128,128]{2,1,0:T(8,128)(2,1)S(1)}, u32[]{:S(2)}, u32[]{:S(2)}) collective-permute-start(bf16[8,128,128]{2,1,0:T(8,128)(2,1)S(1)} %get-tuple-element.52), channel_id=1, source_target_pairs={{0,12},{4,8},{8,4},{12,0},{1,13},{5,9},{9,5},{13,1},{2,14},{6,10},... | collective-permute-start | bytes 786440 | tf_op jit(solution)/shard_map/ppermute | solution.py:413
  (44 other events, 542.4 us)
